TPU v7x, 256 devices: a whole 4x4x8 slice. The times are simulated.
256 devices in a mesh: dp: 16 (over y_lo, x, core), fsdp: 16 (over z, y_hi).
Axes of the slice: x: 4, y: 4 (y_hi: 2, y_lo: 2; y = y_hi * 2 + y_lo), z: 8, core: 2. Of those that a mesh axis runs over, the one named last changes fastest.
Arguments:
- img_emb: bfloat16 [8192, 1024], P(('dp', 'fsdp')), may hold values from -0.25 to 0.25
- txt_emb: bfloat16 [8192, 1024], P(('dp', 'fsdp')), may hold values from -0.25 to 0.25
- img_ids: int32 [8192], P(('dp', 'fsdp')), may hold values from 0 to 8191
- txt_ids: int32 [8192], P(('dp', 'fsdp')), may hold values from 0 to 8191
- temp_log: float32 [1], replicated, may hold values from 1.5 to 2.5
- logit_bias: float32 [1], replicated, may hold values from -6 to -2
- block_in: bfloat16 [16384, 3072], P(('dp', 'fsdp')), may hold values from -6 to 6
- dw_kernel: float32 [49, 3072], replicated, may hold values from -0.875 to 0.875
- ln_gain: float32 [3072], replicated, may hold values from 0.5 to 1.5
- ln_bias: float32 [3072], replicated, may hold values from -3 to 3
- w_up: bfloat16 [3072, 6144], P(None, 'fsdp'), may hold values from -0.109375 to 0.109375
- w_down: bfloat16 [6144, 3072], P('fsdp'), may hold values from -0.078125 to 0.078125
- layer_scale: float32 [3072], replicated, may hold values from 0.1 to 1
- head_gain: float32 [3072], replicated, may hold values from 0.5 to 1.5
- head_bias: float32 [3072], replicated, may hold values from -3 to 3
- w_proj: bfloat16 [3072, 1024], replicated, may hold values from -0.109375 to 0.109375
Outputs:
- img_grad: float32 [8192, 1024], P(('dp', 'fsdp'))
- txt_grad: float32 [8192, 1024], P(('dp', 'fsdp'))
- w_up_grad: float32 [3072, 6144], P('dp', 'fsdp')
- w_down_grad: float32 [6144, 3072], P('fsdp', 'dp')
All inputs are finite; a program needn't handle non-finite values.
Results may differ from a plain program's by a relative error of at most 0.02.
Values may be sent and summed in bfloat16 or wider, within the bound.
No kernel may reach another device: no remote copies, remote signals or barrier semaphores. Data moves between devices by JAX's collectives and lax.ppermute only.
A program may use at most 128 MiB of HBM per device.

v0:
```python
import functools
import math

import jax
import jax.numpy as jnp
from jax import lax
from jax.experimental import pallas as pl
from jax.experimental.pallas import tpu as pltpu
from jax.sharding import Mesh
from jax.sharding import PartitionSpec as P

KERNEL = 7
SIDE = 8
PATCHES = SIDE * SIDE
DP = ("ylo", "x", "core")
FSDP = ("z", "yhi")
ALL = DP + FSDP
NZ = 8
PAIRS = 32
EMBED = 1024
WIDTH = 3072
HID = 384
SEG = WIDTH // EMBED
IMG_AT = SEG * PATCHES
ROWS = IMG_AT + PAIRS + 8
TXT_ROWS = PAIRS + 8
SLAB = WIDTH // 16
BF = jnp.bfloat16
F32 = jnp.float32

GROUPS = [[(0, 0), (0, 1)]]
for _step in range(1, NZ // 2):
    GROUPS.append([(NZ - _step, 0), (NZ - _step, 1), (_step, 0), (_step, 1)])
GROUPS.append([(NZ // 2, 0), (NZ // 2, 1)])
KEYS = [key for group in GROUPS for key in group]


def params(mib):
    return pltpu.CompilerParams(vmem_limit_bytes=mib << 20)


def whole(count):
    return [pl.BlockSpec(memory_space=pltpu.VMEM)] * count


def shape(rows, columns, dtype):
    return jax.ShapeDtypeStruct((rows, columns), dtype)


def hop(value, axis, length, step):
    return lax.ppermute(value, axis, [(i, (i + step) % length) for i in range(length)])


def absolute(key):
    z = lax.rem(lax.axis_index("z") + key[0], NZ)
    y = lax.axis_index("yhi")
    return z * 2 + (y if key[1] == 0 else 1 - y)


def unit_rows(values):
    length = jnp.sqrt(jnp.sum(values * values, axis=1, keepdims=True) + 1e-06)
    return (values / length, length)


def front_kernel(
    img, txt, img_ids, txt_ids, block_in, taps, gain, bias, blk, txt_pay, means, mixed, ids
):
    def id_rows(source):
        ids[...] = jnp.zeros_like(ids)
        ids[0:1, 0:PAIRS] = source[...]
        row = lax.broadcasted_iota(jnp.int32, (8, EMBED), 0)
        value = jnp.broadcast_to(ids[0:1, :], (8, EMBED))
        return jnp.where(row == 0, value >> 7, jnp.where(row == 1, value & 127, 0)).astype(F32)

    blk[IMG_AT : IMG_AT + PAIRS, :] = unit_rows(img[...].astype(F32))[0].astype(BF)
    blk[IMG_AT + PAIRS : ROWS, :] = id_rows(img_ids).astype(BF)
    txt_pay[0:PAIRS, :] = unit_rows(txt[...].astype(F32))[0].astype(BF)
    place = (lax.axis_index("ylo") * 4 + lax.axis_index("x")) * 2 + lax.axis_index("core")
    txt_pay[PAIRS:TXT_ROWS, :] = pltpu.roll(id_rows(txt_ids), place * PAIRS, 1).astype(BF)

    column = lax.broadcasted_iota(jnp.int32, (SIDE, 128), 0)

    def lanes(c, sums):
        at = pl.ds(pl.multiple_of(c * 128, 128), 128)
        patch = block_in[:, at].astype(F32)
        rows = [patch[r * SIDE : (r + 1) * SIDE] for r in range(SIDE)]
        total = rows[0]
        for r in range(1, SIDE):
            total = total + rows[r]
        mean = jnp.sum(total, axis=0, keepdims=True) / PATCHES
        means[0:1, at] = mean.astype(BF).astype(F32)
        acc = [jnp.zeros((SIDE, 128), F32) for _ in range(SIDE)]
        for across in range(KERNEL):
            move = across - KERNEL // 2
            if move == 0:
                moved = rows
            else:
                inside = (column + move >= 0) & (column + move < SIDE)
                moved = [
                    jnp.where(inside, pltpu.roll(row, (-move) % SIDE, 0), 0.0) for row in rows
                ]
            for above in range(KERNEL):
                tap = taps[above * KERNEL + across : above * KERNEL + across + 1, at]
                for r in range(SIDE):
                    source = r + above - KERNEL // 2
                    if 0 <= source < SIDE:
                        acc[r] = acc[r] + tap * moved[source]
        for r in range(SIDE):
            mixed[r * SIDE : (r + 1) * SIDE, at] = acc[r]
        return tuple(s + a for s, a in zip(sums, acc))

    sums = lax.fori_loop(
        0, WIDTH // 128, lanes, tuple(jnp.zeros((SIDE, 128), F32) for _ in range(SIDE))
    )
    centre = jnp.concatenate(
        [jnp.sum(s, axis=1, keepdims=True) / WIDTH for s in sums], axis=0
    )
    square = jnp.zeros((PATCHES, 128), F32)
    for c in range(WIDTH // 128):
        off = mixed[:, c * 128 : (c + 1) * 128] - centre
        square = square + off * off
    inverse = 1.0 / jnp.sqrt(jnp.sum(square, axis=1, keepdims=True) / WIDTH + 1e-06)
    for c in range(WIDTH // 128):
        at = slice(c * 128, (c + 1) * 128)
        normal = (mixed[:, at] - centre) * inverse
        seg, lane = divmod(c * 128, EMBED)
        blk[seg * PATCHES : (seg + 1) * PATCHES, lane : lane + 128] = (
            normal * gain[:, at] + bias[:, at]
        ).astype(BF)


def front(img, txt, img_ids, txt_ids, block_in, taps, gain, bias):
    return pl.pallas_call(
        front_kernel,
        out_shape=(shape(ROWS, EMBED, BF), shape(TXT_ROWS, EMBED, BF), shape(1, WIDTH, F32)),
        in_specs=whole(8),
        out_specs=tuple(whole(3)),
        scratch_shapes=[
            pltpu.VMEM((PATCHES, WIDTH), F32),
            pltpu.VMEM((8, EMBED), jnp.int32),
        ],
        compiler_params=params(16),
        name="front",
    )(img, txt, img_ids, txt_ids, block_in, taps, gain, bias)


def step_kernel(count, *refs):
    blocks = refs[:count]
    w_up, texts, temp_log, logit_bias, slope, sums, image_part, weights = refs[count:]
    root = math.sqrt(2.0 / math.pi)
    hidden = None
    for seg in range(SEG):
        rows = jnp.concatenate(
            [b[seg * PATCHES : (seg + 1) * PATCHES, :] for b in blocks], axis=0
        )
        part = jnp.dot(
            rows, w_up[seg * EMBED : (seg + 1) * EMBED, :], preferred_element_type=F32
        )
        hidden = part if hidden is None else hidden + part
    square = hidden * hidden
    curve = jnp.tanh(root * (hidden + 0.044715 * (square * hidden)))
    half = 0.5 * (1.0 + curve)
    active = (hidden * half).astype(BF).astype(F32)
    slope[...] = half + 0.5 * hidden * (1.0 - curve * curve) * (
        root * (1.0 + 3.0 * 0.044715 * square)
    )
    for i in range(count):
        sums[i : i + 1, :] = jnp.sum(
            active[i * PATCHES : (i + 1) * PATCHES], axis=0, keepdims=True
        )

    temper = jnp.exp(temp_log[...])
    text_rows = jnp.concatenate(
        [texts[d * TXT_ROWS : d * TXT_ROWS + PAIRS, :] for d in range(16)], axis=0
    )
    digits = texts[PAIRS : PAIRS + 8, 0:512].astype(F32)
    for d in range(1, 16):
        at = d * TXT_ROWS + PAIRS
        digits = digits + texts[at : at + 8, 0:512].astype(F32)
    text_ids = digits[0:1] * 128.0 + digits[1:2]
    columns = []
    for b in blocks:
        pair = b[IMG_AT + PAIRS : ROWS, 0:128].astype(F32)
        row = jnp.broadcast_to(pair[0:1] * 128.0 + pair[1:2], (128, 128))
        columns.append(jnp.transpose(row)[0:PAIRS, 0:1])
    image_ids = jnp.concatenate(columns, axis=0)
    images = jnp.concatenate([b[IMG_AT : IMG_AT + PAIRS, :] for b in blocks], axis=0)
    scores = lax.dot_general(
        images, text_rows, (((1,), (1,)), ((), ())), preferred_element_type=F32
    )
    logits = temper * scores + logit_bias[...]
    labels = jnp.where(image_ids == text_ids, 1.0, -1.0)
    weight = (temper * -labels * jax.nn.sigmoid(-labels * logits)).astype(BF)
    weights[...] = weight
    image_part[...] = jnp.dot(weight, text_rows, preferred_element_type=F32).astype(BF)


def step(blocks, w_up, texts, temp_log, logit_bias):
    count = len(blocks)
    return pl.pallas_call(
        functools.partial(step_kernel, count),
        out_shape=(
            shape(count * PATCHES, HID, F32),
            shape(count, HID, F32),
            shape(count * PAIRS, EMBED, BF),
            shape(count * PAIRS, 16 * PAIRS, BF),
        ),
        in_specs=whole(count + 4),
        out_specs=tuple(whole(4)),
        compiler_params=params(20),
        name="step",
    )(*blocks, w_up, texts, temp_log, logit_bias)


def mean_kernel(*refs):
    count = len(GROUPS)
    sums, images = refs[:count], refs[count : 2 * count]
    w_down, out, held = refs[2 * count :]
    mean = jnp.concatenate([s[...] for s in sums], axis=0) / PATCHES
    first = mean.astype(BF)
    rest = mean - first.astype(F32)
    second = rest.astype(BF)
    third = (rest - second.astype(F32)).astype(BF)
    three = jnp.dot(
        jnp.concatenate([first, second, third], axis=0), w_down[...], preferred_element_type=F32
    )
    partial = three[0:16] + three[16:32] + three[32:48]
    rows = jnp.concatenate(
        [
            image[i * PAIRS : i * PAIRS + 8, :].astype(F32)[0:1]
            for image, group in zip(images, GROUPS)
            for i in range(len(group))
        ],
        axis=0,
    )
    for c in range(6):
        held[:, c, :] = partial[:, c * 512 : (c + 1) * 512]
    for c in range(2):
        held[:, 6 + c, :] = rows[:, c * 512 : (c + 1) * 512]
    for j, key in enumerate(KEYS):
        at = pl.ds(pl.multiple_of(absolute(key) * 8, 8), 8)
        out[at, :] = held[j].astype(BF)


def mean_rows(sums, images, w_down):
    return pl.pallas_call(
        mean_kernel,
        out_shape=shape(128, 512, BF),
        in_specs=whole(2 * len(GROUPS) + 1),
        out_specs=pl.BlockSpec(memory_space=pltpu.VMEM),
        scratch_shapes=[pltpu.VMEM((16, 8, 512), F32)],
        compiler_params=params(16),
        name="mean_rows",
    )(*sums, *images, w_down)


def head_kernel(parts, means, scale, gain, bias, w_proj, out):
    total = parts[0:8, :].astype(F32)
    for d in range(1, 16):
        total = total + parts[d * 8 : (d + 1) * 8, :].astype(F32)
    block_mean = jnp.concatenate([total[c : c + 1] for c in range(6)], axis=1)
    image_sum = jnp.concatenate([total[6:7], total[7:8]], axis=1)
    pooled = means[...] + scale[...] * block_mean
    centred = pooled - jnp.sum(pooled, axis=1, keepdims=True) / WIDTH
    inverse = 1.0 / jnp.sqrt(jnp.sum(centred * centred, axis=1, keepdims=True) / WIDTH + 1e-06)
    head_norm = centred * inverse
    head_out = jnp.broadcast_to(head_norm * gain[...] + bias[...], (8, WIDTH)).astype(BF)
    embed = jnp.dot(head_out, w_proj[...], preferred_element_type=F32)[0:1]
    unit, length = unit_rows(embed)
    inner = jnp.sum(unit * image_sum, axis=1, keepdims=True)
    embed_grad = jnp.broadcast_to((image_sum - unit * inner) / length, (8, EMBED)).astype(BF)
    head_grad = lax.dot_general(
        embed_grad, w_proj[...], (((1,), (1,)), ((), ())), preferred_element_type=F32
    )[0:1]
    norm_grad = head_grad * gain[...]
    pool_grad = inverse * (
        norm_grad
        - jnp.sum(norm_grad, axis=1, keepdims=True) / WIDTH
        - head_norm * (jnp.sum(norm_grad * head_norm, axis=1, keepdims=True) / WIDTH)
    )
    row = scale[...] * pool_grad / PATCHES
    tile = jnp.concatenate([row[:, c * HID : (c + 1) * HID] for c in range(8)], axis=0).astype(BF)
    for d in range(16):
        out[d * 8 : (d + 1) * 8, :] = tile


def head(parts, means, scale, gain, bias, w_proj):
    return pl.pallas_call(
        head_kernel,
        out_shape=shape(128, HID, BF),
        in_specs=whole(6),
        out_specs=pl.BlockSpec(memory_space=pltpu.VMEM),
        compiler_params=params(16),
        name="head",
    )(parts, means, scale, gain, bias, w_proj)


def text_kernel(*refs):
    count = len(GROUPS)
    blocks = refs[:16]
    weights, images, sums = (refs[16 + i * count : 16 + (i + 1) * count] for i in range(3))
    txt_out, img_out = refs[16 + 3 * count :]
    weight = jnp.concatenate([w[...] for w in weights], axis=0)
    rows = jnp.concatenate([b[IMG_AT : IMG_AT + PAIRS, :] for b in blocks], axis=0)
    text_part = lax.dot_general(
        weight, rows, (((0,), (0,)), ((), ())), preferred_element_type=F32
    ).astype(BF)
    total = jnp.concatenate([s[...] for s in sums], axis=0)
    active = jnp.concatenate(
        [total[0:8], total[8:16], jnp.zeros((8, EMBED - 2 * HID), F32)], axis=1
    ).astype(BF)
    for d in range(16):
        txt_out[d * TXT_ROWS : d * TXT_ROWS + PAIRS, :] = text_part[d * PAIRS : (d + 1) * PAIRS]
        txt_out[d * TXT_ROWS + PAIRS : (d + 1) * TXT_ROWS, :] = active
    for image, group in zip(images, GROUPS):
        for i, key in enumerate(group):
            at = pl.ds(pl.multiple_of(absolute(key) * PAIRS, PAIRS), PAIRS)
            img_out[at, :] = image[i * PAIRS : (i + 1) * PAIRS, :]


def text_parts(blocks, weights, images, sums):
    return pl.pallas_call(
        text_kernel,
        out_shape=(shape(16 * TXT_ROWS, EMBED, BF), shape(16 * PAIRS, EMBED, BF)),
        in_specs=whole(16 + 3 * len(GROUPS)),
        out_specs=tuple(whole(2)),
        compiler_params=params(24),
        name="text_parts",
    )(*blocks, *weights, *images, *sums)


def turn_kernel(*refs):
    blocks, out = refs[:16], refs[16]
    for p in range(8):
        for seg in range(SEG):
            at = slice(seg * PATCHES, (seg + 1) * PATCHES)
            rows = jnp.concatenate([blocks[2 * p][at, :], blocks[2 * p + 1][at, :]], axis=0)
            out[seg * EMBED : (seg + 1) * EMBED, p * 128 : (p + 1) * 128] = jnp.transpose(rows)


def turned(blocks):
    return pl.pallas_call(
        turn_kernel,
        out_shape=shape(WIDTH, 16 * PATCHES, BF),
        in_specs=whole(16),
        out_specs=pl.BlockSpec(memory_space=pltpu.VMEM),
        compiler_params=params(24),
        name="turned",
    )(*blocks)


def back_kernel(*refs):
    count = len(GROUPS)
    grads, w_down, rows = refs[:3]
    slopes = refs[3 : 3 + count]
    send, keep, held, hid_grad = refs[3 + count :]
    for j, key in enumerate(KEYS):
        at = pl.ds(pl.multiple_of(absolute(key) * 8, 8), 8)
        held[j] = grads[at, :].astype(F32)
    group = jnp.concatenate([held[:, c, :] for c in range(8)], axis=1)
    row_down = lax.dot_general(
        group.astype(BF), w_down[...], (((1,), (1,)), ((), ())), preferred_element_type=F32
    )
    j = 0
    for slope, keys in zip(slopes, GROUPS):
        for i in range(len(keys)):
            hid_grad[j * PATCHES : (j + 1) * PATCHES, :] = (
                slope[i * PATCHES : (i + 1) * PATCHES, :] * row_down[j : j + 1]
            ).astype(BF)
            j += 1
    low, high = slice(0, SLAB), slice(SLAB, 2 * SLAB)
    core = lax.axis_index("core")
    for k in range(8):
        part = jnp.dot(
            rows[k * 2 * SLAB : (k + 1) * 2 * SLAB, :], hid_grad[...], preferred_element_type=F32
        ).astype(BF)
        mine = group[:, k * 2 * SLAB : (k + 1) * 2 * SLAB]
        swapped = pltpu.roll(mine, SLAB, 1).astype(BF)
        mine = mine.astype(BF)
        at = slice(k * (SLAB + 16), k * (SLAB + 16) + SLAB)
        below = slice(k * (SLAB + 16) + SLAB, (k + 1) * (SLAB + 16))

        @pl.when(core == 0)
        def _():
            keep[at, :] = part[low]
            send[at, :] = part[high]
            keep[below, :] = mine
            send[below, :] = swapped

        @pl.when(core == 1)
        def _():
            keep[at, :] = part[high]
            send[at, :] = part[low]
            keep[below, :] = swapped
            send[below, :] = mine


def backward(grads, w_down, rows, slopes):
    out = shape(8 * (SLAB + 16), HID, BF)
    return pl.pallas_call(
        back_kernel,
        out_shape=(out, out),
        in_specs=whole(3 + len(GROUPS)),
        out_specs=tuple(whole(2)),
        scratch_shapes=[pltpu.VMEM((16, 8, HID), F32), pltpu.VMEM((16 * PATCHES, HID), BF)],
        compiler_params=params(32),
        name="backward",
    )(grads, w_down, rows, *slopes)


def join_kernel(keep, got, out):
    lane = lax.broadcasted_iota(jnp.int32, (16, HID), 1)
    for k in range(8):
        at = slice(k * (SLAB + 16), k * (SLAB + 16) + SLAB)
        below = slice(k * (SLAB + 16) + SLAB, (k + 1) * (SLAB + 16))
        out[at, :] = (keep[at, :].astype(F32) + got[at, :].astype(F32)).astype(BF)
        other = pltpu.roll(got[below, :].astype(F32), SLAB, 1)
        out[below, :] = jnp.where(lane < SLAB, keep[below, :].astype(F32), other).astype(BF)


def join(keep, got):
    return pl.pallas_call(
        join_kernel,
        out_shape=shape(8 * (SLAB + 16), HID, BF),
        in_specs=whole(2),
        out_specs=pl.BlockSpec(memory_space=pltpu.VMEM),
        compiler_params=params(16),
        name="join",
    )(keep, got)


def last_kernel(got, texts, up_out, down_out):
    total = got[0:SLAB, :].astype(F32)
    for k in range(1, 8):
        at = k * (SLAB + 16)
        total = total + got[at : at + SLAB, :].astype(F32)
    up_out[...] = total
    core = lax.axis_index("core")
    grads = jnp.concatenate(
        [got[k * (SLAB + 16) + SLAB : (k + 1) * (SLAB + 16), :] for k in range(8)], axis=0
    )
    others = pltpu.roll(grads.astype(F32), SLAB, 1)[:, 0:SLAB].astype(BF)
    down = None
    for own, right in ((core, grads[:, 0:SLAB]), (1 - core, others)):
        pieces = []
        for k in range(8):
            at = pl.ds(pl.multiple_of((2 * k + own) * TXT_ROWS + PAIRS, 8), 8)
            pieces.append(texts[at, 0:HID])
            pieces.append(texts[at, HID : 2 * HID])
        left = jnp.concatenate(pieces, axis=0)
        part = lax.dot_general(
            left, right, (((0,), (0,)), ((), ())), preferred_element_type=F32
        )
        down = part if down is None else down + part
    down_out[...] = down


def last(got, texts):
    return pl.pallas_call(
        last_kernel,
        out_shape=(shape(SLAB, HID, F32), shape(HID, SLAB, F32)),
        in_specs=whole(2),
        out_specs=tuple(whole(2)),
        compiler_params=params(16),
        name="last",
    )(got, texts)


def rows_kernel(stride, parts, emb, out):
    total = parts[0:PAIRS, :].astype(F32)
    for d in range(1, 16):
        total = total + parts[d * stride : d * stride + PAIRS, :].astype(F32)
    unit, length = unit_rows(emb[...].astype(F32))
    inner = jnp.sum(unit * total, axis=1, keepdims=True)
    out[...] = (total - unit * inner) / length


def row_grads(parts, emb, stride, name):
    return pl.pallas_call(
        functools.partial(rows_kernel, stride),
        out_shape=shape(PAIRS, EMBED, F32),
        in_specs=whole(2),
        out_specs=pl.BlockSpec(memory_space=pltpu.VMEM),
        compiler_params=params(16),
        name=name,
    )(parts, emb)


def swap(value, axes, count):
    rows, columns = value.shape
    parts = value.reshape(count, rows // count, columns)
    return lax.all_to_all(parts, axes, 0, 0, tiled=True).reshape(rows, columns)


def on_device(
    img_emb,
    txt_emb,
    img_ids,
    txt_ids,
    temp_log,
    logit_bias,
    block_in,
    dw_kernel,
    ln_gain,
    ln_bias,
    w_up,
    w_down,
    layer_scale,
    head_gain,
    head_bias,
    w_proj,
):
    blk, txt_pay, means = front(
        img_emb,
        txt_emb,
        img_ids.reshape(1, PAIRS),
        txt_ids.reshape(1, PAIRS),
        block_in,
        dw_kernel,
        ln_gain.reshape(1, WIDTH),
        ln_bias.reshape(1, WIDTH),
    )
    got = {(0, 0): blk, (0, 1): hop(blk, "yhi", 2, 1)}
    for distance in range(1, NZ // 2 + 1):
        last_hop = distance == NZ // 2
        for side in range(2):
            if not last_hop or side == 0:
                got[NZ - distance, side] = hop(
                    got[(NZ - distance + 1) % NZ, side], "z", NZ, 1
                )
            if not last_hop or side == 1:
                got[distance, side] = hop(got[distance - 1, side], "z", NZ, -1)
    texts = swap(
        jnp.broadcast_to(txt_pay[None], (16, TXT_ROWS, EMBED)).reshape(-1, EMBED), DP, 16
    )
    temper = temp_log.reshape(1, 1)
    offset = logit_bias.reshape(1, 1)
    slopes, sums, images, weights = [], [], [], []
    for group in GROUPS:
        done = step([got[key] for key in group], w_up, texts, temper, offset)
        for into, value in zip((slopes, sums, images, weights), done):
            into.append(value)
    parts = swap(mean_rows(sums, images, w_down), FSDP, 16)
    blocks = [got[key] for key in KEYS]
    txt_parts, img_parts = text_parts(blocks, weights, images, sums)
    txt_parts = swap(txt_parts, DP, 16)
    rows = turned(blocks)
    grads = head(
        parts,
        means,
        layer_scale.reshape(1, WIDTH),
        head_gain.reshape(1, WIDTH),
        head_bias.reshape(1, WIDTH),
        w_proj,
    )
    grads = swap(grads, FSDP, 16)
    img_parts = swap(img_parts, FSDP, 16)
    send, keep = backward(grads, w_down, rows, slopes)
    both = join(keep, hop(send, "core", 2, 1))
    w_up_grad, w_down_grad = last(swap(both, ("ylo", "x"), 8), txt_parts)
    txt_grad = row_grads(txt_parts, txt_emb, TXT_ROWS, "txt_rows")
    img_grad = row_grads(img_parts, img_emb, PAIRS, "img_rows")
    return (img_grad, txt_grad, w_up_grad, w_down_grad)


def solution(mesh):
    split = Mesh(mesh.devices.reshape(2, 4, 2, NZ, 2), ALL)
    in_specs = (
        P(ALL, None),
        P(ALL, None),
        P(ALL),
        P(ALL),
        P(),
        P(),
        P(ALL, None),
        P(),
        P(),
        P(),
        P(None, FSDP),
        P(FSDP, None),
        P(),
        P(),
        P(),
        P(),
    )
    out_specs = (P(ALL, None), P(ALL, None), P(DP, FSDP), P(FSDP, DP))
    return jax.shard_map(
        on_device, mesh=split, in_specs=in_specs, out_specs=out_specs, check_vma=False
    )
```

profile of v0, /device:TPU:1, one launch (start us, length us, event | category | flops | bytes accessed | tf_op | source)
XLA Modules:
  0.0 226.7 jit_solution(4162193878671492892)
XLA Ops:
  0.6 1.1 copy-done.14
  1.7 1.0 copy-done.23
  2.7 0.8 copy-done.24
  3.6 0.8 copy-done.26
  4.4 0.7 copy-done.44
  5.1 0.7 copy-done.45
  5.8 0.7 copy-done.53
  6.5 0.7 copy-done.54
  7.1 3.5 %front.1 = (bf16[232,1024]{1,0:T(8,128)(2,1)S(1)}, bf16[40,1024]{1,0:T(8,128)(2,1)S(1)}, f32[1,3072]{1,0:T(1,128)S(1)}) custom-call(bf16[32,1024]{1,0:T(8,128)(2,1)S(1)} %copy-done.26, bf16[32,1024]{1,0:T(8,128)(2,1)S(1)} %copy-done.24, s32[1,32]{1,0:T(1,128)S(1)} %bitcast.47, s32[1,32]{1,0:T(1,128)S(1)} %bitcast.48, bf16[64,3072]{1,0:T(8,128)(2,1)S(1)} %copy-done.23, ...), custom_call_target="tpu_custom_call" | custom-call | tf_op jit(solution)/shard_map/front/pallas_call | solution.py:133
  10.6 3.8 %collective-permute-start = (bf16[232,1024]{1,0:T(8,128)(2,1)S(1)}, bf16[232,1024]{1,0:T(8,128)(2,1)S(1)}, u32[]{:S(2)}, u32[]{:S(2)}) collective-permute-start(bf16[232,1024]{1,0:T(8,128)(2,1)S(1)} %get-tuple-element.33.refs_0_), channel_id=1, source_target_pairs={{0,1},{1,0},{2,3},{3,2},{4,5},{5,4},{6,7},{7,6},{8,9},{9,8},{10,11... | collective-permute-start | bytes 1425416 | tf_op jit(solution)/shard_map/ppermute | solution.py:51
  14.4 1.6 collective-permute-start.1
  16.1 7.9 %collective-permute-done.refs_1_ = bf16[232,1024]{1,0:T(8,128)(2,1)S(1)} collective-permute-done((bf16[232,1024]{1,0:T(8,128)(2,1)S(1)}, bf16[232,1024]{1,0:T(8,128)(2,1)S(1)}, u32[]{:S(2)}, u32[]{:S(2)}) %collective-permute-start) | collective-permute-done | bytes 475168 | tf_op jit(solution)/shard_map/ppermute | solution.py:51
  24.0 6.4 %collective-permute-start.4 = (bf16[232,1024]{1,0:T(8,128)(2,1)S(1)}, bf16[232,1024]{1,0:T(8,128)(2,1)}, u32[]{:S(2)}, u32[]{:S(2)}) collective-permute-start(bf16[232,1024]{1,0:T(8,128)(2,1)S(1)} %collective-permute-done.refs_1_), channel_id=1, source_target_pairs={{0,14},{2,0},{4,2},{6,4},{8,6},{10,8},{12,10},{14,12},{1,15},{3,1}... | collective-permute-start | bytes 1425416 | tf_op jit(solution)/shard_map/ppermute | solution.py:51
  30.4 0.7 collective-permute-start.3
  31.1 0.7 collective-permute-start.2
  31.9 7.1 %collective-permute-done.4.refs_3_.refs_5_ = bf16[232,1024]{1,0:T(8,128)(2,1)} collective-permute-done((bf16[232,1024]{1,0:T(8,128)(2,1)S(1)}, bf16[232,1024]{1,0:T(8,128)(2,1)}, u32[]{:S(2)}, u32[]{:S(2)}) %collective-permute-start.4) | collective-permute-done | bytes 475168 | tf_op jit(solution)/shard_map/ppermute | solution.py:51
  39.0 3.5 %collective-permute-start.8 = (bf16[232,1024]{1,0:T(8,128)(2,1)}, bf16[232,1024]{1,0:T(8,128)(2,1)}, u32[]{:S(2)}, u32[]{:S(2)}) collective-permute-start(bf16[232,1024]{1,0:T(8,128)(2,1)} %collective-permute-done.4.refs_3_.refs_5_), channel_id=1, source_target_pairs={{0,14},{2,0},{4,2},{6,4},{8,6},{10,8},{12,10},{14,12},{1,15},{3,1}... | collective-permute-start | bytes 1425416 | tf_op jit(solution)/shard_map/ppermute | solution.py:51
  42.5 1.2 broadcast_in_dim.2
  43.7 10.3 %all-to-all-start = ((bf16[16,40,1024]{2,1,0:T(8,128)(2,1)}), bf16[16,40,1024]{2,1,0:T(8,128)(2,1)}, u32[]{:S(2)}, u32[]{:S(2)}) async-start(bf16[16,40,1024]{2,1,0:T(8,128)(2,1)} %broadcast_in_dim.2), calls=%async_computation | async-start | bytes 2621440 | tf_op jit(solution)/shard_map/all_to_all | solution.py:492
  54.1 1.4 collective-permute-start.6
  55.6 3.8 %collective-permute-done.8.refs_3_.refs_9_ = bf16[232,1024]{1,0:T(8,128)(2,1)} collective-permute-done((bf16[232,1024]{1,0:T(8,128)(2,1)}, bf16[232,1024]{1,0:T(8,128)(2,1)}, u32[]{:S(2)}, u32[]{:S(2)}) %collective-permute-start.8) | collective-permute-done | bytes 475168 | tf_op jit(solution)/shard_map/ppermute | solution.py:51
  59.4 3.4 %collective-permute-start.12 = (bf16[232,1024]{1,0:T(8,128)(2,1)}, bf16[232,1024]{1,0:T(8,128)(2,1)}, u32[]{:S(2)}, u32[]{:S(2)}) collective-permute-start(bf16[232,1024]{1,0:T(8,128)(2,1)} %collective-permute-done.8.refs_3_.refs_9_), channel_id=1, source_target_pairs={{0,14},{2,0},{4,2},{6,4},{8,6},{10,8},{12,10},{14,12},{1,15},{3,1}... | collective-permute-start | bytes 1425416 | tf_op jit(solution)/shard_map/ppermute | solution.py:51
  62.8 6.8 %collective-permute-done.7.refs_2_.refs_8_ = bf16[232,1024]{1,0:T(8,128)(2,1)} collective-permute-done((bf16[232,1024]{1,0:T(8,128)(2,1)}, bf16[232,1024]{1,0:T(8,128)(2,1)}, u32[]{:S(2)}, u32[]{:S(2)}) %collective-permute-start.7) | collective-permute-done | bytes 475168 | tf_op jit(solution)/shard_map/ppermute | solution.py:51
  69.6 3.4 %collective-permute-start.11 = (bf16[232,1024]{1,0:T(8,128)(2,1)}, bf16[232,1024]{1,0:T(8,128)(2,1)}, u32[]{:S(2)}, u32[]{:S(2)}) collective-permute-start(bf16[232,1024]{1,0:T(8,128)(2,1)} %collective-permute-done.7.refs_2_.refs_8_), channel_id=1, source_target_pairs={{0,14},{2,0},{4,2},{6,4},{8,6},{10,8},{12,10},{14,12},{1,15},{3,1}... | collective-permute-start | bytes 1425416 | tf_op jit(solution)/shard_map/ppermute | solution.py:51
  73.0 1.9 collective-permute-done.9.refs_0_.refs_10_
  74.9 1.8 collective-permute-start.13
  76.7 3.1 %collective-permute-done.12.refs_3_.refs_13_ = bf16[232,1024]{1,0:T(8,128)(2,1)} collective-permute-done((bf16[232,1024]{1,0:T(8,128)(2,1)}, bf16[232,1024]{1,0:T(8,128)(2,1)}, u32[]{:S(2)}, u32[]{:S(2)}) %collective-permute-start.12) | collective-permute-done | bytes 475168 | tf_op jit(solution)/shard_map/ppermute | solution.py:51
  79.8 3.4 %collective-permute-start.14 = (bf16[232,1024]{1,0:T(8,128)(2,1)}, bf16[232,1024]{1,0:T(8,128)(2,1)}, u32[]{:S(2)}, u32[]{:S(2)}) collective-permute-start(bf16[232,1024]{1,0:T(8,128)(2,1)} %collective-permute-done.12.refs_3_.refs_13_), channel_id=1, source_target_pairs={{0,14},{2,0},{4,2},{6,4},{8,6},{10,8},{12,10},{14,12},{1,15},{3,1}... | collective-permute-start | bytes 1425416 | tf_op jit(solution)/shard_map/ppermute | solution.py:51
  84.5 2.5 %step.5 = (f32[128,384]{1,0:T(8,128)S(1)}, f32[2,384]{1,0:T(2,128)S(1)}, bf16[64,1024]{1,0:T(8,128)(2,1)S(1)}, bf16[64,512]{1,0:T(8,128)(2,1)S(1)}) custom-call(bf16[232,1024]{1,0:T(8,128)(2,1)S(1)} %get-tuple-element.33.refs_0_, bf16[232,1024]{1,0:T(8,128)(2,1)S(1)} %collective-permute-done.refs_1_, bf16[3072,384]{1,0:T(8,128)(2,1)S(1)} %copy-done, ...), custom_call_target="tpu_custom_call" | custom-call | tf_op jit(solution)/shard_map/step/pallas_call | solution.py:200
  87.1 0.7 copy-done.28
  87.8 0.6 copy-done.38
  88.4 3.7 %step.6 = (f32[256,384]{1,0:T(8,128)S(1)}, f32[4,384]{1,0:T(4,128)S(1)}, bf16[128,1024]{1,0:T(8,128)(2,1)S(1)}, bf16[128,512]{1,0:T(8,128)(2,1)S(1)}) custom-call(bf16[232,1024]{1,0:T(8,128)(2,1)} %collective-permute-done.1.refs_0_.refs_2_, bf16[232,1024]{1,0:T(8,128)(2,1)} %collective-permute-done.2.refs_1_.refs_3_, ...), custom_call_target="tpu_custom_call" | custom-call | tf_op jit(solution)/shard_map/step/pallas_call | solution.py:200
  92.0 0.7 copy-done.17
  92.8 0.7 copy-done.32
  93.4 3.8 %step.7 = (f32[256,384]{1,0:T(8,128)S(1)}, f32[4,384]{1,0:T(4,128)S(1)}, bf16[128,1024]{1,0:T(8,128)(2,1)S(1)}, bf16[128,512]{1,0:T(8,128)(2,1)S(1)}) custom-call(bf16[232,1024]{1,0:T(8,128)(2,1)} %collective-permute-done.5.refs_0_.refs_6_, bf16[232,1024]{1,0:T(8,128)(2,1)} %collective-permute-done.6.refs_1_.refs_7_, ...), custom_call_target="tpu_custom_call" | custom-call | tf_op jit(solution)/shard_map/step/pallas_call | solution.py:200
  97.3 0.7 copy-done.19
  98.0 0.7 copy-done.34
  98.7 3.8 %step.8 = (f32[256,384]{1,0:T(8,128)S(1)}, f32[4,384]{1,0:T(4,128)S(1)}, bf16[128,1024]{1,0:T(8,128)(2,1)S(1)}, bf16[128,512]{1,0:T(8,128)(2,1)S(1)}) custom-call(bf16[232,1024]{1,0:T(8,128)(2,1)} %collective-permute-done.9.refs_0_.refs_10_, bf16[232,1024]{1,0:T(8,128)(2,1)} %collective-permute-done.10.refs_1_.refs_11_, ...), custom_call_target="tpu_custom_call" | custom-call | tf_op jit(solution)/shard_map/step/pallas_call | solution.py:200
  102.5 0.7 copy-done.21
  103.2 0.7 copy-done.36
  103.9 3.0 %step.9 = (f32[128,384]{1,0:T(8,128)S(1)}, f32[2,384]{1,0:T(2,128)S(1)}, bf16[64,1024]{1,0:T(8,128)(2,1)S(1)}, bf16[64,512]{1,0:T(8,128)(2,1)S(1)}) custom-call(bf16[232,1024]{1,0:T(8,128)(2,1)} %collective-permute-done.13.refs_0_.refs_14_, bf16[232,1024]{1,0:T(8,128)(2,1)} %collective-permute-done.14.refs_1_.refs_15_, bf16[3072,384]{1,0:T(8,128)(2,1)S(1)} %copy-done, ...), custom_call_target="tpu_custom_call" | custom-call | tf_op jit(solution)/shard_map/step/pallas_call | solution.py:200
  107.0 0.5 mean_rows.1
  107.6 15.5 %all_to_all.30 = bf16[16,8,512]{2,1,0:T(8,128)(2,1)S(1)} all-to-all(bf16[16,8,512]{2,1,0:T(8,128)(2,1)S(1)} %bitcast.39), channel_id=1, replica_groups=mesh['ylo'=2,'x'=4,'core'=2,'z'=8,'yhi'=2] {'z','yhi'}, dimensions={0} | all-to-all | bytes 262144 | tf_op jit(solution)/shard_map/all_to_all | solution.py:492
  123.2 3.8 %head.1 = bf16[128,384]{1,0:T(8,128)(2,1)} custom-call(bf16[128,512]{1,0:T(8,128)(2,1)S(1)} %bitcast.40, f32[1,3072]{1,0:T(1,128)S(1)} %get-tuple-element.52.means, f32[1,3072]{1,0:T(1,128)S(1)} %bitcast.44, f32[1,3072]{1,0:T(1,128)S(1)} %bitcast.45, f32[1,3072]{1,0:T(1,128)S(1)} %bitcast.46, bf16[3072,1024]{1,0:T(8,128)(2,1)S(1)} %bitcast.33), custom_call_target="tpu_custom_call" | custom-call | tf_op jit(solution)/shard_map/head/pallas_call | solution.py:288
  127.0 3.5 %all-to-all-start.4 = ((bf16[16,8,384]{2,1,0:T(8,128)(2,1)}), bf16[16,8,384]{2,1,0:T(8,128)(2,1)S(1)}, u32[]{:S(2)}, u32[]{:S(2)}) async-start(bf16[16,8,384]{2,1,0:T(8,128)(2,1)} %bitcast.16), calls=%async_computation.4 | async-start | bytes 196608 | tf_op jit(solution)/shard_map/all_to_all | solution.py:492
  130.6 3.8 %text_parts.1 = (bf16[640,1024]{1,0:T(8,128)(2,1)S(1)}, bf16[512,1024]{1,0:T(8,128)(2,1)S(1)}) custom-call(bf16[232,1024]{1,0:T(8,128)(2,1)S(1)} %get-tuple-element.33.refs_0_, bf16[232,1024]{1,0:T(8,128)(2,1)S(1)} %collective-permute-done.refs_1_, bf16[232,1024]{1,0:T(8,128)(2,1)} %collective-permute-done.1.refs_0_.refs_2_, ...), custom_call_target="tpu_custom_call" | custom-call | tf_op jit(solution)/shard_map/text_parts/pallas_call | solution.py:322
  134.4 1.0 copy-done.6
  135.5 1.0 copy-done.7
  136.5 3.8 %all-to-all-done.4 = bf16[16,8,384]{2,1,0:T(8,128)(2,1)S(1)} async-done(((bf16[16,8,384]{2,1,0:T(8,128)(2,1)}), bf16[16,8,384]{2,1,0:T(8,128)(2,1)S(1)}, u32[]{:S(2)}, u32[]{:S(2)}) %all-to-all-start.4) | async-done | bytes 98336 | tf_op jit(solution)/shard_map/all_to_all | solution.py:492
  140.3 29.7 %all_to_all.31 = bf16[16,40,1024]{2,1,0:T(8,128)(2,1)S(1)} all-to-all(bf16[16,40,1024]{2,1,0:T(8,128)(2,1)} %bitcast.37), channel_id=1, replica_groups=mesh['ylo'=2,'x'=4,'core'=2,'z'=8,'yhi'=2] {'ylo','x','core'}, dimensions={0} | all-to-all | bytes 2621440 | tf_op jit(solution)/shard_map/all_to_all | solution.py:492
  170.0 4.9 %all-to-all-start.1 = ((bf16[16,32,1024]{2,1,0:T(8,128)(2,1)}), bf16[16,32,1024]{2,1,0:T(8,128)(2,1)S(1)}, u32[]{:S(2)}, u32[]{:S(2)}) async-start(bf16[16,32,1024]{2,1,0:T(8,128)(2,1)} %bitcast.38), calls=%async_computation.1 | async-start | bytes 2097152 | tf_op jit(solution)/shard_map/all_to_all | solution.py:492
  175.0 5.0 %turned.1.refs_2_ = bf16[3072,1024]{1,0:T(8,128)(2,1)S(1)} custom-call(bf16[232,1024]{1,0:T(8,128)(2,1)S(1)} %get-tuple-element.33.refs_0_, bf16[232,1024]{1,0:T(8,128)(2,1)S(1)} %collective-permute-done.refs_1_, bf16[232,1024]{1,0:T(8,128)(2,1)} %collective-permute-done.1.refs_0_.refs_2_, bf16[232,1024]{1,0:T(8,128)(2,1)} %collective-permute-done.2.refs_1_.refs_3_, ...), custom_call_target="tpu_custom_call" | custom-call | tf_op jit(solution)/shard_map/turned/pallas_call | solution.py:342
  180.0 6.0 %backward.1 = (bf16[1664,384]{1,0:T(8,128)(2,1)S(1)}, bf16[1664,384]{1,0:T(8,128)(2,1)S(1)}) custom-call(bf16[128,384]{1,0:T(8,128)(2,1)S(1)} %bitcast.41, bf16[384,3072]{1,0:T(8,128)(2,1)S(1)} %copy-done.2, bf16[3072,1024]{1,0:T(8,128)(2,1)S(1)} %turned.1.refs_2_, f32[128,384]{1,0:T(8,128)S(1)} %copy-done.29, f32[256,384]{1,0:T(8,128)S(1)} %copy-done.18, ...), custom_call_target="tpu_custom_call" | custom-call | tf_op jit(solution)/shard_map/backward/pallas_call | solution.py:400
  186.0 1.1 collective-permute-start.15
  187.2 2.6 %collective-permute-done.15.got = bf16[1664,384]{1,0:T(8,128)(2,1)S(1)} collective-permute-done((bf16[1664,384]{1,0:T(8,128)(2,1)S(1)}, bf16[1664,384]{1,0:T(8,128)(2,1)S(1)}, u32[]{:S(2)}, u32[]{:S(2)}) %collective-permute-start.15) | collective-permute-done | bytes 1277984 | tf_op jit(solution)/shard_map/ppermute | solution.py:51
  190.2 1.0 copy-done.3
  191.3 10.3 %all-to-all-done.1 = bf16[16,32,1024]{2,1,0:T(8,128)(2,1)S(1)} async-done(((bf16[16,32,1024]{2,1,0:T(8,128)(2,1)}), bf16[16,32,1024]{2,1,0:T(8,128)(2,1)S(1)}, u32[]{:S(2)}, u32[]{:S(2)}) %all-to-all-start.1) | async-done | bytes 1048608 | tf_op jit(solution)/shard_map/all_to_all | solution.py:492
  201.5 1.0 copy-done.4
  202.5 4.1 %all-to-all-start.5 = ((bf16[8,208,384]{2,1,0:T(8,128)(2,1)}), bf16[8,208,384]{2,1,0:T(8,128)(2,1)S(1)}, u32[]{:S(2)}, u32[]{:S(2)}) async-start(bf16[8,208,384]{2,1,0:T(8,128)(2,1)} %bitcast.35), calls=%async_computation.5 | async-start | bytes 2555904 | tf_op jit(solution)/shard_map/all_to_all | solution.py:492
  206.6 0.9 txt_rows.1
  207.8 0.9 img_rows.1
  208.7 15.9 %all-to-all-done.5 = bf16[8,208,384]{2,1,0:T(8,128)(2,1)S(1)} async-done(((bf16[8,208,384]{2,1,0:T(8,128)(2,1)}), bf16[8,208,384]{2,1,0:T(8,128)(2,1)S(1)}, u32[]{:S(2)}, u32[]{:S(2)}) %all-to-all-start.5) | async-done | bytes 1277984 | tf_op jit(solution)/shard_map/all_to_all | solution.py:492
  224.7 1.2 last.1
  225.9 0.9 copy.20
  (110 shorter events, 1.2 us)
Async XLA Ops:
  0.6 1.1 copy-start.14
  1.7 1.0 copy-start.23
  2.7 0.8 copy-start.24
  3.6 0.8 copy-start.26
  10.6 13.4 %collective-permute-start = (bf16[232,1024]{1,0:T(8,128)(2,1)S(1)}, bf16[232,1024]{1,0:T(8,128)(2,1)S(1)}, u32[]{:S(2)}, u32[]{:S(2)}) collective-permute-start(bf16[232,1024]{1,0:T(8,128)(2,1)S(1)} %get-tuple-element.33.refs_0_), channel_id=1, source_target_pairs={{0,1},{1,0},{2,3},{3,2},{4,5},{5,4},{6,7},{7,6},{8,9},{9,8},{10,11... | collective-permute-start | bytes 1425416 | tf_op jit(solution)/shard_map/ppermute | solution.py:51
  14.4 17.4 %collective-permute-start.1 = (bf16[232,1024]{1,0:T(8,128)(2,1)S(1)}, bf16[232,1024]{1,0:T(8,128)(2,1)}, u32[]{:S(2)}, u32[]{:S(2)}) collective-permute-start(bf16[232,1024]{1,0:T(8,128)(2,1)S(1)} %get-tuple-element.33.refs_0_), channel_id=1, source_target_pairs={{0,2},{2,4},{4,6},{6,8},{8,10},{10,12},{12,14},{14,0},{1,3},{3,5},... | collective-permute-start | bytes 1425416 | tf_op jit(solution)/shard_map/ppermute | solution.py:51
  24.0 15.0 %collective-permute-start.4 = (bf16[232,1024]{1,0:T(8,128)(2,1)S(1)}, bf16[232,1024]{1,0:T(8,128)(2,1)}, u32[]{:S(2)}, u32[]{:S(2)}) collective-permute-start(bf16[232,1024]{1,0:T(8,128)(2,1)S(1)} %collective-permute-done.refs_1_), channel_id=1, source_target_pairs={{0,14},{2,0},{4,2},{6,4},{8,6},{10,8},{12,10},{14,12},{1,15},{3,1}... | collective-permute-start | bytes 1425416 | tf_op jit(solution)/shard_map/ppermute | solution.py:51
  30.4 23.6 %collective-permute-start.3 = (bf16[232,1024]{1,0:T(8,128)(2,1)S(1)}, bf16[232,1024]{1,0:T(8,128)(2,1)}, u32[]{:S(2)}, u32[]{:S(2)}) collective-permute-start(bf16[232,1024]{1,0:T(8,128)(2,1)S(1)} %get-tuple-element.33.refs_0_), channel_id=1, source_target_pairs={{0,14},{2,0},{4,2},{6,4},{8,6},{10,8},{12,10},{14,12},{1,15},{3,1}... | collective-permute-start | bytes 1425416 | tf_op jit(solution)/shard_map/ppermute | solution.py:51
  31.1 23.0 %collective-permute-start.2 = (bf16[232,1024]{1,0:T(8,128)(2,1)S(1)}, bf16[232,1024]{1,0:T(8,128)(2,1)}, u32[]{:S(2)}, u32[]{:S(2)}) collective-permute-start(bf16[232,1024]{1,0:T(8,128)(2,1)S(1)} %collective-permute-done.refs_1_), channel_id=1, source_target_pairs={{0,2},{2,4},{4,6},{6,8},{8,10},{10,12},{12,14},{14,0},{1,3},{3,5},... | collective-permute-start | bytes 1425416 | tf_op jit(solution)/shard_map/ppermute | solution.py:51
  31.8 23.7 %collective-permute-start.5 = (bf16[232,1024]{1,0:T(8,128)(2,1)}, bf16[232,1024]{1,0:T(8,128)(2,1)}, u32[]{:S(2)}, u32[]{:S(2)}) collective-permute-start(bf16[232,1024]{1,0:T(8,128)(2,1)} %collective-permute-done.1.refs_0_.refs_2_), channel_id=1, source_target_pairs={{0,2},{2,4},{4,6},{6,8},{8,10},{10,12},{12,14},{14,0},{1,3},{3,5},... | collective-permute-start | bytes 1425416 | tf_op jit(solution)/shard_map/ppermute | solution.py:51
  39.0 20.5 %collective-permute-start.8 = (bf16[232,1024]{1,0:T(8,128)(2,1)}, bf16[232,1024]{1,0:T(8,128)(2,1)}, u32[]{:S(2)}, u32[]{:S(2)}) collective-permute-start(bf16[232,1024]{1,0:T(8,128)(2,1)} %collective-permute-done.4.refs_3_.refs_5_), channel_id=1, source_target_pairs={{0,14},{2,0},{4,2},{6,4},{8,6},{10,8},{12,10},{14,12},{1,15},{3,1}... | collective-permute-start | bytes 1425416 | tf_op jit(solution)/shard_map/ppermute | solution.py:51
  43.7 40.8 %copy-start = (bf16[3072,384]{1,0:T(8,128)(2,1)S(1)}, bf16[3072,384]{1,0:T(8,128)(2,1)}, u32[]{:S(2)}) copy-start(bf16[3072,384]{1,0:T(8,128)(2,1)} %refs_2_.3) | copy-start | bytes 7077892
  43.7 40.8 %all-to-all-start = ((bf16[16,40,1024]{2,1,0:T(8,128)(2,1)}), bf16[16,40,1024]{2,1,0:T(8,128)(2,1)}, u32[]{:S(2)}, u32[]{:S(2)}) async-start(bf16[16,40,1024]{2,1,0:T(8,128)(2,1)} %broadcast_in_dim.2), calls=%async_computation | async-start | bytes 2621440 | tf_op jit(solution)/shard_map/all_to_all | solution.py:492
  54.0 15.6 %collective-permute-start.7 = (bf16[232,1024]{1,0:T(8,128)(2,1)}, bf16[232,1024]{1,0:T(8,128)(2,1)}, u32[]{:S(2)}, u32[]{:S(2)}) collective-permute-start(bf16[232,1024]{1,0:T(8,128)(2,1)} %collective-permute-done.3.refs_2_.refs_4_), channel_id=1, source_target_pairs={{0,14},{2,0},{4,2},{6,4},{8,6},{10,8},{12,10},{14,12},{1,15},{3,1}... | collective-permute-start | bytes 1425416 | tf_op jit(solution)/shard_map/ppermute | solution.py:51
  54.1 19.0 %collective-permute-start.6 = (bf16[232,1024]{1,0:T(8,128)(2,1)}, bf16[232,1024]{1,0:T(8,128)(2,1)}, u32[]{:S(2)}, u32[]{:S(2)}) collective-permute-start(bf16[232,1024]{1,0:T(8,128)(2,1)} %collective-permute-done.2.refs_1_.refs_3_), channel_id=1, source_target_pairs={{0,2},{2,4},{4,6},{6,8},{8,10},{10,12},{12,14},{14,0},{1,3},{3,5},... | collective-permute-start | bytes 1425416 | tf_op jit(solution)/shard_map/ppermute | solution.py:51
  55.5 19.4 %collective-permute-start.9 = (bf16[232,1024]{1,0:T(8,128)(2,1)}, bf16[232,1024]{1,0:T(8,128)(2,1)}, u32[]{:S(2)}, u32[]{:S(2)}) collective-permute-start(bf16[232,1024]{1,0:T(8,128)(2,1)} %collective-permute-done.5.refs_0_.refs_6_), channel_id=1, source_target_pairs={{0,2},{2,4},{4,6},{6,8},{8,10},{10,12},{12,14},{14,0},{1,3},{3,5},... | collective-permute-start | bytes 1425416 | tf_op jit(solution)/shard_map/ppermute | solution.py:51
  59.4 20.4 %collective-permute-start.12 = (bf16[232,1024]{1,0:T(8,128)(2,1)}, bf16[232,1024]{1,0:T(8,128)(2,1)}, u32[]{:S(2)}, u32[]{:S(2)}) collective-permute-start(bf16[232,1024]{1,0:T(8,128)(2,1)} %collective-permute-done.8.refs_3_.refs_9_), channel_id=1, source_target_pairs={{0,14},{2,0},{4,2},{6,4},{8,6},{10,8},{12,10},{14,12},{1,15},{3,1}... | collective-permute-start | bytes 1425416 | tf_op jit(solution)/shard_map/ppermute | solution.py:51
  69.6 29.0 %collective-permute-start.11 = (bf16[232,1024]{1,0:T(8,128)(2,1)}, bf16[232,1024]{1,0:T(8,128)(2,1)}, u32[]{:S(2)}, u32[]{:S(2)}) collective-permute-start(bf16[232,1024]{1,0:T(8,128)(2,1)} %collective-permute-done.7.refs_2_.refs_8_), channel_id=1, source_target_pairs={{0,14},{2,0},{4,2},{6,4},{8,6},{10,8},{12,10},{14,12},{1,15},{3,1}... | collective-permute-start | bytes 1425416 | tf_op jit(solution)/shard_map/ppermute | solution.py:51
  73.0 25.6 %collective-permute-start.10 = (bf16[232,1024]{1,0:T(8,128)(2,1)}, bf16[232,1024]{1,0:T(8,128)(2,1)}, u32[]{:S(2)}, u32[]{:S(2)}) collective-permute-start(bf16[232,1024]{1,0:T(8,128)(2,1)} %collective-permute-done.6.refs_1_.refs_7_), channel_id=1, source_target_pairs={{0,2},{2,4},{4,6},{6,8},{8,10},{10,12},{12,14},{14,0},{1,3},{3,5},... | collective-permute-start | bytes 1425416 | tf_op jit(solution)/shard_map/ppermute | solution.py:51
  74.9 29.0 %collective-permute-start.13 = (bf16[232,1024]{1,0:T(8,128)(2,1)}, bf16[232,1024]{1,0:T(8,128)(2,1)}, u32[]{:S(2)}, u32[]{:S(2)}) collective-permute-start(bf16[232,1024]{1,0:T(8,128)(2,1)} %collective-permute-done.9.refs_0_.refs_10_), channel_id=1, source_target_pairs={{0,2},{2,4},{4,6},{6,8},{8,10},{10,12},{12,14},{14,0},{1,3},{3,5},... | collective-permute-start | bytes 1425416 | tf_op jit(solution)/shard_map/ppermute | solution.py:51
  79.8 24.1 %collective-permute-start.14 = (bf16[232,1024]{1,0:T(8,128)(2,1)}, bf16[232,1024]{1,0:T(8,128)(2,1)}, u32[]{:S(2)}, u32[]{:S(2)}) collective-permute-start(bf16[232,1024]{1,0:T(8,128)(2,1)} %collective-permute-done.12.refs_3_.refs_13_), channel_id=1, source_target_pairs={{0,14},{2,0},{4,2},{6,4},{8,6},{10,8},{12,10},{14,12},{1,15},{3,1}... | collective-permute-start | bytes 1425416 | tf_op jit(solution)/shard_map/ppermute | solution.py:51
  88.4 18.5 %copy-start.49 = (f32[2,384]{1,0:T(2,128)}, f32[2,384]{1,0:T(2,128)S(1)}, u32[]{:S(2)}) copy-start(f32[2,384]{1,0:T(2,128)S(1)} %get-tuple-element.45.refs_26_.refs_0_) | copy-start | bytes 9220
  92.0 0.8 copy-start.17
  93.4 13.5 %copy-start.8 = (bf16[128,1024]{1,0:T(8,128)(2,1)}, bf16[128,1024]{1,0:T(8,128)(2,1)S(1)}, u32[]{:S(2)}) copy-start(bf16[128,1024]{1,0:T(8,128)(2,1)S(1)} %get-tuple-element.41.refs_22_.refs_6_) | copy-start | bytes 786436
  93.4 29.6 %slice-start = ((s8[6291456]{0:T(1024)(128)(4,1)}), s8[4194304]{0:T(1024)(128)(4,1)S(1)}, s32[]{:S(2)}) async-start(s8[6291456]{0:T(1024)(128)(4,1)} %bitcast.32), calls=%async_computation.6 | async-start | bytes 8388608
  97.2 0.7 copy-start.19
  98.6 8.3 %copy-start.10 = (bf16[128,1024]{1,0:T(8,128)(2,1)}, bf16[128,1024]{1,0:T(8,128)(2,1)S(1)}, u32[]{:S(2)}) copy-start(bf16[128,1024]{1,0:T(8,128)(2,1)S(1)} %get-tuple-element.42.refs_23_.refs_7_) | copy-start | bytes 786436
  98.7 24.4 %slice-start.1 = ((s8[6291456]{0:T(1024)(128)(4,1)}), s8[2097152]{0:T(1024)(128)(4,1)S(1)}, s32[]{:S(2)}) async-start(s8[6291456]{0:T(1024)(128)(4,1)} %bitcast.32), calls=%async_computation.7 | async-start | bytes 4194304
  102.5 0.7 copy-start.21
  103.9 3.1 %copy-start.12 = (bf16[128,1024]{1,0:T(8,128)(2,1)}, bf16[128,1024]{1,0:T(8,128)(2,1)S(1)}, u32[]{:S(2)}) copy-start(bf16[128,1024]{1,0:T(8,128)(2,1)S(1)} %get-tuple-element.43.refs_24_.refs_8_) | copy-start | bytes 786436
  103.9 3.1 %copy-start.42 = (f32[4,384]{1,0:T(4,128)}, f32[4,384]{1,0:T(4,128)S(1)}, u32[]{:S(2)}) copy-start(f32[4,384]{1,0:T(4,128)S(1)} %get-tuple-element.48.refs_29_.refs_3_) | copy-start | bytes 18436
  103.9 3.1 %copy-start.1 = (bf16[384,3072]{1,0:T(8,128)(2,1)S(1)}, bf16[384,3072]{1,0:T(8,128)(2,1)}, u32[]{:S(2)}) copy-start(bf16[384,3072]{1,0:T(8,128)(2,1)} %refs_1_.1) | copy-start | bytes 7077892
  107.0 16.1 %copy-start.46 = (f32[3072]{0:T(1024)S(1)}, f32[3072]{0:T(1024)}, u32[]{:S(2)}) copy-start(f32[3072]{0:T(1024)} %param.28) | copy-start | bytes 36868
  107.0 16.1 %copy-start.47 = (f32[3072]{0:T(1024)S(1)}, f32[3072]{0:T(1024)}, u32[]{:S(2)}) copy-start(f32[3072]{0:T(1024)} %param.29) | copy-start | bytes 36868
  107.0 16.1 %copy-start.48 = (f32[3072]{0:T(1024)S(1)}, f32[3072]{0:T(1024)}, u32[]{:S(2)}) copy-start(f32[3072]{0:T(1024)} %param.30) | copy-start | bytes 36868
  123.1 7.4 %copy-start.9 = (bf16[128,1024]{1,0:T(8,128)(2,1)S(1)}, bf16[128,1024]{1,0:T(8,128)(2,1)}, u32[]{:S(2)}) copy-start(bf16[128,1024]{1,0:T(8,128)(2,1)} %copy-done.8) | copy-start | bytes 786436
  123.1 7.4 %copy-start.11 = (bf16[128,1024]{1,0:T(8,128)(2,1)S(1)}, bf16[128,1024]{1,0:T(8,128)(2,1)}, u32[]{:S(2)}) copy-start(bf16[128,1024]{1,0:T(8,128)(2,1)} %copy-done.10) | copy-start | bytes 786436
  123.1 7.4 %copy-start.13 = (bf16[128,1024]{1,0:T(8,128)(2,1)S(1)}, bf16[128,1024]{1,0:T(8,128)(2,1)}, u32[]{:S(2)}) copy-start(bf16[128,1024]{1,0:T(8,128)(2,1)} %copy-done.12) | copy-start | bytes 786436
  123.2 7.4 %copy-start.16 = (bf16[64,1024]{1,0:T(8,128)(2,1)S(1)}, bf16[64,1024]{1,0:T(8,128)(2,1)}, u32[]{:S(2)}) copy-start(bf16[64,1024]{1,0:T(8,128)(2,1)} %copy-done.15) | copy-start | bytes 393220
  123.2 7.4 %copy-start.33 = (bf16[128,512]{1,0:T(8,128)(2,1)S(1)}, bf16[128,512]{1,0:T(8,128)(2,1)}, u32[]{:S(2)}) copy-start(bf16[128,512]{1,0:T(8,128)(2,1)} %copy-done.32) | copy-start | bytes 393220
  123.2 7.4 %copy-start.35 = (bf16[128,512]{1,0:T(8,128)(2,1)S(1)}, bf16[128,512]{1,0:T(8,128)(2,1)}, u32[]{:S(2)}) copy-start(bf16[128,512]{1,0:T(8,128)(2,1)} %copy-done.34) | copy-start | bytes 393220
  123.2 7.4 %copy-start.37 = (bf16[128,512]{1,0:T(8,128)(2,1)S(1)}, bf16[128,512]{1,0:T(8,128)(2,1)}, u32[]{:S(2)}) copy-start(bf16[128,512]{1,0:T(8,128)(2,1)} %copy-done.36) | copy-start | bytes 393220
  123.2 7.4 %copy-start.39 = (bf16[64,512]{1,0:T(8,128)(2,1)S(1)}, bf16[64,512]{1,0:T(8,128)(2,1)}, u32[]{:S(2)}) copy-start(bf16[64,512]{1,0:T(8,128)(2,1)} %copy-done.38) | copy-start | bytes 196612
  123.2 7.4 %copy-start.41 = (bf16[64,512]{1,0:T(8,128)(2,1)S(1)}, bf16[64,512]{1,0:T(8,128)(2,1)}, u32[]{:S(2)}) copy-start(bf16[64,512]{1,0:T(8,128)(2,1)} %copy-done.40) | copy-start | bytes 196612
  123.2 7.4 %copy-start.43 = (f32[4,384]{1,0:T(4,128)S(1)}, f32[4,384]{1,0:T(4,128)}, u32[]{:S(2)}) copy-start(f32[4,384]{1,0:T(4,128)} %copy-done.42) | copy-start | bytes 18436
  123.2 7.4 %copy-start.50 = (f32[2,384]{1,0:T(2,128)S(1)}, f32[2,384]{1,0:T(2,128)}, u32[]{:S(2)}) copy-start(f32[2,384]{1,0:T(2,128)} %copy-done.49) | copy-start | bytes 9220
  123.2 7.4 %copy-start.52 = (f32[2,384]{1,0:T(2,128)S(1)}, f32[2,384]{1,0:T(2,128)}, u32[]{:S(2)}) copy-start(f32[2,384]{1,0:T(2,128)} %copy-done.51) | copy-start | bytes 9220
  127.0 13.3 %all-to-all-start.4 = ((bf16[16,8,384]{2,1,0:T(8,128)(2,1)}), bf16[16,8,384]{2,1,0:T(8,128)(2,1)S(1)}, u32[]{:S(2)}, u32[]{:S(2)}) async-start(bf16[16,8,384]{2,1,0:T(8,128)(2,1)} %bitcast.16), calls=%async_computation.4 | async-start | bytes 196608 | tf_op jit(solution)/shard_map/all_to_all | solution.py:492
  134.4 1.1 copy-start.6
  135.5 1.0 copy-start.7
  170.0 31.6 %all-to-all-start.1 = ((bf16[16,32,1024]{2,1,0:T(8,128)(2,1)}), bf16[16,32,1024]{2,1,0:T(8,128)(2,1)S(1)}, u32[]{:S(2)}, u32[]{:S(2)}) async-start(bf16[16,32,1024]{2,1,0:T(8,128)(2,1)} %bitcast.38), calls=%async_computation.1 | async-start | bytes 2097152 | tf_op jit(solution)/shard_map/all_to_all | solution.py:492
  174.9 5.1 %copy-start.2 = (bf16[384,3072]{1,0:T(8,128)(2,1)S(1)}, bf16[384,3072]{1,0:T(8,128)(2,1)}, u32[]{:S(2)}) copy-start(bf16[384,3072]{1,0:T(8,128)(2,1)} %refs_1_.1) | copy-start | bytes 7077892
  174.9 5.1 %copy-start.18 = (f32[256,384]{1,0:T(8,128)S(1)}, f32[256,384]{1,0:T(8,128)}, u32[]{:S(2)}) copy-start(f32[256,384]{1,0:T(8,128)} %copy-done.17) | copy-start | bytes 1179652
  174.9 5.1 %copy-start.20 = (f32[256,384]{1,0:T(8,128)S(1)}, f32[256,384]{1,0:T(8,128)}, u32[]{:S(2)}) copy-start(f32[256,384]{1,0:T(8,128)} %copy-done.19) | copy-start | bytes 1179652
  174.9 5.1 %copy-start.22 = (f32[256,384]{1,0:T(8,128)S(1)}, f32[256,384]{1,0:T(8,128)}, u32[]{:S(2)}) copy-start(f32[256,384]{1,0:T(8,128)} %copy-done.21) | copy-start | bytes 1179652
  174.9 5.1 %copy-start.29 = (f32[128,384]{1,0:T(8,128)S(1)}, f32[128,384]{1,0:T(8,128)}, u32[]{:S(2)}) copy-start(f32[128,384]{1,0:T(8,128)} %copy-done.28) | copy-start | bytes 589828
  174.9 5.1 %copy-start.31 = (f32[128,384]{1,0:T(8,128)S(1)}, f32[128,384]{1,0:T(8,128)}, u32[]{:S(2)}) copy-start(f32[128,384]{1,0:T(8,128)} %copy-done.30) | copy-start | bytes 589828
  186.0 3.8 %collective-permute-start.15 = (bf16[1664,384]{1,0:T(8,128)(2,1)S(1)}, bf16[1664,384]{1,0:T(8,128)(2,1)S(1)}, u32[]{:S(2)}, u32[]{:S(2)}) collective-permute-start(bf16[1664,384]{1,0:T(8,128)(2,1)S(1)} %get-tuple-element.59), channel_id=1, source_target_pairs={{0,16},{16,0},{1,17},{17,1},{2,18},{18,2},{3,19},{19,3},{4,20},{20... | collective-permute-start | bytes 3833864 | tf_op jit(solution)/shard_map/ppermute | solution.py:51
  190.2 1.0 copy-start.3
  191.3 15.3 %copy-start.25 = (bf16[32,1024]{1,0:T(8,128)(2,1)S(1)}, bf16[32,1024]{1,0:T(8,128)(2,1)}, u32[]{:S(2)}) copy-start(bf16[32,1024]{1,0:T(8,128)(2,1)} %emb.3) | copy-start | bytes 196612
  201.5 1.0 copy-start.4
  202.5 22.2 %all-to-all-start.5 = ((bf16[8,208,384]{2,1,0:T(8,128)(2,1)}), bf16[8,208,384]{2,1,0:T(8,128)(2,1)S(1)}, u32[]{:S(2)}, u32[]{:S(2)}) async-start(bf16[8,208,384]{2,1,0:T(8,128)(2,1)} %bitcast.35), calls=%async_computation.5 | async-start | bytes 2555904 | tf_op jit(solution)/shard_map/all_to_all | solution.py:492
  206.6 1.2 copy-start.5
  206.6 1.2 copy-start.27
  (13 other events, 8.8 us)
where the time goes:
time: 228 us; the launch traced here: 227 us
  waiting for transfers between devices  63.2 us (28%)
  starting transfers between devices  54.4 us (24%)
  blocking collectives  45.2 us (20%)
  Pallas kernels  42.7 us (19%)
  local copies, waits for them, and re-layouts  18.6 us (8%)
  between operations  2.62 us (1%)
    all_to_all x2, blocking collectives, swap(): return lax.all_to_all(parts, axes, 0, 0, tiled=True).reshape(rows, columns)  45.2 us
    ppermute x16, waiting for transfers between devices, hop(): lax.ppermute(value, axis, [(i, (i + step) % length) for i in range(length)])  33.2 us
    ppermute x16, starting transfers between devices, hop(): lax.ppermute(value, axis, [(i, (i + step) % length) for i in range(length)])  31.6 us
    all_to_all x4, waiting for transfers between devices, swap(): return lax.all_to_all(parts, axes, 0, 0, tiled=True).reshape(rows, columns)  30 us
    all_to_all x4, starting transfers between devices, swap(): return lax.all_to_all(parts, axes, 0, 0, tiled=True).reshape(rows, columns)  22.8 us
    unnamed x115, local copies, waits for them, and re-layouts  17.4 us
    pallas_call x5, Pallas kernels, step(): pl.pallas_call(functools.partial(step_kernel, count), out_shape=(shape(co...  16.7 us
    pallas_call x1, Pallas kernels, backward(): pl.pallas_call(back_kernel, out_shape=(out, out), in_specs=whole(3 + len(...  5.99 us
  transfers between devices with their start and end apart: 20, of which 10 were waited for; matrix products, arithmetic and copies ran while one was open for 1% of the time, Pallas kernels for 14%

commit v1 on v0

v1 whole, which is shorter than its diff:
```python
import functools
import math

import jax
import jax.numpy as jnp
from jax import lax
from jax.experimental import pallas as pl
from jax.experimental.pallas import tpu as pltpu
from jax.sharding import Mesh
from jax.sharding import PartitionSpec as P

KERNEL = 7
SIDE = 8
PATCHES = SIDE * SIDE
DP = ("ylo", "x", "core")
FSDP = ("z", "yhi")
ALL = DP + FSDP
NZ = 8
PAIRS = 32
EMBED = 1024
WIDTH = 3072
HID = 384
SEG = WIDTH // EMBED
IMG_AT = SEG * PATCHES
ROWS = IMG_AT + PAIRS + 8
TXT_ROWS = PAIRS + 8
SLAB = WIDTH // 16
HALF = SLAB + 16
FULL = HALF + 32
BF = jnp.bfloat16
F32 = jnp.float32

GROUPS = [[(0, 0), (0, 1)]]
for _step in range(1, NZ // 2):
    GROUPS.append([(NZ - _step, 0), (NZ - _step, 1), (_step, 0), (_step, 1)])
GROUPS.append([(NZ // 2, 0), (NZ // 2, 1)])
KEYS = [key for group in GROUPS for key in group]
UNITS = len(GROUPS)


def params(mib):
    return pltpu.CompilerParams(vmem_limit_bytes=mib << 20)


def cost(micros):
    return pl.CostEstimate(flops=0, transcendentals=0, bytes_accessed=int(micros * 3_690_000))


def whole(count):
    return [pl.BlockSpec(memory_space=pltpu.VMEM)] * count


def loose(count):
    return [pl.BlockSpec(memory_space=pl.ANY)] * count


def near(rows, columns, dtype):
    return jax.ShapeDtypeStruct((rows, columns), dtype)


def far(rows, columns, dtype):
    return pltpu.HBM((rows, columns), dtype)


def from_far(*arrays):
    return [pltpu.with_memory_space_constraint(array, pltpu.HBM) for array in arrays]


def hop(value, axis, length, step):
    return lax.ppermute(value, axis, [(i, (i + step) % length) for i in range(length)])


def absolute(key):
    z = lax.rem(lax.axis_index("z") + key[0], NZ)
    y = lax.axis_index("yhi")
    return z * 2 + (y if key[1] == 0 else 1 - y)


def unit_rows(values):
    length = jnp.sqrt(jnp.sum(values * values, axis=1, keepdims=True) + 1e-06)
    return (values / length, length)


def front_kernel(
    img, txt, img_ids, txt_ids, block_in, taps, gain, bias, blk, txt_all, means, mixed, ids, txt_pay, sems
):
    def id_rows(source):
        ids[...] = jnp.zeros_like(ids)
        ids[0:1, 0:PAIRS] = source[...]
        row = lax.broadcasted_iota(jnp.int32, (8, EMBED), 0)
        value = jnp.broadcast_to(ids[0:1, :], (8, EMBED))
        return jnp.where(row == 0, value >> 7, jnp.where(row == 1, value & 127, 0)).astype(F32)

    blk[IMG_AT : IMG_AT + PAIRS, :] = unit_rows(img[...].astype(F32))[0].astype(BF)
    blk[IMG_AT + PAIRS : ROWS, :] = id_rows(img_ids).astype(BF)
    txt_pay[0:PAIRS, :] = unit_rows(txt[...].astype(F32))[0].astype(BF)
    place = (lax.axis_index("ylo") * 4 + lax.axis_index("x")) * 2 + lax.axis_index("core")
    txt_pay[PAIRS:TXT_ROWS, :] = pltpu.roll(id_rows(txt_ids), place * PAIRS, 1).astype(BF)

    copies = [
        pltpu.make_async_copy(
            txt_pay, txt_all.at[d * TXT_ROWS : (d + 1) * TXT_ROWS, :], sems.at[d]
        )
        for d in range(16)
    ]
    for copy in copies:
        copy.start()

    column = lax.broadcasted_iota(jnp.int32, (SIDE, 128), 0)

    def lanes(c, sums):
        at = pl.ds(pl.multiple_of(c * 128, 128), 128)
        patch = block_in[:, at].astype(F32)
        rows = [patch[r * SIDE : (r + 1) * SIDE] for r in range(SIDE)]
        total = rows[0]
        for r in range(1, SIDE):
            total = total + rows[r]
        mean = jnp.sum(total, axis=0, keepdims=True) / PATCHES
        means[0:1, at] = mean.astype(BF).astype(F32)
        acc = [jnp.zeros((SIDE, 128), F32) for _ in range(SIDE)]
        for across in range(KERNEL):
            move = across - KERNEL // 2
            if move == 0:
                moved = rows
            else:
                inside = (column + move >= 0) & (column + move < SIDE)
                moved = [
                    jnp.where(inside, pltpu.roll(row, (-move) % SIDE, 0), 0.0) for row in rows
                ]
            for above in range(KERNEL):
                tap = taps[above * KERNEL + across : above * KERNEL + across + 1, at]
                for r in range(SIDE):
                    source = r + above - KERNEL // 2
                    if 0 <= source < SIDE:
                        acc[r] = acc[r] + tap * moved[source]
        for r in range(SIDE):
            mixed[r * SIDE : (r + 1) * SIDE, at] = acc[r]
        return tuple(s + a for s, a in zip(sums, acc))

    sums = lax.fori_loop(
        0, WIDTH // 128, lanes, tuple(jnp.zeros((SIDE, 128), F32) for _ in range(SIDE))
    )
    centre = jnp.concatenate(
        [jnp.sum(s, axis=1, keepdims=True) / WIDTH for s in sums], axis=0
    )
    square = jnp.zeros((PATCHES, 128), F32)
    for c in range(WIDTH // 128):
        off = mixed[:, c * 128 : (c + 1) * 128] - centre
        square = square + off * off
    inverse = 1.0 / jnp.sqrt(jnp.sum(square, axis=1, keepdims=True) / WIDTH + 1e-06)
    for c in range(WIDTH // 128):
        at = slice(c * 128, (c + 1) * 128)
        normal = (mixed[:, at] - centre) * inverse
        seg, lane = divmod(c * 128, EMBED)
        blk[seg * PATCHES : (seg + 1) * PATCHES, lane : lane + 128] = (
            normal * gain[:, at] + bias[:, at]
        ).astype(BF)
    for copy in copies:
        copy.wait()


def front(*args):
    return pl.pallas_call(
        front_kernel,
        out_shape=(
            near(ROWS, EMBED, BF),
            far(16 * TXT_ROWS, EMBED, BF),
            far(1, WIDTH, F32),
        ),
        out_specs=(pl.BlockSpec(), *loose(1), pl.BlockSpec()),
        scratch_shapes=[
            pltpu.VMEM((PATCHES, WIDTH), F32),
            pltpu.VMEM((8, EMBED), jnp.int32),
            pltpu.VMEM((TXT_ROWS, EMBED), BF),
            pltpu.SemaphoreType.DMA((16,)),
        ],
        compiler_params=params(8),
        cost_estimate=cost(4.5),
        name="front",
    )(*from_far(*args))


def turn_into(blocks, turn):
    for seg in range(SEG):
        at = slice(seg * PATCHES, (seg + 1) * PATCHES)
        for p in range(len(blocks) // 2):
            rows = jnp.concatenate([b[at, :] for b in blocks[2 * p : 2 * p + 2]], axis=0)
            turn[seg * EMBED : (seg + 1) * EMBED, p * 128 : (p + 1) * 128] = jnp.transpose(rows)


def step_kernel(count, *refs):
    blocks, refs = refs[:count], refs[count:]
    w_up, texts, temp_log, logit_bias, *refs = refs
    outs, (sums, firsts), scratch, sems = refs[:4], refs[4:6], refs[6:10], refs[10]
    slope, image_part, weights, turn = scratch
    copies = [
        pltpu.make_async_copy(source, into, sems.at[i])
        for i, (source, into) in enumerate(zip(scratch, outs))
    ]
    turn_into(blocks, turn)
    copies[3].start()
    root = math.sqrt(2.0 / math.pi)
    hidden = None
    for seg in range(SEG):
        rows = jnp.concatenate(
            [b[seg * PATCHES : (seg + 1) * PATCHES, :] for b in blocks], axis=0
        )
        part = jnp.dot(
            rows, w_up[seg * EMBED : (seg + 1) * EMBED, :], preferred_element_type=F32
        )
        hidden = part if hidden is None else hidden + part
    square = hidden * hidden
    curve = jnp.tanh(root * (hidden + 0.044715 * (square * hidden)))
    half = 0.5 * (1.0 + curve)
    active = (hidden * half).astype(BF).astype(F32)
    slope[...] = half + 0.5 * hidden * (1.0 - curve * curve) * (
        root * (1.0 + 3.0 * 0.044715 * square)
    )
    copies[0].start()
    for i in range(count):
        sums[i : i + 1, :] = jnp.sum(
            active[i * PATCHES : (i + 1) * PATCHES], axis=0, keepdims=True
        )

    temper = jnp.exp(temp_log[...])
    text_rows = jnp.concatenate(
        [texts[d * TXT_ROWS : d * TXT_ROWS + PAIRS, :] for d in range(16)], axis=0
    )
    digits = texts[PAIRS : PAIRS + 8, 0:512].astype(F32)
    for d in range(1, 16):
        at = d * TXT_ROWS + PAIRS
        digits = digits + texts[at : at + 8, 0:512].astype(F32)
    text_ids = digits[0:1] * 128.0 + digits[1:2]
    columns = []
    for b in blocks:
        pair = b[IMG_AT + PAIRS : ROWS, 0:128].astype(F32)
        row = jnp.broadcast_to(pair[0:1] * 128.0 + pair[1:2], (128, 128))
        columns.append(jnp.transpose(row)[0:PAIRS, 0:1])
    image_ids = jnp.concatenate(columns, axis=0)
    images = jnp.concatenate([b[IMG_AT : IMG_AT + PAIRS, :] for b in blocks], axis=0)
    scores = lax.dot_general(
        images, text_rows, (((1,), (1,)), ((), ())), preferred_element_type=F32
    )
    logits = temper * scores + logit_bias[...]
    labels = jnp.where(image_ids == text_ids, 1.0, -1.0)
    weight = (temper * -labels * jax.nn.sigmoid(-labels * logits)).astype(BF)
    weights[...] = weight
    copies[2].start()
    image = jnp.dot(weight, text_rows, preferred_element_type=F32)
    image_part[...] = image.astype(BF)
    copies[1].start()
    for i in range(count):
        firsts[i : i + 1, :] = image[i * PAIRS : i * PAIRS + 1]
    for copy in copies:
        copy.wait()


def step(blocks, w_up, texts, temp_log, logit_bias):
    count = len(blocks)
    dims = [
        (count * PATCHES, HID, F32),
        (count * PAIRS, EMBED, BF),
        (count * PAIRS, 16 * PAIRS, BF),
        (WIDTH, count * PATCHES, BF),
    ]
    return pl.pallas_call(
        functools.partial(step_kernel, count),
        out_shape=(
            *(far(*dim) for dim in dims),
            near(count, HID, F32),
            near(count, EMBED, F32),
        ),
        in_specs=whole(count + 4),
        out_specs=(*loose(4), *whole(2)),
        scratch_shapes=[pltpu.VMEM(dim[:2], dim[2]) for dim in dims]
        + [pltpu.SemaphoreType.DMA((4,))],
        compiler_params=params(14),
        cost_estimate=cost(1.5 + 0.8 * count),
        name="step",
    )(*blocks, w_up, texts, temp_log, logit_bias)


def mean_kernel(*refs):
    count = UNITS
    sums, firsts = refs[:count], refs[count : 2 * count]
    w_down, out, held = refs[2 * count :]
    mean = jnp.concatenate([s[...] for s in sums], axis=0) / PATCHES
    first = mean.astype(BF)
    rest = mean - first.astype(F32)
    second = rest.astype(BF)
    third = (rest - second.astype(F32)).astype(BF)
    three = jnp.dot(
        jnp.concatenate([first, second, third], axis=0), w_down[...], preferred_element_type=F32
    )
    partial = three[0:16] + three[16:32] + three[32:48]
    rows = jnp.concatenate([f[...] for f in firsts], axis=0)
    for c in range(6):
        held[:, c, :] = partial[:, c * 512 : (c + 1) * 512]
    for c in range(2):
        held[:, 6 + c, :] = rows[:, c * 512 : (c + 1) * 512]
    for j, key in enumerate(KEYS):
        at = pl.ds(pl.multiple_of(absolute(key) * 8, 8), 8)
        out[at, :] = held[j].astype(BF)


def mean_rows(sums, firsts, w_down):
    return pl.pallas_call(
        mean_kernel,
        out_shape=far(128, 512, BF),
        in_specs=whole(2 * len(GROUPS) + 1),
        scratch_shapes=[pltpu.VMEM((16, 8, 512), F32)],
        compiler_params=params(6),
        cost_estimate=cost(0.8),
        name="mean_rows",
    )(*sums, *firsts, w_down)


def head_kernel(parts, means, scale, gain, bias, w_far, out, w_proj, sems):
    quarter = WIDTH // 4
    copies = [
        pltpu.make_async_copy(
            w_far.at[i * quarter : (i + 1) * quarter, :],
            w_proj.at[i * quarter : (i + 1) * quarter, :],
            sems.at[i],
        )
        for i in range(4)
    ]
    for copy in copies:
        copy.start()
    total = parts[0:8, :].astype(F32)
    for d in range(1, 16):
        total = total + parts[d * 8 : (d + 1) * 8, :].astype(F32)
    block_mean = jnp.concatenate([total[c : c + 1] for c in range(6)], axis=1)
    image_sum = jnp.concatenate([total[6:7], total[7:8]], axis=1)
    pooled = means[...] + scale[...] * block_mean
    centred = pooled - jnp.sum(pooled, axis=1, keepdims=True) / WIDTH
    inverse = 1.0 / jnp.sqrt(jnp.sum(centred * centred, axis=1, keepdims=True) / WIDTH + 1e-06)
    head_norm = centred * inverse
    head_out = jnp.broadcast_to(head_norm * gain[...] + bias[...], (8, WIDTH)).astype(BF)
    embed = None
    for i in range(4):
        at = slice(i * quarter, (i + 1) * quarter)
        copies[i].wait()
        piece = jnp.dot(head_out[:, at], w_proj[at, :], preferred_element_type=F32)
        embed = piece if embed is None else embed + piece
    embed = embed[0:1]
    unit, length = unit_rows(embed)
    inner = jnp.sum(unit * image_sum, axis=1, keepdims=True)
    embed_grad = jnp.broadcast_to((image_sum - unit * inner) / length, (8, EMBED)).astype(BF)
    head_grad = lax.dot_general(
        embed_grad, w_proj[...], (((1,), (1,)), ((), ())), preferred_element_type=F32
    )[0:1]
    norm_grad = head_grad * gain[...]
    pool_grad = inverse * (
        norm_grad
        - jnp.sum(norm_grad, axis=1, keepdims=True) / WIDTH
        - head_norm * (jnp.sum(norm_grad * head_norm, axis=1, keepdims=True) / WIDTH)
    )
    row = scale[...] * pool_grad / PATCHES
    tile = jnp.concatenate([row[:, c * HID : (c + 1) * HID] for c in range(8)], axis=0).astype(BF)
    for d in range(16):
        out[d * 8 : (d + 1) * 8, :] = tile


def head(parts, means, scale, gain, bias, w_proj):
    return pl.pallas_call(
        head_kernel,
        out_shape=far(128, HID, BF),
        in_specs=whole(5) + loose(1),
        scratch_shapes=[pltpu.VMEM((WIDTH, EMBED), BF), pltpu.SemaphoreType.DMA((4,))],
        compiler_params=params(14),
        cost_estimate=cost(5.0),
        name="head",
    )(parts, *from_far(means, scale, gain, bias, w_proj))


def text_kernel(*refs):
    blocks = refs[:16]
    weights, images = (refs[16 + i * UNITS : 16 + (i + 1) * UNITS] for i in range(2))
    txt_send, txt_keep, img_send, img_keep, rows, weight, image, sems = refs[16 + 2 * UNITS :]
    copies, first = [], 0
    for u, group in enumerate(GROUPS):
        at = slice(first, first + len(group) * PAIRS)
        first += len(group) * PAIRS
        copies.append(pltpu.make_async_copy(weights[u], weight.at[at, :], sems.at[2 * u]))
        copies.append(pltpu.make_async_copy(images[u], image.at[at, :], sems.at[2 * u + 1]))
    for i in range(16):
        at = slice(i * PAIRS, (i + 1) * PAIRS)
        source = blocks[i].at[IMG_AT : IMG_AT + PAIRS, :]
        copies.append(pltpu.make_async_copy(source, rows.at[at, :], sems.at[2 * UNITS + i]))
    for copy in copies:
        copy.start()
    for copy in copies:
        copy.wait()
    text_part = lax.dot_general(
        weight[...], rows[...], (((0,), (0,)), ((), ())), preferred_element_type=F32
    ).astype(BF)
    core = lax.axis_index("core")
    for k in range(8):
        at = slice(k * PAIRS, (k + 1) * PAIRS)
        even = text_part[2 * k * PAIRS : (2 * k + 1) * PAIRS]
        odd = text_part[(2 * k + 1) * PAIRS : (2 * k + 2) * PAIRS]

        @pl.when(core == 0)
        def _():
            txt_keep[at, :] = even
            txt_send[at, :] = odd

        @pl.when(core == 1)
        def _():
            txt_keep[at, :] = odd
            txt_send[at, :] = even

    z = lax.axis_index("z")
    for j, (offset, side) in enumerate(KEYS):
        owner = lax.rem(z + offset, NZ)
        place = (owner & 1) * 4 + (owner & 2) + (owner >> 2)
        at = pl.ds(pl.multiple_of(place * PAIRS, PAIRS), PAIRS)
        into = img_keep if side == 0 else img_send
        into[at, :] = image[j * PAIRS : (j + 1) * PAIRS, :]


def text_parts(blocks, weights, images):
    return pl.pallas_call(
        text_kernel,
        out_shape=(far(8 * PAIRS, EMBED, BF),) * 4,
        in_specs=loose(16 + 2 * UNITS),
        out_specs=tuple(whole(4)),
        scratch_shapes=[
            pltpu.VMEM((16 * PAIRS, EMBED), BF),
            pltpu.VMEM((16 * PAIRS, 16 * PAIRS), BF),
            pltpu.VMEM((16 * PAIRS, EMBED), BF),
            pltpu.SemaphoreType.DMA((16 + 2 * UNITS,)),
        ],
        compiler_params=params(14),
        cost_estimate=cost(3.8),
        name="text_parts",
    )(*blocks, *from_far(*weights, *images))


def halve_kernel(bits, *refs):
    keeps, gots, sends, outs = (refs[2 * i : 2 * i + 2] for i in range(4))
    for (axis, shift), first, second, send, keep in zip(bits, keeps, gots, sends, outs):
        mine = (lax.axis_index(axis) >> shift) & 1
        rows = send.shape[0]
        for part in range(2):
            at = slice(part * rows, (part + 1) * rows)
            total = (first[at, :].astype(F32) + second[at, :].astype(F32)).astype(BF)

            @pl.when(mine == part)
            def _():
                keep[...] = total

            @pl.when(mine != part)
            def _():
                send[...] = total


def halved(bits, keeps, gots):
    outs = pl.pallas_call(
        functools.partial(halve_kernel, bits),
        out_shape=(far(keeps[0].shape[0] // 2, EMBED, BF),) * 4,
        in_specs=whole(4),
        compiler_params=params(8),
        cost_estimate=cost(1.5),
        name="halved",
    )(*from_far(*keeps), *gots)
    return outs[:2], outs[2:]


def partner(value, axis, length, bit):
    return lax.ppermute(value, axis, [(i, i ^ bit) for i in range(length)])


def back_kernel(*refs):
    grads, w_down = refs[:2]
    sums, slopes, turns = (refs[2 + i * UNITS : 2 + (i + 1) * UNITS] for i in range(3))
    send, keep, held, hid_grad, slope, rows, sems = refs[2 + 3 * UNITS :]
    slope_copies, low_copies, high_copies, first = [], [], [], 0
    low, high = slice(0, WIDTH // 2), slice(WIDTH // 2, WIDTH)
    for u, group in enumerate(GROUPS):
        at = slice(first, first + len(group) * PATCHES)
        first += len(group) * PATCHES
        slope_copies.append(pltpu.make_async_copy(slopes[u], slope.at[at, :], sems.at[3 * u]))
        for half, into, sem in ((low, low_copies, 1), (high, high_copies, 2)):
            into.append(
                pltpu.make_async_copy(
                    turns[u].at[half, :], rows.at[half, at], sems.at[3 * u + sem]
                )
            )
    for copy in (*slope_copies, *low_copies, *high_copies):
        copy.start()
    total = jnp.concatenate([s[...] for s in sums], axis=0).astype(BF)
    keep[8 * HALF :, :] = total
    send[8 * HALF :, :] = total
    for j, key in enumerate(KEYS):
        at = pl.ds(pl.multiple_of(absolute(key) * 8, 8), 8)
        held[j] = grads[at, :].astype(F32)
    group = jnp.concatenate([held[:, c, :] for c in range(8)], axis=1)
    row_down = lax.dot_general(
        group.astype(BF), w_down[...], (((1,), (1,)), ((), ())), preferred_element_type=F32
    )
    for copy in slope_copies:
        copy.wait()
    for j in range(16):
        at = slice(j * PATCHES, (j + 1) * PATCHES)
        hid_grad[at, :] = (slope[at, :] * row_down[j : j + 1]).astype(BF)
    for copy in low_copies:
        copy.wait()
    low, high = slice(0, SLAB), slice(SLAB, 2 * SLAB)
    core = lax.axis_index("core")
    for k in range(8):
        if k == 4:
            for copy in high_copies:
                copy.wait()
        part = jnp.dot(
            rows[k * 2 * SLAB : (k + 1) * 2 * SLAB, :], hid_grad[...], preferred_element_type=F32
        ).astype(BF)
        mine = group[:, k * 2 * SLAB : (k + 1) * 2 * SLAB]
        swapped = pltpu.roll(mine, SLAB, 1).astype(BF)
        mine = mine.astype(BF)
        at = slice(k * HALF, k * HALF + SLAB)
        below = slice(k * HALF + SLAB, (k + 1) * HALF)

        @pl.when(core == 0)
        def _():
            keep[at, :] = part[low]
            send[at, :] = part[high]
            keep[below, :] = mine
            send[below, :] = swapped

        @pl.when(core == 1)
        def _():
            keep[at, :] = part[high]
            send[at, :] = part[low]
            keep[below, :] = swapped
            send[below, :] = mine


def backward(grads, w_down, sums, slopes, turns):
    return pl.pallas_call(
        back_kernel,
        out_shape=(near(8 * HALF + 16, HID, BF),) * 2,
        in_specs=whole(2 + UNITS) + loose(2 * UNITS),
        out_specs=tuple(whole(2)),
        scratch_shapes=[
            pltpu.VMEM((16, 8, HID), F32),
            pltpu.VMEM((16 * PATCHES, HID), BF),
            pltpu.VMEM((16 * PATCHES, HID), F32),
            pltpu.VMEM((WIDTH, 16 * PATCHES), BF),
            pltpu.SemaphoreType.DMA((3 * UNITS,)),
        ],
        compiler_params=params(16),
        cost_estimate=cost(6.5),
        name="backward",
    )(grads, w_down, *sums, *from_far(*slopes, *turns))


def join_kernel(keep, got, out):
    lane = lax.broadcasted_iota(jnp.int32, (16, HID), 1)
    for k in range(8):
        at = slice(k * HALF, k * HALF + SLAB)
        below = slice(k * HALF + SLAB, (k + 1) * HALF)
        to = k * FULL
        out[to : to + SLAB, :] = (keep[at, :].astype(F32) + got[at, :].astype(F32)).astype(BF)
        other = pltpu.roll(got[below, :].astype(F32), SLAB, 1)
        out[to + SLAB : to + HALF, :] = jnp.where(
            lane < SLAB, keep[below, :].astype(F32), other
        ).astype(BF)
        out[to + HALF : to + HALF + 16, :] = keep[8 * HALF :, :]
        out[to + HALF + 16 : to + FULL, :] = got[8 * HALF :, :]


def join(keep, got):
    return pl.pallas_call(
        join_kernel,
        out_shape=far(8 * FULL, HID, BF),
        in_specs=whole(2),
        compiler_params=params(12),
        cost_estimate=cost(1.0),
        name="join",
    )(keep, got)


def last_kernel(got, up_out, down_out):
    total = got[0:SLAB, :].astype(F32)
    for k in range(1, 8):
        total = total + got[k * FULL : k * FULL + SLAB, :].astype(F32)
    up_out[...] = total
    grads = jnp.concatenate(
        [got[k * FULL + SLAB : k * FULL + HALF, :] for k in range(8)], axis=0
    )
    others = pltpu.roll(grads.astype(F32), SLAB, 1).astype(BF)
    down = None
    for side, left in enumerate((grads, others)):
        right = jnp.concatenate(
            [
                got[k * FULL + HALF + side * 16 : k * FULL + HALF + side * 16 + 16, :]
                for k in range(8)
            ],
            axis=0,
        )
        part = lax.dot_general(
            left, right, (((0,), (0,)), ((), ())), preferred_element_type=F32
        )
        down = part if down is None else down + part
    down_out[...] = down[0:SLAB, :]


def last(got):
    return pl.pallas_call(
        last_kernel,
        out_shape=(far(SLAB, HID, F32), far(SLAB, HID, F32)),
        in_specs=whole(1),
        compiler_params=params(12),
        cost_estimate=cost(2.0),
        name="last",
    )(got)


def rows_kernel(count, *refs):
    emb, out = refs[count:]
    total = None
    for ref in refs[:count]:
        for d in range(ref.shape[0] // PAIRS):
            part = ref[d * PAIRS : (d + 1) * PAIRS, :].astype(F32)
            total = part if total is None else total + part
    unit, length = unit_rows(emb[...].astype(F32))
    inner = jnp.sum(unit * total, axis=1, keepdims=True)
    out[...] = (total - unit * inner) / length


def row_grads(parts, emb, name):
    return pl.pallas_call(
        functools.partial(rows_kernel, len(parts)),
        out_shape=far(PAIRS, EMBED, F32),
        compiler_params=params(8),
        cost_estimate=cost(0.9),
        name=name,
    )(*parts, *from_far(emb))


def swap(value, axes, count):
    rows, columns = value.shape
    parts = value.reshape(count, rows // count, columns)
    return lax.all_to_all(parts, axes, 0, 0, tiled=True).reshape(rows, columns)


def on_device(
    img_emb,
    txt_emb,
    img_ids,
    txt_ids,
    temp_log,
    logit_bias,
    block_in,
    dw_kernel,
    ln_gain,
    ln_bias,
    w_up,
    w_down,
    layer_scale,
    head_gain,
    head_bias,
    w_proj,
):
    blk, txt_all, means = front(
        img_emb,
        txt_emb,
        img_ids.reshape(1, PAIRS),
        txt_ids.reshape(1, PAIRS),
        block_in,
        dw_kernel,
        ln_gain.reshape(1, WIDTH),
        ln_bias.reshape(1, WIDTH),
    )
    temper = temp_log.reshape(1, 1)
    offset = logit_bias.reshape(1, 1)
    got = {(0, 0): blk}
    kept = []

    def send_on(side, distance, up=True, down=True):
        if up:
            got[NZ - distance, side] = hop(got[(NZ - distance + 1) % NZ, side], "z", NZ, 1)
        if down:
            got[distance, side] = hop(got[distance - 1, side], "z", NZ, -1)

    def tie(keys, *values):
        tied = lax.optimization_barrier((*(got[key] for key in keys), *values))
        got.update(zip(keys, tied))
        return tied[len(keys) :]

    def work(unit):
        return step([got[key] for key in GROUPS[unit]], w_up, texts, temper, offset)

    got[0, 1] = hop(blk, "yhi", 2, 1)
    texts = swap(txt_all, DP, 16)
    for distance in range(1, NZ // 2):
        send_on(0, distance)
        send_on(1, distance)
    send_on(0, NZ // 2, down=False)
    done = tie([(3, 1)], *work(0), *work(1))
    send_on(1, NZ // 2, up=False)
    kept += [done[:6], done[6:]]
    kept += [work(unit) for unit in range(2, UNITS)]

    slopes, images, weights, turns, sums, firsts = zip(*kept)
    means_out, *weights = lax.optimization_barrier((mean_rows(sums, firsts, w_down), *weights))
    parts = swap(means_out, FSDP, 16)
    txt_send, txt_keep, img_send, img_keep = text_parts(
        [got[key] for key in KEYS], weights, images
    )
    keeps = (txt_keep, img_keep)
    gots = (hop(txt_send, "core", 2, 1), hop(img_send, "yhi", 2, 1))
    parts, txt_got = lax.optimization_barrier((parts, gots[0]))
    grads = head(
        parts,
        means,
        layer_scale.reshape(1, WIDTH),
        head_gain.reshape(1, WIDTH),
        head_bias.reshape(1, WIDTH),
        w_proj,
    )
    grads, img_got = lax.optimization_barrier((grads, gots[1]))
    grads = swap(grads, FSDP, 16)
    sends, keeps = halved((("ylo", 0), ("z", 0)), keeps, (txt_got, img_got))
    gots = (partner(sends[0], "ylo", 2, 1), partner(sends[1], "z", NZ, 1))
    grads, *gots = lax.optimization_barrier((grads, *gots))
    send, keep = backward(grads, w_down, sums, slopes, turns)
    sends, keeps = halved((("x", 1), ("z", 1)), keeps, gots)
    send, *sends = lax.optimization_barrier((send, *sends))
    gots = (partner(sends[0], "x", 4, 2), partner(sends[1], "z", NZ, 2))
    got_core, *gots = lax.optimization_barrier((hop(send, "core", 2, 1), *gots))
    both = join(keep, got_core)
    sends, keeps = halved((("x", 0), ("z", 2)), keeps, gots)
    w_up_grad, w_down_grad = last(swap(both, ("ylo", "x"), 8))
    w_down_grad = w_down_grad.T
    txt_grad = row_grads((keeps[0], partner(sends[0], "x", 4, 1)), txt_emb, "txt_rows")
    img_grad = row_grads((keeps[1], partner(sends[1], "z", NZ, 4)), img_emb, "img_rows")
    return (img_grad, txt_grad, w_up_grad, w_down_grad)


def solution(mesh):
    split = Mesh(mesh.devices.reshape(2, 4, 2, NZ, 2), ALL)
    in_specs = (
        P(ALL, None),
        P(ALL, None),
        P(ALL),
        P(ALL),
        P(),
        P(),
        P(ALL, None),
        P(),
        P(),
        P(),
        P(None, FSDP),
        P(FSDP, None),
        P(),
        P(),
        P(),
        P(),
    )
    out_specs = (P(ALL, None), P(ALL, None), P(DP, FSDP), P(FSDP, DP))
    return jax.shard_map(
        on_device, mesh=split, in_specs=in_specs, out_specs=out_specs, check_vma=False
    )
```

time: 228 us -> 213 us (0.934)
  Pallas kernels: 42.7 us -> 60.1 us
  blocking collectives: 45.2 us -> 28.3 us
  local copies, waits for them, and re-layouts: 18.6 us -> 2.5 us
    all_to_all x4 -> x2, waiting for transfers between devices: 30 us -> 0.01 us  [swap(): return lax.all_to_all(parts, axes, 0, 0, tiled=True).reshape(rows, columns)]
    ppermute x0 -> x6, waiting for transfers between devices: none -> 23.3 us  [partner(): return lax.ppermute(value, axis, [(i, i ^ bit) for i in range(length)])]
    pallas_call x15 -> x17, Pallas kernels: 42.7 us -> 60.1 us  [the longest x5 22.4 us: step(): pl.pallas_call(functools.partial(step_kernel, count), out_shape=(*(far(*d...]
    all_to_all x2, blocking collectives: 45.2 us -> 28.3 us  [swap(): return lax.all_to_all(parts, axes, 0, 0, tiled=True).reshape(rows, columns)]
    unnamed x115 -> x20, local copies, waits for them, and re-layouts: 17.4 us -> 2.5 us
    all_to_all x4 -> x2, starting transfers between devices: 22.8 us -> 10.7 us  [swap(): return lax.all_to_all(parts, axes, 0, 0, tiled=True).reshape(rows, columns)]
    ppermute x16 -> x18, starting transfers between devices: 31.6 us -> 39.7 us  [hop(): lax.ppermute(value, axis, [(i, (i + step) % length) for i in range(length)])]
    ppermute x16 -> x18, waiting for transfers between devices: 33.2 us -> 39.5 us  [hop(): lax.ppermute(value, axis, [(i, (i + step) % length) for i in range(length)])]
  transfers between devices with their start and end apart: 20 -> 26, of which waited for: 10 -> 11; matrix products, arithmetic and copies ran while one was open for 1% -> 0% of each run, Pallas kernels for 14% -> 14%
where the time goes in v1:
time: 213 us; the launch traced here: 212 us
  waiting for transfers between devices  62.8 us (29%)
  Pallas kernels  60.1 us (28%)
  starting transfers between devices  56.3 us (26%)
  blocking collectives  28.3 us (13%)
  local copies, waits for them, and re-layouts  2.5 us (1%)
  between operations  2.13 us (1%)
    ppermute x18, starting transfers between devices, hop(): lax.ppermute(value, axis, [(i, (i + step) % length) for i in range(length)])  39.7 us
    ppermute x18, waiting for transfers between devices, hop(): lax.ppermute(value, axis, [(i, (i + step) % length) for i in range(length)])  39.5 us
    all_to_all x2, blocking collectives, swap(): return lax.all_to_all(parts, axes, 0, 0, tiled=True).reshape(rows, columns)  28.3 us
    ppermute x6, waiting for transfers between devices, partner(): return lax.ppermute(value, axis, [(i, i ^ bit) for i in range(length)])  23.3 us
    pallas_call x5, Pallas kernels, step(): pl.pallas_call(functools.partial(step_kernel, count), out_shape=(*(far(*d...  22.4 us
    all_to_all x2, starting transfers between devices, swap(): return lax.all_to_all(parts, axes, 0, 0, tiled=True).reshape(rows, columns)  10.7 us
    pallas_call x1, Pallas kernels, backward(): pl.pallas_call(back_kernel, out_shape=(near(8 * HALF + 16, HID, BF),) * 2...  7.6 us
    pallas_call x1, Pallas kernels, head(): pl.pallas_call(head_kernel, out_shape=far(128, HID, BF), in_specs=whole(5...  6.57 us
  transfers between devices with their start and end apart: 26, of which 11 were waited for; matrix products, arithmetic and copies ran while one was open for 0% of the time, Pallas kernels for 14%

profile of v1, /device:TPU:1, one launch (start us, length us, event | category | flops | bytes accessed | tf_op | source)
XLA Modules:
  0.0 212.1 jit_solution(3031824791878427506)
XLA Ops:
  0.6 5.6 %front.1 = (bf16[232,1024]{1,0:T(8,128)(2,1)S(1)}, bf16[640,1024]{1,0:T(8,128)(2,1)}, f32[1,3072]{1,0:T(1,128)}) custom-call(bf16[32,1024]{1,0:T(8,128)(2,1)} %refs_2_.6, bf16[32,1024]{1,0:T(8,128)(2,1)} %refs_2_.7, s32[1,32]{1,0:T(1,128)} %bitcast.40, s32[1,32]{1,0:T(1,128)} %bitcast.41, bf16[64,3072]{1,0:T(8,128)(2,1)} %block_in.1, f32[49,3072]{1,0:T(8,128)} %taps.1, ...), custom_call_target="tpu_custom_call" | custom-call | bytes 16605000 | tf_op jit(solution)/shard_map/front/pallas_call | solution.py:163
  6.2 0.0 copy-start
  6.2 3.8 %collective-permute-start = (bf16[232,1024]{1,0:T(8,128)(2,1)S(1)}, bf16[232,1024]{1,0:T(8,128)(2,1)S(1)}, u32[]{:S(2)}, u32[]{:S(2)}) collective-permute-start(bf16[232,1024]{1,0:T(8,128)(2,1)S(1)} %get-tuple-element.89.refs_0_), channel_id=1, source_target_pairs={{0,1},{1,0},{2,3},{3,2},{4,5},{5,4},{6,7},{7,6},{8,9},{9,8},{10,11... | collective-permute-start | bytes 1425416 | tf_op jit(solution)/shard_map/ppermute | solution.py:70
  10.0 1.6 collective-permute-start.1
  11.7 7.9 %collective-permute-done.refs_1_ = bf16[232,1024]{1,0:T(8,128)(2,1)S(1)} collective-permute-done((bf16[232,1024]{1,0:T(8,128)(2,1)S(1)}, bf16[232,1024]{1,0:T(8,128)(2,1)S(1)}, u32[]{:S(2)}, u32[]{:S(2)}) %collective-permute-start) | collective-permute-done | bytes 475168 | tf_op jit(solution)/shard_map/ppermute | solution.py:70
  19.6 6.4 %collective-permute-start.4 = (bf16[232,1024]{1,0:T(8,128)(2,1)S(1)}, bf16[232,1024]{1,0:T(8,128)(2,1)}, u32[]{:S(2)}, u32[]{:S(2)}) collective-permute-start(bf16[232,1024]{1,0:T(8,128)(2,1)S(1)} %collective-permute-done.refs_1_), channel_id=1, source_target_pairs={{0,14},{2,0},{4,2},{6,4},{8,6},{10,8},{12,10},{14,12},{1,15},{3,1}... | collective-permute-start | bytes 1425416 | tf_op jit(solution)/shard_map/ppermute | solution.py:70
  25.9 7.2 %all-to-all-start = ((bf16[16,40,1024]{2,1,0:T(8,128)(2,1)}), bf16[16,40,1024]{2,1,0:T(8,128)(2,1)}, u32[]{:S(2)}, u32[]{:S(2)}) async-start(bf16[16,40,1024]{2,1,0:T(8,128)(2,1)} %bitcast.32), calls=%async_computation | async-start | bytes 2621440 | tf_op jit(solution)/shard_map/all_to_all | solution.py:646
  33.1 0.7 collective-permute-start.3
  33.8 0.0 collective-permute-done.1.refs_0_.refs_2_
  33.8 0.7 collective-permute-start.5
  34.6 0.0 collective-permute-start.2
  34.6 0.0 collective-permute-done.4.refs_3_.refs_5_
  34.6 3.5 %collective-permute-start.8 = (bf16[232,1024]{1,0:T(8,128)(2,1)}, bf16[232,1024]{1,0:T(8,128)(2,1)}, u32[]{:S(2)}, u32[]{:S(2)}) collective-permute-start(bf16[232,1024]{1,0:T(8,128)(2,1)} %collective-permute-done.4.refs_3_.refs_5_), channel_id=1, source_target_pairs={{0,14},{2,0},{4,2},{6,4},{8,6},{10,8},{12,10},{14,12},{1,15},{3,1}... | collective-permute-start | bytes 1425416 | tf_op jit(solution)/shard_map/ppermute | solution.py:70
  38.1 7.4 %collective-permute-done.3.refs_2_.refs_4_ = bf16[232,1024]{1,0:T(8,128)(2,1)S(1)} collective-permute-done((bf16[232,1024]{1,0:T(8,128)(2,1)S(1)}, bf16[232,1024]{1,0:T(8,128)(2,1)S(1)}, u32[]{:S(2)}, u32[]{:S(2)}) %collective-permute-start.3) | collective-permute-done | bytes 475168 | tf_op jit(solution)/shard_map/ppermute | solution.py:70
  45.5 2.7 %collective-permute-start.7 = (bf16[232,1024]{1,0:T(8,128)(2,1)S(1)}, bf16[232,1024]{1,0:T(8,128)(2,1)}, u32[]{:S(2)}, u32[]{:S(2)}) collective-permute-start(bf16[232,1024]{1,0:T(8,128)(2,1)S(1)} %collective-permute-done.3.refs_2_.refs_4_), channel_id=1, source_target_pairs={{0,14},{2,0},{4,2},{6,4},{8,6},{10,8},{12,10},{14,12},{1,15},{3,1}... | collective-permute-start | bytes 1425416 | tf_op jit(solution)/shard_map/ppermute | solution.py:70
  48.2 0.8 copy-done.2
  49.0 8.5 %collective-permute-done.2.refs_1_.refs_3_ = bf16[232,1024]{1,0:T(8,128)(2,1)} collective-permute-done((bf16[232,1024]{1,0:T(8,128)(2,1)S(1)}, bf16[232,1024]{1,0:T(8,128)(2,1)}, u32[]{:S(2)}, u32[]{:S(2)}) %collective-permute-start.2) | collective-permute-done | bytes 475168 | tf_op jit(solution)/shard_map/ppermute | solution.py:70
  57.5 2.7 %collective-permute-start.12 = (bf16[232,1024]{1,0:T(8,128)(2,1)}, bf16[232,1024]{1,0:T(8,128)(2,1)}, u32[]{:S(2)}, u32[]{:S(2)}) collective-permute-start(bf16[232,1024]{1,0:T(8,128)(2,1)} %collective-permute-done.8.refs_3_.refs_9_), channel_id=1, source_target_pairs={{0,14},{2,0},{4,2},{6,4},{8,6},{10,8},{12,10},{14,12},{1,15},{3,1}... | collective-permute-start | bytes 1425416 | tf_op jit(solution)/shard_map/ppermute | solution.py:70
  61.4 4.4 %collective-permute-done.7.refs_2_.refs_8_ = bf16[232,1024]{1,0:T(8,128)(2,1)} collective-permute-done((bf16[232,1024]{1,0:T(8,128)(2,1)S(1)}, bf16[232,1024]{1,0:T(8,128)(2,1)}, u32[]{:S(2)}, u32[]{:S(2)}) %collective-permute-start.7) | collective-permute-done | bytes 475168 | tf_op jit(solution)/shard_map/ppermute | solution.py:70
  65.8 2.8 %collective-permute-start.11 = (bf16[232,1024]{1,0:T(8,128)(2,1)}, bf16[232,1024]{1,0:T(8,128)(2,1)}, u32[]{:S(2)}, u32[]{:S(2)}) collective-permute-start(bf16[232,1024]{1,0:T(8,128)(2,1)} %collective-permute-done.7.refs_2_.refs_8_), channel_id=1, source_target_pairs={{0,14},{2,0},{4,2},{6,4},{8,6},{10,8},{12,10},{14,12},{1,15},{3,1}... | collective-permute-start | bytes 1425416 | tf_op jit(solution)/shard_map/ppermute | solution.py:70
  68.6 0.0 all-to-all-done
  68.6 3.6 %step.5 = (f32[128,384]{1,0:T(8,128)}, bf16[64,1024]{1,0:T(8,128)(2,1)}, bf16[64,512]{1,0:T(8,128)(2,1)}, bf16[3072,128]{1,0:T(8,128)(2,1)}, f32[2,384]{1,0:T(2,128)S(1)}, /*index=5*/f32[2,1024]{1,0:T(2,128)S(1)}) custom-call(bf16[232,1024]{1,0:T(8,128)(2,1)S(1)} %get-tuple-element.89.refs_0_, bf16[232,1024]{1,0:T(8,128)(2,1)S(1)} %collective-permute-done.refs_1_, ...), custom_call_target="tpu_custom_call" | custom-call | bytes 11439000 | tf_op jit(solution)/shard_map/step/pallas_call | solution.py:266
  72.2 5.0 %step.6 = (f32[256,384]{1,0:T(8,128)}, bf16[128,1024]{1,0:T(8,128)(2,1)}, bf16[128,512]{1,0:T(8,128)(2,1)}, bf16[3072,256]{1,0:T(8,128)(2,1)}, f32[4,384]{1,0:T(4,128)S(1)}, /*index=5*/f32[4,1024]{1,0:T(4,128)S(1)}) custom-call(bf16[232,1024]{1,0:T(8,128)(2,1)} %collective-permute-done.1.refs_0_.refs_2_, ...), custom_call_target="tpu_custom_call" | custom-call | bytes 17343000 | tf_op jit(solution)/shard_map/step/pallas_call | solution.py:266
  77.2 0.0 collective-permute-done.9.refs_0_.refs_10_
  77.2 0.1 collective-permute-start.13
  77.3 0.5 collective-permute-done.6.refs_1_.refs_7_
  77.8 0.0 collective-permute-start.10
  77.8 0.0 collective-permute-done.12.refs_3_.refs_13_
  77.8 2.7 %collective-permute-start.14 = (bf16[232,1024]{1,0:T(8,128)(2,1)}, bf16[232,1024]{1,0:T(8,128)(2,1)S(1)}, u32[]{:S(2)}, u32[]{:S(2)}) collective-permute-start(bf16[232,1024]{1,0:T(8,128)(2,1)} %collective-permute-done.12.refs_3_.refs_13_), channel_id=1, source_target_pairs={{0,14},{2,0},{4,2},{6,4},{8,6},{10,8},{12,10},{14,12},{1,15},{3,1}... | collective-permute-start | bytes 1425416 | tf_op jit(solution)/shard_map/ppermute | solution.py:70
  80.5 5.1 %step.7 = (f32[256,384]{1,0:T(8,128)}, bf16[128,1024]{1,0:T(8,128)(2,1)}, bf16[128,512]{1,0:T(8,128)(2,1)}, bf16[3072,256]{1,0:T(8,128)(2,1)}, f32[4,384]{1,0:T(4,128)S(1)}, /*index=5*/f32[4,1024]{1,0:T(4,128)S(1)}) custom-call(bf16[232,1024]{1,0:T(8,128)(2,1)} %collective-permute-done.5.refs_0_.refs_6_, ...), custom_call_target="tpu_custom_call" | custom-call | bytes 17343000 | tf_op jit(solution)/shard_map/step/pallas_call | solution.py:266
  85.6 0.6 collective-permute-done.11.refs_2_.refs_12_
  86.2 10.2 %collective-permute-done.10.refs_1_.refs_11_ = bf16[232,1024]{1,0:T(8,128)(2,1)S(1)} collective-permute-done((bf16[232,1024]{1,0:T(8,128)(2,1)}, bf16[232,1024]{1,0:T(8,128)(2,1)S(1)}, u32[]{:S(2)}, u32[]{:S(2)}) %collective-permute-start.10) | collective-permute-done | bytes 475168 | tf_op jit(solution)/shard_map/ppermute | solution.py:70
  96.4 5.0 %step.8 = (f32[256,384]{1,0:T(8,128)}, bf16[128,1024]{1,0:T(8,128)(2,1)}, bf16[128,512]{1,0:T(8,128)(2,1)}, bf16[3072,256]{1,0:T(8,128)(2,1)}, f32[4,384]{1,0:T(4,128)S(1)}, /*index=5*/f32[4,1024]{1,0:T(4,128)S(1)}) custom-call(bf16[232,1024]{1,0:T(8,128)(2,1)} %collective-permute-done.9.refs_0_.refs_10_, ...), custom_call_target="tpu_custom_call" | custom-call | bytes 17343000 | tf_op jit(solution)/shard_map/step/pallas_call | solution.py:266
  101.4 0.0 collective-permute-done.14.refs_1_.refs_15_
  101.4 0.0 copy-start.1
  101.4 3.8 %step.9 = (f32[128,384]{1,0:T(8,128)}, bf16[64,1024]{1,0:T(8,128)(2,1)}, bf16[64,512]{1,0:T(8,128)(2,1)}, bf16[3072,128]{1,0:T(8,128)(2,1)}, f32[2,384]{1,0:T(2,128)S(1)}, /*index=5*/f32[2,1024]{1,0:T(2,128)S(1)}) custom-call(bf16[232,1024]{1,0:T(8,128)(2,1)S(1)} %collective-permute-done.13.refs_0_.refs_14_, ...), custom_call_target="tpu_custom_call" | custom-call | bytes 11439000 | tf_op jit(solution)/shard_map/step/pallas_call | solution.py:266
  105.2 1.2 mean_rows.1
  106.4 4.1 %text_parts.1 = (bf16[256,1024]{1,0:T(8,128)(2,1)}, bf16[256,1024]{1,0:T(8,128)(2,1)}, bf16[256,1024]{1,0:T(8,128)(2,1)}, bf16[256,1024]{1,0:T(8,128)(2,1)}) custom-call(bf16[232,1024]{1,0:T(8,128)(2,1)S(1)} %get-tuple-element.89.refs_0_, bf16[232,1024]{1,0:T(8,128)(2,1)S(1)} %collective-permute-done.refs_1_, ...), custom_call_target="tpu_custom_call" | custom-call | bytes 14022000 | tf_op jit(solution)/shard_map/text_parts/pallas_call | solution.py:424
  110.6 5.8 %collective-permute-start.15 = (bf16[256,1024]{1,0:T(8,128)(2,1)}, bf16[256,1024]{1,0:T(8,128)(2,1)S(1)}, u32[]{:S(2)}, u32[]{:S(2)}) collective-permute-start(bf16[256,1024]{1,0:T(8,128)(2,1)} %get-tuple-element.132), channel_id=1, source_target_pairs={{0,16},{16,0},{1,17},{17,1},{2,18},{18,2},{3,19},{19,3},{4,20},{20... | collective-permute-start | bytes 1572872 | tf_op jit(solution)/shard_map/ppermute | solution.py:70
  116.4 2.9 %collective-permute-start.16 = (bf16[256,1024]{1,0:T(8,128)(2,1)}, bf16[256,1024]{1,0:T(8,128)(2,1)S(1)}, u32[]{:S(2)}, u32[]{:S(2)}) collective-permute-start(bf16[256,1024]{1,0:T(8,128)(2,1)} %get-tuple-element.136), channel_id=1, source_target_pairs={{0,1},{1,0},{2,3},{3,2},{4,5},{5,4},{6,7},{7,6},{8,9},{9,8},{10,11... | collective-permute-start | bytes 1572872 | tf_op jit(solution)/shard_map/ppermute | solution.py:70
  119.3 13.1 %all_to_all.20 = bf16[16,8,512]{2,1,0:T(8,128)(2,1)S(1)} all-to-all(bf16[16,8,512]{2,1,0:T(8,128)(2,1)S(1)} %bitcast.33), channel_id=1, replica_groups=mesh['ylo'=2,'x'=4,'core'=2,'z'=8,'yhi'=2] {'z','yhi'}, dimensions={0} | all-to-all | bytes 262144 | tf_op jit(solution)/shard_map/all_to_all | solution.py:646
  132.4 6.6 %head.1 = bf16[128,384]{1,0:T(8,128)(2,1)} custom-call(bf16[128,512]{1,0:T(8,128)(2,1)S(1)} %bitcast.29, f32[1,3072]{1,0:T(1,128)} %get-tuple-element.135.means, f32[1,3072]{1,0:T(1,128)} %bitcast.37, f32[1,3072]{1,0:T(1,128)} %bitcast.38, f32[1,3072]{1,0:T(1,128)} %bitcast.39, bf16[3072,1024]{1,0:T(8,128)(2,1)} %w_far.1), custom_call_target="tpu_custom_call" | custom-call | bytes 18450000 | tf_op jit(solution)/shard_map/head/pallas_call | solution.py:366
  139.0 0.0 copy-start.7
  139.0 2.7 %halved.3 = (bf16[128,1024]{1,0:T(8,128)(2,1)}, bf16[128,1024]{1,0:T(8,128)(2,1)}, bf16[128,1024]{1,0:T(8,128)(2,1)}, bf16[128,1024]{1,0:T(8,128)(2,1)}) custom-call(bf16[256,1024]{1,0:T(8,128)(2,1)} %get-tuple-element.129.refs_0_, bf16[256,1024]{1,0:T(8,128)(2,1)} %get-tuple-element.130.refs_1_, bf16[256,1024]{1,0:T(8,128)(2,1)S(1)} %collective-permute-done.15.refs_2_, ...), custom_call_target="tpu_custom_call" | custom-call | bytes 5535000 | tf_op jit(solution)/shard_map/halved/pallas_call | solution.py:460
  141.7 1.4 collective-permute-start.17
  143.1 15.2 %all_to_all.21 = bf16[16,8,384]{2,1,0:T(8,128)(2,1)S(1)} all-to-all(bf16[16,8,384]{2,1,0:T(8,128)(2,1)S(1)} %bitcast.34), channel_id=1, replica_groups=mesh['ylo'=2,'x'=4,'core'=2,'z'=8,'yhi'=2] {'z','yhi'}, dimensions={0} | all-to-all | bytes 196608 | tf_op jit(solution)/shard_map/all_to_all | solution.py:646
  158.3 2.0 halved.4
  160.3 7.6 %backward.1 = (bf16[1680,384]{1,0:T(8,128)(2,1)S(1)}, bf16[1680,384]{1,0:T(8,128)(2,1)S(1)}) custom-call(bf16[128,384]{1,0:T(8,128)(2,1)S(1)} %bitcast.30, bf16[384,3072]{1,0:T(8,128)(2,1)S(1)} %copy-done.1, f32[2,384]{1,0:T(2,128)S(1)} %get-tuple-element.104.refs_0_.refs_2_, f32[4,384]{1,0:T(4,128)S(1)} %get-tuple-element.105.refs_1_.refs_3_, ...), custom_call_target="tpu_custom_call" | custom-call | bytes 23985000 | tf_op jit(solution)/shard_map/backward/pallas_call | solution.py:541
  167.9 3.2 %collective-permute-start.19 = (bf16[1680,384]{1,0:T(8,128)(2,1)S(1)}, bf16[1680,384]{1,0:T(8,128)(2,1)S(1)}, u32[]{:S(2)}, u32[]{:S(2)}) collective-permute-start(bf16[1680,384]{1,0:T(8,128)(2,1)S(1)} %get-tuple-element.161), channel_id=1, source_target_pairs={{0,16},{16,0},{1,17},{17,1},{2,18},{18,2},{3,19},{19,3},{4,20},{20... | collective-permute-start | bytes 3870728 | tf_op jit(solution)/shard_map/ppermute | solution.py:70
  171.1 2.8 %collective-permute-start.20 = (bf16[64,1024]{1,0:T(8,128)(2,1)S(1)}, bf16[64,1024]{1,0:T(8,128)(2,1)S(1)}, u32[]{:S(2)}, u32[]{:S(2)}) collective-permute-start(bf16[64,1024]{1,0:T(8,128)(2,1)S(1)} %copy-done.9), channel_id=1, source_target_pairs={{0,64},{32,96},{64,0},{96,32},{1,65},{33,97},{65,1},{97,33},{2,66}... | collective-permute-start | bytes 393224 | tf_op jit(solution)/shard_map/ppermute | solution.py:472
  173.9 0.4 collective-permute-start.21
  174.2 3.4 %collective-permute-done.20.refs_2_ = bf16[64,1024]{1,0:T(8,128)(2,1)S(1)} collective-permute-done((bf16[64,1024]{1,0:T(8,128)(2,1)S(1)}, bf16[64,1024]{1,0:T(8,128)(2,1)S(1)}, u32[]{:S(2)}, u32[]{:S(2)}) %collective-permute-start.20) | collective-permute-done | bytes 131104 | tf_op jit(solution)/shard_map/ppermute | solution.py:472
  177.7 5.2 %collective-permute-done.21.refs_3_ = bf16[64,1024]{1,0:T(8,128)(2,1)S(1)} collective-permute-done((bf16[64,1024]{1,0:T(8,128)(2,1)S(1)}, bf16[64,1024]{1,0:T(8,128)(2,1)S(1)}, u32[]{:S(2)}, u32[]{:S(2)}) %collective-permute-start.21) | collective-permute-done | bytes 131104 | tf_op jit(solution)/shard_map/ppermute | solution.py:472
  182.9 1.6 join.1
  184.5 3.6 %all-to-all-start.3 = ((bf16[8,240,384]{2,1,0:T(8,128)(2,1)}), bf16[8,240,384]{2,1,0:T(8,128)(2,1)S(1)}, u32[]{:S(2)}, u32[]{:S(2)}) async-start(bf16[8,240,384]{2,1,0:T(8,128)(2,1)} %bitcast.31), calls=%async_computation.3 | async-start | bytes 2949120 | tf_op jit(solution)/shard_map/all_to_all | solution.py:646
  188.1 1.7 halved.5
  189.8 1.4 collective-permute-start.23
  191.2 5.9 %collective-permute-done.22.refs_1_ = bf16[32,1024]{1,0:T(8,128)(2,1)S(1)} collective-permute-done((bf16[32,1024]{1,0:T(8,128)(2,1)}, bf16[32,1024]{1,0:T(8,128)(2,1)S(1)}, u32[]{:S(2)}, u32[]{:S(2)}) %collective-permute-start.22) | collective-permute-done | bytes 65568 | tf_op jit(solution)/shard_map/ppermute | solution.py:472
  197.1 0.8 copy-done.5
  197.9 1.7 img_rows.1
  199.6 8.7 %collective-permute-done.23.refs_1_ = bf16[32,1024]{1,0:T(8,128)(2,1)S(1)} collective-permute-done((bf16[32,1024]{1,0:T(8,128)(2,1)}, bf16[32,1024]{1,0:T(8,128)(2,1)S(1)}, u32[]{:S(2)}, u32[]{:S(2)}) %collective-permute-start.23) | collective-permute-done | bytes 65568 | tf_op jit(solution)/shard_map/ppermute | solution.py:472
  208.3 0.8 copy-done.4
  209.2 1.7 txt_rows.1
  210.9 1.3 last.1
  (27 shorter events, 0.1 us)
Async XLA Ops:
  6.2 62.4 %copy-start = (bf16[3072,384]{1,0:T(8,128)(2,1)S(1)}, bf16[3072,384]{1,0:T(8,128)(2,1)}, u32[]{:S(2)}) copy-start(bf16[3072,384]{1,0:T(8,128)(2,1)} %refs_2_.5) | copy-start | bytes 7077892
  6.2 13.4 %collective-permute-start = (bf16[232,1024]{1,0:T(8,128)(2,1)S(1)}, bf16[232,1024]{1,0:T(8,128)(2,1)S(1)}, u32[]{:S(2)}, u32[]{:S(2)}) collective-permute-start(bf16[232,1024]{1,0:T(8,128)(2,1)S(1)} %get-tuple-element.89.refs_0_), channel_id=1, source_target_pairs={{0,1},{1,0},{2,3},{3,2},{4,5},{5,4},{6,7},{7,6},{8,9},{9,8},{10,11... | collective-permute-start | bytes 1425416 | tf_op jit(solution)/shard_map/ppermute | solution.py:70
  10.0 23.8 %collective-permute-start.1 = (bf16[232,1024]{1,0:T(8,128)(2,1)S(1)}, bf16[232,1024]{1,0:T(8,128)(2,1)}, u32[]{:S(2)}, u32[]{:S(2)}) collective-permute-start(bf16[232,1024]{1,0:T(8,128)(2,1)S(1)} %get-tuple-element.89.refs_0_), channel_id=1, source_target_pairs={{0,2},{2,4},{4,6},{6,8},{8,10},{10,12},{12,14},{14,0},{1,3},{3,5},... | collective-permute-start | bytes 1425416 | tf_op jit(solution)/shard_map/ppermute | solution.py:70
  19.6 15.0 %collective-permute-start.4 = (bf16[232,1024]{1,0:T(8,128)(2,1)S(1)}, bf16[232,1024]{1,0:T(8,128)(2,1)}, u32[]{:S(2)}, u32[]{:S(2)}) collective-permute-start(bf16[232,1024]{1,0:T(8,128)(2,1)S(1)} %collective-permute-done.refs_1_), channel_id=1, source_target_pairs={{0,14},{2,0},{4,2},{6,4},{8,6},{10,8},{12,10},{14,12},{1,15},{3,1}... | collective-permute-start | bytes 1425416 | tf_op jit(solution)/shard_map/ppermute | solution.py:70
  25.9 42.7 %all-to-all-start = ((bf16[16,40,1024]{2,1,0:T(8,128)(2,1)}), bf16[16,40,1024]{2,1,0:T(8,128)(2,1)}, u32[]{:S(2)}, u32[]{:S(2)}) async-start(bf16[16,40,1024]{2,1,0:T(8,128)(2,1)} %bitcast.32), calls=%async_computation | async-start | bytes 2621440 | tf_op jit(solution)/shard_map/all_to_all | solution.py:646
  33.1 12.4 %collective-permute-start.3 = (bf16[232,1024]{1,0:T(8,128)(2,1)S(1)}, bf16[232,1024]{1,0:T(8,128)(2,1)S(1)}, u32[]{:S(2)}, u32[]{:S(2)}) collective-permute-start(bf16[232,1024]{1,0:T(8,128)(2,1)S(1)} %get-tuple-element.89.refs_0_), channel_id=1, source_target_pairs={{0,14},{2,0},{4,2},{6,4},{8,6},{10,8},{12,10},{14,12},{1,15},{3,1}... | collective-permute-start | bytes 1425416 | tf_op jit(solution)/shard_map/ppermute | solution.py:70
  33.8 15.1 %collective-permute-start.5 = (bf16[232,1024]{1,0:T(8,128)(2,1)}, bf16[232,1024]{1,0:T(8,128)(2,1)}, u32[]{:S(2)}, u32[]{:S(2)}) collective-permute-start(bf16[232,1024]{1,0:T(8,128)(2,1)} %collective-permute-done.1.refs_0_.refs_2_), channel_id=1, source_target_pairs={{0,2},{2,4},{4,6},{6,8},{8,10},{10,12},{12,14},{14,0},{1,3},{3,5},... | collective-permute-start | bytes 1425416 | tf_op jit(solution)/shard_map/ppermute | solution.py:70
  34.6 22.9 %collective-permute-start.2 = (bf16[232,1024]{1,0:T(8,128)(2,1)S(1)}, bf16[232,1024]{1,0:T(8,128)(2,1)}, u32[]{:S(2)}, u32[]{:S(2)}) collective-permute-start(bf16[232,1024]{1,0:T(8,128)(2,1)S(1)} %collective-permute-done.refs_1_), channel_id=1, source_target_pairs={{0,2},{2,4},{4,6},{6,8},{8,10},{10,12},{12,14},{14,0},{1,3},{3,5},... | collective-permute-start | bytes 1425416 | tf_op jit(solution)/shard_map/ppermute | solution.py:70
  34.6 22.9 %collective-permute-start.8 = (bf16[232,1024]{1,0:T(8,128)(2,1)}, bf16[232,1024]{1,0:T(8,128)(2,1)}, u32[]{:S(2)}, u32[]{:S(2)}) collective-permute-start(bf16[232,1024]{1,0:T(8,128)(2,1)} %collective-permute-done.4.refs_3_.refs_5_), channel_id=1, source_target_pairs={{0,14},{2,0},{4,2},{6,4},{8,6},{10,8},{12,10},{14,12},{1,15},{3,1}... | collective-permute-start | bytes 1425416 | tf_op jit(solution)/shard_map/ppermute | solution.py:70
  45.5 20.4 %collective-permute-start.7 = (bf16[232,1024]{1,0:T(8,128)(2,1)S(1)}, bf16[232,1024]{1,0:T(8,128)(2,1)}, u32[]{:S(2)}, u32[]{:S(2)}) collective-permute-start(bf16[232,1024]{1,0:T(8,128)(2,1)S(1)} %collective-permute-done.3.refs_2_.refs_4_), channel_id=1, source_target_pairs={{0,14},{2,0},{4,2},{6,4},{8,6},{10,8},{12,10},{14,12},{1,15},{3,1}... | collective-permute-start | bytes 1425416 | tf_op jit(solution)/shard_map/ppermute | solution.py:70
  48.2 0.8 copy-start.2
  49.0 28.2 %collective-permute-start.9 = (bf16[232,1024]{1,0:T(8,128)(2,1)}, bf16[232,1024]{1,0:T(8,128)(2,1)}, u32[]{:S(2)}, u32[]{:S(2)}) collective-permute-start(bf16[232,1024]{1,0:T(8,128)(2,1)} %collective-permute-done.5.refs_0_.refs_6_), channel_id=1, source_target_pairs={{0,2},{2,4},{4,6},{6,8},{8,10},{10,12},{12,14},{14,0},{1,3},{3,5},... | collective-permute-start | bytes 1425416 | tf_op jit(solution)/shard_map/ppermute | solution.py:70
  57.5 20.4 %collective-permute-start.6 = (bf16[232,1024]{1,0:T(8,128)(2,1)}, bf16[232,1024]{1,0:T(8,128)(2,1)}, u32[]{:S(2)}, u32[]{:S(2)}) collective-permute-start(bf16[232,1024]{1,0:T(8,128)(2,1)} %collective-permute-done.2.refs_1_.refs_3_), channel_id=1, source_target_pairs={{0,2},{2,4},{4,6},{6,8},{8,10},{10,12},{12,14},{14,0},{1,3},{3,5},... | collective-permute-start | bytes 1425416 | tf_op jit(solution)/shard_map/ppermute | solution.py:70
  57.5 20.4 %collective-permute-start.12 = (bf16[232,1024]{1,0:T(8,128)(2,1)}, bf16[232,1024]{1,0:T(8,128)(2,1)}, u32[]{:S(2)}, u32[]{:S(2)}) collective-permute-start(bf16[232,1024]{1,0:T(8,128)(2,1)} %collective-permute-done.8.refs_3_.refs_9_), channel_id=1, source_target_pairs={{0,14},{2,0},{4,2},{6,4},{8,6},{10,8},{12,10},{14,12},{1,15},{3,1}... | collective-permute-start | bytes 1425416 | tf_op jit(solution)/shard_map/ppermute | solution.py:70
  65.8 20.4 %collective-permute-start.11 = (bf16[232,1024]{1,0:T(8,128)(2,1)}, bf16[232,1024]{1,0:T(8,128)(2,1)}, u32[]{:S(2)}, u32[]{:S(2)}) collective-permute-start(bf16[232,1024]{1,0:T(8,128)(2,1)} %collective-permute-done.7.refs_2_.refs_8_), channel_id=1, source_target_pairs={{0,14},{2,0},{4,2},{6,4},{8,6},{10,8},{12,10},{14,12},{1,15},{3,1}... | collective-permute-start | bytes 1425416 | tf_op jit(solution)/shard_map/ppermute | solution.py:70
  68.6 3.6 %copy-start.3 = (bf16[232,1024]{1,0:T(8,128)(2,1)S(1)}, bf16[232,1024]{1,0:T(8,128)(2,1)}, u32[]{:S(2)}) copy-start(bf16[232,1024]{1,0:T(8,128)(2,1)} %copy-done.2) | copy-start | bytes 1425412
  77.2 24.2 %collective-permute-start.13 = (bf16[232,1024]{1,0:T(8,128)(2,1)}, bf16[232,1024]{1,0:T(8,128)(2,1)S(1)}, u32[]{:S(2)}, u32[]{:S(2)}) collective-permute-start(bf16[232,1024]{1,0:T(8,128)(2,1)} %collective-permute-done.9.refs_0_.refs_10_), channel_id=1, source_target_pairs={{0,2},{2,4},{4,6},{6,8},{8,10},{10,12},{12,14},{14,0},{1,3},{3,5},... | collective-permute-start | bytes 1425416 | tf_op jit(solution)/shard_map/ppermute | solution.py:70
  77.8 18.6 %collective-permute-start.10 = (bf16[232,1024]{1,0:T(8,128)(2,1)}, bf16[232,1024]{1,0:T(8,128)(2,1)S(1)}, u32[]{:S(2)}, u32[]{:S(2)}) collective-permute-start(bf16[232,1024]{1,0:T(8,128)(2,1)} %collective-permute-done.6.refs_1_.refs_7_), channel_id=1, source_target_pairs={{0,2},{2,4},{4,6},{6,8},{8,10},{10,12},{12,14},{14,0},{1,3},{3,5},... | collective-permute-start | bytes 1425416 | tf_op jit(solution)/shard_map/ppermute | solution.py:70
  77.8 23.6 %collective-permute-start.14 = (bf16[232,1024]{1,0:T(8,128)(2,1)}, bf16[232,1024]{1,0:T(8,128)(2,1)S(1)}, u32[]{:S(2)}, u32[]{:S(2)}) collective-permute-start(bf16[232,1024]{1,0:T(8,128)(2,1)} %collective-permute-done.12.refs_3_.refs_13_), channel_id=1, source_target_pairs={{0,14},{2,0},{4,2},{6,4},{8,6},{10,8},{12,10},{14,12},{1,15},{3,1}... | collective-permute-start | bytes 1425416 | tf_op jit(solution)/shard_map/ppermute | solution.py:70
  101.4 3.8 %copy-start.1 = (bf16[384,3072]{1,0:T(8,128)(2,1)S(1)}, bf16[384,3072]{1,0:T(8,128)(2,1)}, u32[]{:S(2)}) copy-start(bf16[384,3072]{1,0:T(8,128)(2,1)} %refs_1_.1) | copy-start | bytes 7077892
  106.4 12.9 %copy-start.6 = (bf16[128,512]{1,0:T(8,128)(2,1)S(1)}, bf16[128,512]{1,0:T(8,128)(2,1)}, u32[]{:S(2)}) copy-start(bf16[128,512]{1,0:T(8,128)(2,1)} %mean_rows.1) | copy-start | bytes 393220
  110.6 21.9 %collective-permute-start.15 = (bf16[256,1024]{1,0:T(8,128)(2,1)}, bf16[256,1024]{1,0:T(8,128)(2,1)S(1)}, u32[]{:S(2)}, u32[]{:S(2)}) collective-permute-start(bf16[256,1024]{1,0:T(8,128)(2,1)} %get-tuple-element.132), channel_id=1, source_target_pairs={{0,16},{16,0},{1,17},{17,1},{2,18},{18,2},{3,19},{19,3},{4,20},{20... | collective-permute-start | bytes 1572872 | tf_op jit(solution)/shard_map/ppermute | solution.py:70
  116.4 22.7 %collective-permute-start.16 = (bf16[256,1024]{1,0:T(8,128)(2,1)}, bf16[256,1024]{1,0:T(8,128)(2,1)S(1)}, u32[]{:S(2)}, u32[]{:S(2)}) collective-permute-start(bf16[256,1024]{1,0:T(8,128)(2,1)} %get-tuple-element.136), channel_id=1, source_target_pairs={{0,1},{1,0},{2,3},{3,2},{4,5},{5,4},{6,7},{7,6},{8,9},{9,8},{10,11... | collective-permute-start | bytes 1572872 | tf_op jit(solution)/shard_map/ppermute | solution.py:70
  139.0 4.1 %copy-start.7 = (bf16[128,384]{1,0:T(8,128)(2,1)S(1)}, bf16[128,384]{1,0:T(8,128)(2,1)}, u32[]{:S(2)}) copy-start(bf16[128,384]{1,0:T(8,128)(2,1)} %head.1) | copy-start | bytes 294916
  141.7 16.6 %collective-permute-start.17 = (bf16[128,1024]{1,0:T(8,128)(2,1)}, bf16[128,1024]{1,0:T(8,128)(2,1)S(1)}, u32[]{:S(2)}, u32[]{:S(2)}) collective-permute-start(bf16[128,1024]{1,0:T(8,128)(2,1)} %get-tuple-element.141), channel_id=1, source_target_pairs={{0,128},{128,0},{1,129},{129,1},{2,130},{130,2},{3,131},{131,3},{4... | collective-permute-start | bytes 786440 | tf_op jit(solution)/shard_map/ppermute | solution.py:472
  143.1 15.2 %collective-permute-start.18 = (bf16[128,1024]{1,0:T(8,128)(2,1)}, bf16[128,1024]{1,0:T(8,128)(2,1)S(1)}, u32[]{:S(2)}, u32[]{:S(2)}) collective-permute-start(bf16[128,1024]{1,0:T(8,128)(2,1)} %get-tuple-element.142), channel_id=1, source_target_pairs={{0,2},{2,0},{4,6},{6,4},{8,10},{10,8},{12,14},{14,12},{1,3},{3,1},... | collective-permute-start | bytes 786440 | tf_op jit(solution)/shard_map/ppermute | solution.py:472
  160.3 10.8 %copy-start.9 = (bf16[64,1024]{1,0:T(8,128)(2,1)S(1)}, bf16[64,1024]{1,0:T(8,128)(2,1)}, u32[]{:S(2)}) copy-start(bf16[64,1024]{1,0:T(8,128)(2,1)} %get-tuple-element.162) | copy-start | bytes 393220
  160.3 13.5 %copy-start.8 = (bf16[64,1024]{1,0:T(8,128)(2,1)S(1)}, bf16[64,1024]{1,0:T(8,128)(2,1)}, u32[]{:S(2)}) copy-start(bf16[64,1024]{1,0:T(8,128)(2,1)} %get-tuple-element.163) | copy-start | bytes 393220
  167.9 15.0 %collective-permute-start.19 = (bf16[1680,384]{1,0:T(8,128)(2,1)S(1)}, bf16[1680,384]{1,0:T(8,128)(2,1)S(1)}, u32[]{:S(2)}, u32[]{:S(2)}) collective-permute-start(bf16[1680,384]{1,0:T(8,128)(2,1)S(1)} %get-tuple-element.161), channel_id=1, source_target_pairs={{0,16},{16,0},{1,17},{17,1},{2,18},{18,2},{3,19},{19,3},{4,20},{20... | collective-permute-start | bytes 3870728 | tf_op jit(solution)/shard_map/ppermute | solution.py:70
  171.1 6.6 %collective-permute-start.20 = (bf16[64,1024]{1,0:T(8,128)(2,1)S(1)}, bf16[64,1024]{1,0:T(8,128)(2,1)S(1)}, u32[]{:S(2)}, u32[]{:S(2)}) collective-permute-start(bf16[64,1024]{1,0:T(8,128)(2,1)S(1)} %copy-done.9), channel_id=1, source_target_pairs={{0,64},{32,96},{64,0},{96,32},{1,65},{33,97},{65,1},{97,33},{2,66}... | collective-permute-start | bytes 393224 | tf_op jit(solution)/shard_map/ppermute | solution.py:472
  173.9 9.0 %collective-permute-start.21 = (bf16[64,1024]{1,0:T(8,128)(2,1)S(1)}, bf16[64,1024]{1,0:T(8,128)(2,1)S(1)}, u32[]{:S(2)}, u32[]{:S(2)}) collective-permute-start(bf16[64,1024]{1,0:T(8,128)(2,1)S(1)} %copy-done.8), channel_id=1, source_target_pairs={{0,4},{2,6},{4,0},{6,2},{8,12},{10,14},{12,8},{14,10},{1,5},{3,7},... | collective-permute-start | bytes 393224 | tf_op jit(solution)/shard_map/ppermute | solution.py:472
  184.5 26.4 %all-to-all-start.3 = ((bf16[8,240,384]{2,1,0:T(8,128)(2,1)}), bf16[8,240,384]{2,1,0:T(8,128)(2,1)S(1)}, u32[]{:S(2)}, u32[]{:S(2)}) async-start(bf16[8,240,384]{2,1,0:T(8,128)(2,1)} %bitcast.31), calls=%async_computation.3 | async-start | bytes 2949120 | tf_op jit(solution)/shard_map/all_to_all | solution.py:646
  189.8 7.2 %collective-permute-start.22 = (bf16[32,1024]{1,0:T(8,128)(2,1)}, bf16[32,1024]{1,0:T(8,128)(2,1)S(1)}, u32[]{:S(2)}, u32[]{:S(2)}) collective-permute-start(bf16[32,1024]{1,0:T(8,128)(2,1)} %get-tuple-element.167), channel_id=1, source_target_pairs={{0,8},{2,10},{4,12},{6,14},{8,0},{10,2},{12,4},{14,6},{1,9},{3,11}... | collective-permute-start | bytes 196616 | tf_op jit(solution)/shard_map/ppermute | solution.py:472
  189.8 18.5 %collective-permute-start.23 = (bf16[32,1024]{1,0:T(8,128)(2,1)}, bf16[32,1024]{1,0:T(8,128)(2,1)S(1)}, u32[]{:S(2)}, u32[]{:S(2)}) collective-permute-start(bf16[32,1024]{1,0:T(8,128)(2,1)} %get-tuple-element.169), channel_id=1, source_target_pairs={{0,32},{32,0},{64,96},{96,64},{1,33},{33,1},{65,97},{97,65},{2,34}... | collective-permute-start | bytes 196616 | tf_op jit(solution)/shard_map/ppermute | solution.py:472
  197.0 0.8 copy-start.5
  208.3 0.8 copy-start.4

commit v2 on v1

--- a/solution.py
+++ b/solution.py
@@ -81,22 +81,18 @@
     return (values / length, length)
 
 
-def front_kernel(
-    img, txt, img_ids, txt_ids, block_in, taps, gain, bias, blk, txt_all, means, mixed, ids, txt_pay, sems
-):
-    def id_rows(source):
-        ids[...] = jnp.zeros_like(ids)
-        ids[0:1, 0:PAIRS] = source[...]
-        row = lax.broadcasted_iota(jnp.int32, (8, EMBED), 0)
-        value = jnp.broadcast_to(ids[0:1, :], (8, EMBED))
-        return jnp.where(row == 0, value >> 7, jnp.where(row == 1, value & 127, 0)).astype(F32)
-
-    blk[IMG_AT : IMG_AT + PAIRS, :] = unit_rows(img[...].astype(F32))[0].astype(BF)
-    blk[IMG_AT + PAIRS : ROWS, :] = id_rows(img_ids).astype(BF)
+def id_rows(source, ids):
+    ids[...] = jnp.zeros_like(ids)
+    ids[0:1, 0:PAIRS] = source[...]
+    row = lax.broadcasted_iota(jnp.int32, (8, EMBED), 0)
+    value = jnp.broadcast_to(ids[0:1, :], (8, EMBED))
+    return jnp.where(row == 0, value >> 7, jnp.where(row == 1, value & 127, 0)).astype(F32)
+
+
+def text_rows_kernel(txt, txt_ids, txt_all, ids, txt_pay, sems):
     txt_pay[0:PAIRS, :] = unit_rows(txt[...].astype(F32))[0].astype(BF)
     place = (lax.axis_index("ylo") * 4 + lax.axis_index("x")) * 2 + lax.axis_index("core")
-    txt_pay[PAIRS:TXT_ROWS, :] = pltpu.roll(id_rows(txt_ids), place * PAIRS, 1).astype(BF)
-
+    txt_pay[PAIRS:TXT_ROWS, :] = pltpu.roll(id_rows(txt_ids, ids), place * PAIRS, 1).astype(BF)
     copies = [
         pltpu.make_async_copy(
             txt_pay, txt_all.at[d * TXT_ROWS : (d + 1) * TXT_ROWS, :], sems.at[d]
@@ -105,7 +101,29 @@
     ]
     for copy in copies:
         copy.start()
-
+    for copy in copies:
+        copy.wait()
+
+
+def text_rows(*args):
+    return pl.pallas_call(
+        text_rows_kernel,
+        out_shape=far(16 * TXT_ROWS, EMBED, BF),
+        out_specs=loose(1)[0],
+        scratch_shapes=[
+            pltpu.VMEM((8, EMBED), jnp.int32),
+            pltpu.VMEM((TXT_ROWS, EMBED), BF),
+            pltpu.SemaphoreType.DMA((16,)),
+        ],
+        compiler_params=params(4),
+        cost_estimate=cost(1.0),
+        name="text_rows",
+    )(*from_far(*args))
+
+
+def front_kernel(img, img_ids, block_in, taps, gain, bias, blk, means, mixed, ids):
+    blk[IMG_AT : IMG_AT + PAIRS, :] = unit_rows(img[...].astype(F32))[0].astype(BF)
+    blk[IMG_AT + PAIRS : ROWS, :] = id_rows(img_ids, ids).astype(BF)
     column = lax.broadcasted_iota(jnp.int32, (SIDE, 128), 0)
 
     def lanes(c, sums):
@@ -155,24 +173,15 @@
         blk[seg * PATCHES : (seg + 1) * PATCHES, lane : lane + 128] = (
             normal * gain[:, at] + bias[:, at]
         ).astype(BF)
-    for copy in copies:
-        copy.wait()
 
 
 def front(*args):
     return pl.pallas_call(
         front_kernel,
-        out_shape=(
-            near(ROWS, EMBED, BF),
-            far(16 * TXT_ROWS, EMBED, BF),
-            far(1, WIDTH, F32),
-        ),
-        out_specs=(pl.BlockSpec(), *loose(1), pl.BlockSpec()),
+        out_shape=(near(ROWS, EMBED, BF), far(1, WIDTH, F32)),
         scratch_shapes=[
             pltpu.VMEM((PATCHES, WIDTH), F32),
             pltpu.VMEM((8, EMBED), jnp.int32),
-            pltpu.VMEM((TXT_ROWS, EMBED), BF),
-            pltpu.SemaphoreType.DMA((16,)),
         ],
         compiler_params=params(8),
         cost_estimate=cost(4.5),
@@ -283,8 +292,10 @@
 def mean_kernel(*refs):
     count = UNITS
     sums, firsts = refs[:count], refs[count : 2 * count]
-    w_down, out, held = refs[2 * count :]
-    mean = jnp.concatenate([s[...] for s in sums], axis=0) / PATCHES
+    w_down, out, total_out, held = refs[2 * count :]
+    total = jnp.concatenate([s[...] for s in sums], axis=0)
+    total_out[...] = total.astype(BF)
+    mean = total / PATCHES
     first = mean.astype(BF)
     rest = mean - first.astype(F32)
     second = rest.astype(BF)
@@ -306,7 +317,7 @@
 def mean_rows(sums, firsts, w_down):
     return pl.pallas_call(
         mean_kernel,
-        out_shape=far(128, 512, BF),
+        out_shape=(far(128, 512, BF), far(16, HID, BF)),
         in_specs=whole(2 * len(GROUPS) + 1),
         scratch_shapes=[pltpu.VMEM((16, 8, 512), F32)],
         compiler_params=params(6),
@@ -395,21 +406,14 @@
     text_part = lax.dot_general(
         weight[...], rows[...], (((0,), (0,)), ((), ())), preferred_element_type=F32
     ).astype(BF)
-    core = lax.axis_index("core")
+    rows[...] = text_part
+    high = lax.axis_index("x") >> 1
     for k in range(8):
+        low, ylo, core = k >> 2, (k >> 1) & 1, k & 1
         at = slice(k * PAIRS, (k + 1) * PAIRS)
-        even = text_part[2 * k * PAIRS : (2 * k + 1) * PAIRS]
-        odd = text_part[(2 * k + 1) * PAIRS : (2 * k + 2) * PAIRS]
-
-        @pl.when(core == 0)
-        def _():
-            txt_keep[at, :] = even
-            txt_send[at, :] = odd
-
-        @pl.when(core == 1)
-        def _():
-            txt_keep[at, :] = odd
-            txt_send[at, :] = even
+        for into, side in ((txt_keep, high), (txt_send, 1 - high)):
+            first = (ylo * 8 + low * 2 + core + 4 * side) * PAIRS
+            into[at, :] = rows[pl.ds(pl.multiple_of(first, PAIRS), PAIRS), :]
 
     z = lax.axis_index("z")
     for j, (offset, side) in enumerate(KEYS):
@@ -435,7 +439,7 @@
         compiler_params=params(14),
         cost_estimate=cost(3.8),
         name="text_parts",
-    )(*blocks, *from_far(*weights, *images))
+    )(*from_far(*blocks, *weights, *images))
 
 
 def halve_kernel(bits, *refs):
@@ -443,17 +447,9 @@
     for (axis, shift), first, second, send, keep in zip(bits, keeps, gots, sends, outs):
         mine = (lax.axis_index(axis) >> shift) & 1
         rows = send.shape[0]
-        for part in range(2):
-            at = slice(part * rows, (part + 1) * rows)
-            total = (first[at, :].astype(F32) + second[at, :].astype(F32)).astype(BF)
-
-            @pl.when(mine == part)
-            def _():
-                keep[...] = total
-
-            @pl.when(mine != part)
-            def _():
-                send[...] = total
+        for into, part in ((keep, mine), (send, 1 - mine)):
+            at = pl.ds(pl.multiple_of(part * rows, rows), rows)
+            into[...] = (first[at, :].astype(F32) + second[at, :].astype(F32)).astype(BF)
 
 
 def halved(bits, keeps, gots):
@@ -473,9 +469,9 @@
 
 
 def back_kernel(*refs):
-    grads, w_down = refs[:2]
-    sums, slopes, turns = (refs[2 + i * UNITS : 2 + (i + 1) * UNITS] for i in range(3))
-    send, keep, held, hid_grad, slope, rows, sems = refs[2 + 3 * UNITS :]
+    grads, w_down, total = refs[:3]
+    slopes, turns = refs[3 : 3 + UNITS], refs[3 + UNITS : 3 + 2 * UNITS]
+    send, keep, held, wide, hid_grad, slope, rows, block, sems = refs[3 + 2 * UNITS :]
     slope_copies, low_copies, high_copies, first = [], [], [], 0
     low, high = slice(0, WIDTH // 2), slice(WIDTH // 2, WIDTH)
     for u, group in enumerate(GROUPS):
@@ -490,70 +486,60 @@
             )
     for copy in (*slope_copies, *low_copies, *high_copies):
         copy.start()
-    total = jnp.concatenate([s[...] for s in sums], axis=0).astype(BF)
-    keep[8 * HALF :, :] = total
-    send[8 * HALF :, :] = total
+    keep[8 * HALF :, :] = total[...]
+    send[8 * HALF :, :] = total[...]
     for j, key in enumerate(KEYS):
         at = pl.ds(pl.multiple_of(absolute(key) * 8, 8), 8)
         held[j] = grads[at, :].astype(F32)
-    group = jnp.concatenate([held[:, c, :] for c in range(8)], axis=1)
+    for c in range(8):
+        wide[:, c * HID : (c + 1) * HID] = held[:, c, :]
     row_down = lax.dot_general(
-        group.astype(BF), w_down[...], (((1,), (1,)), ((), ())), preferred_element_type=F32
+        wide[...].astype(BF), w_down[...], (((1,), (1,)), ((), ())), preferred_element_type=F32
     )
     for copy in slope_copies:
         copy.wait()
     for j in range(16):
         at = slice(j * PATCHES, (j + 1) * PATCHES)
         hid_grad[at, :] = (slope[at, :] * row_down[j : j + 1]).astype(BF)
-    for copy in low_copies:
-        copy.wait()
-    low, high = slice(0, SLAB), slice(SLAB, 2 * SLAB)
     core = lax.axis_index("core")
-    for k in range(8):
-        if k == 4:
-            for copy in high_copies:
-                copy.wait()
-        part = jnp.dot(
-            rows[k * 2 * SLAB : (k + 1) * 2 * SLAB, :], hid_grad[...], preferred_element_type=F32
-        ).astype(BF)
-        mine = group[:, k * 2 * SLAB : (k + 1) * 2 * SLAB]
-        swapped = pltpu.roll(mine, SLAB, 1).astype(BF)
-        mine = mine.astype(BF)
-        at = slice(k * HALF, k * HALF + SLAB)
-        below = slice(k * HALF + SLAB, (k + 1) * HALF)
-
-        @pl.when(core == 0)
-        def _():
-            keep[at, :] = part[low]
-            send[at, :] = part[high]
-            keep[below, :] = mine
-            send[below, :] = swapped
-
-        @pl.when(core == 1)
-        def _():
-            keep[at, :] = part[high]
-            send[at, :] = part[low]
-            keep[below, :] = swapped
-            send[below, :] = mine
-
-
-def backward(grads, w_down, sums, slopes, turns):
+
+    def slabs(k, carry):
+        at = pl.ds(pl.multiple_of(k * 2 * SLAB, 128), 2 * SLAB)
+        block[...] = jnp.dot(rows[at, :], hid_grad[...], preferred_element_type=F32).astype(BF)
+        mine = wide[:, at]
+        swapped = pltpu.roll(mine, SLAB, 1)
+        to = pl.ds(pl.multiple_of(k * HALF, 16), SLAB)
+        below = pl.ds(pl.multiple_of(k * HALF + SLAB, 16), 16)
+        for into, side in ((keep, core), (send, 1 - core)):
+            into[to, :] = block[pl.ds(pl.multiple_of(side * SLAB, SLAB), SLAB), :]
+            into[below, :] = jnp.where(side == 0, mine, swapped).astype(BF)
+        return carry
+
+    for half, copies in enumerate((low_copies, high_copies)):
+        for copy in copies:
+            copy.wait()
+        lax.fori_loop(half * 4, half * 4 + 4, slabs, 0)
+
+
+def backward(grads, w_down, total, slopes, turns):
     return pl.pallas_call(
         back_kernel,
         out_shape=(near(8 * HALF + 16, HID, BF),) * 2,
-        in_specs=whole(2 + UNITS) + loose(2 * UNITS),
+        in_specs=whole(3) + loose(2 * UNITS),
         out_specs=tuple(whole(2)),
         scratch_shapes=[
             pltpu.VMEM((16, 8, HID), F32),
+            pltpu.VMEM((16, WIDTH), F32),
             pltpu.VMEM((16 * PATCHES, HID), BF),
             pltpu.VMEM((16 * PATCHES, HID), F32),
             pltpu.VMEM((WIDTH, 16 * PATCHES), BF),
+            pltpu.VMEM((2 * SLAB, HID), BF),
             pltpu.SemaphoreType.DMA((3 * UNITS,)),
         ],
         compiler_params=params(16),
         cost_estimate=cost(6.5),
         name="backward",
-    )(grads, w_down, *sums, *from_far(*slopes, *turns))
+    )(grads, w_down, *from_far(total, *slopes, *turns))
 
 
 def join_kernel(keep, got, out):
@@ -664,11 +650,10 @@
     head_bias,
     w_proj,
 ):
-    blk, txt_all, means = front(
+    texts = swap(text_rows(txt_emb, txt_ids.reshape(1, PAIRS)), DP, 16)
+    blk, means = front(
         img_emb,
-        txt_emb,
         img_ids.reshape(1, PAIRS),
-        txt_ids.reshape(1, PAIRS),
         block_in,
         dw_kernel,
         ln_gain.reshape(1, WIDTH),
@@ -694,25 +679,27 @@
         return step([got[key] for key in GROUPS[unit]], w_up, texts, temper, offset)
 
     got[0, 1] = hop(blk, "yhi", 2, 1)
-    texts = swap(txt_all, DP, 16)
-    for distance in range(1, NZ // 2):
-        send_on(0, distance)
-        send_on(1, distance)
+    send_on(0, 1)
+    tie([(NZ - 1, 0), (1, 0)])
+    send_on(1, 1)
+    send_on(0, 2)
+    send_on(1, 2)
+    send_on(0, 3)
+    kept.append(tie([(NZ - 2, 1)], *work(0)))
+    send_on(1, 3)
     send_on(0, NZ // 2, down=False)
-    done = tie([(3, 1)], *work(0), *work(1))
+    kept.append(tie([(3, 1)], *work(1)))
     send_on(1, NZ // 2, up=False)
-    kept += [done[:6], done[6:]]
     kept += [work(unit) for unit in range(2, UNITS)]
 
     slopes, images, weights, turns, sums, firsts = zip(*kept)
-    means_out, *weights = lax.optimization_barrier((mean_rows(sums, firsts, w_down), *weights))
+    means_out, total = mean_rows(sums, firsts, w_down)
+    means_out, *weights = lax.optimization_barrier((means_out, *weights))
     parts = swap(means_out, FSDP, 16)
-    txt_send, txt_keep, img_send, img_keep = text_parts(
-        [got[key] for key in KEYS], weights, images
-    )
-    keeps = (txt_keep, img_keep)
-    gots = (hop(txt_send, "core", 2, 1), hop(img_send, "yhi", 2, 1))
-    parts, txt_got = lax.optimization_barrier((parts, gots[0]))
+    sends = text_parts([got[key] for key in KEYS], weights, images)
+    parts, txt_send, txt_keep, img_send, img_keep = lax.optimization_barrier((parts, *sends))
+    txt_got = partner(txt_send, "x", 4, 2)
+    img_got = hop(img_send, "yhi", 2, 1)
     grads = head(
         parts,
         means,
@@ -721,21 +708,21 @@
         head_bias.reshape(1, WIDTH),
         w_proj,
     )
-    grads, img_got = lax.optimization_barrier((grads, gots[1]))
     grads = swap(grads, FSDP, 16)
-    sends, keeps = halved((("ylo", 0), ("z", 0)), keeps, (txt_got, img_got))
-    gots = (partner(sends[0], "ylo", 2, 1), partner(sends[1], "z", NZ, 1))
-    grads, *gots = lax.optimization_barrier((grads, *gots))
-    send, keep = backward(grads, w_down, sums, slopes, turns)
-    sends, keeps = halved((("x", 1), ("z", 1)), keeps, gots)
-    send, *sends = lax.optimization_barrier((send, *sends))
-    gots = (partner(sends[0], "x", 4, 2), partner(sends[1], "z", NZ, 2))
-    got_core, *gots = lax.optimization_barrier((hop(send, "core", 2, 1), *gots))
+    sends, keeps = halved((("x", 0), ("z", 0)), (txt_keep, img_keep), (txt_got, img_got))
+    grads, *sends = lax.optimization_barrier((grads, *sends))
+    gots = (partner(sends[0], "x", 4, 1), partner(sends[1], "z", NZ, 1))
+    send, keep = backward(grads, w_down, total, slopes, turns)
+    send, *gots = lax.optimization_barrier((send, *gots))
+    got_core = hop(send, "core", 2, 1)
+    sends, keeps = halved((("ylo", 0), ("z", 1)), keeps, gots)
+    gots = (partner(sends[0], "ylo", 2, 1), partner(sends[1], "z", NZ, 2))
     both = join(keep, got_core)
-    sends, keeps = halved((("x", 0), ("z", 2)), keeps, gots)
+    both, *gots = lax.optimization_barrier((both, *gots))
+    sends, keeps = halved((("core", 0), ("z", 2)), keeps, gots)
     w_up_grad, w_down_grad = last(swap(both, ("ylo", "x"), 8))
     w_down_grad = w_down_grad.T
-    txt_grad = row_grads((keeps[0], partner(sends[0], "x", 4, 1)), txt_emb, "txt_rows")
+    txt_grad = row_grads((keeps[0], partner(sends[0], "core", 2, 1)), txt_emb, "txt_rows")
     img_grad = row_grads((keeps[1], partner(sends[1], "z", NZ, 4)), img_emb, "img_rows")
     return (img_grad, txt_grad, w_up_grad, w_down_grad)
 

time: 213 us -> 195 us (0.915)
  blocking collectives: 28.3 us -> 0 us
  waiting for transfers between devices: 62.8 us -> 67.6 us
  starting transfers between devices: 56.3 us -> 60 us
  Pallas kernels: 60.1 us -> 62.3 us
    all_to_all x2 -> x0, blocking collectives: 28.3 us -> none  [swap(): return lax.all_to_all(parts, axes, 0, 0, tiled=True).reshape(rows, columns)]
    all_to_all x2 -> x4, waiting for transfers between devices: 0.01 us -> 18.4 us  [swap(): return lax.all_to_all(parts, axes, 0, 0, tiled=True).reshape(rows, columns)]
    ppermute x6 -> x7, waiting for transfers between devices: 23.3 us -> 11.8 us  [partner(): return lax.ppermute(value, axis, [(i, i ^ bit) for i in range(length)])]
    all_to_all x2 -> x4, starting transfers between devices: 10.7 us -> 20.7 us  [swap(): return lax.all_to_all(parts, axes, 0, 0, tiled=True).reshape(rows, columns)]
    ppermute x18 -> x17, starting transfers between devices: 39.7 us -> 32.4 us  [hop(): lax.ppermute(value, axis, [(i, (i + step) % length) for i in range(length)])]
    ppermute x18 -> x17, waiting for transfers between devices: 39.5 us -> 37.4 us  [hop(): lax.ppermute(value, axis, [(i, (i + step) % length) for i in range(length)])]
    pallas_call x2 -> x3, Pallas kernels: 6.72 us -> 8.26 us  [the longest x1 4.89 us: front(): pl.pallas_call(front_kernel, out_shape=(near(ROWS, EMBED, BF), far(1, WID...]
    ppermute x6 -> x7, starting transfers between devices: 5.86 us -> 6.95 us  [partner(): return lax.ppermute(value, axis, [(i, i ^ bit) for i in range(length)])]
  transfers between devices with their start and end apart: 26 -> 28, of which waited for: 11 -> 13; matrix products, arithmetic and copies ran while one was open for 0% -> 0% of each run, Pallas kernels for 14% -> 26%
where the time goes in v2:
time: 195 us; the launch traced here: 194 us
  waiting for transfers between devices  67.6 us (35%)
  Pallas kernels  62.3 us (32%)
  starting transfers between devices  60 us (31%)
  between operations  2.22 us (1%)
    ppermute x17, waiting for transfers between devices, hop(): lax.ppermute(value, axis, [(i, (i + step) % length) for i in range(length)])  37.4 us
    ppermute x17, starting transfers between devices, hop(): lax.ppermute(value, axis, [(i, (i + step) % length) for i in range(length)])  32.4 us
    pallas_call x5, Pallas kernels, step(): pl.pallas_call(functools.partial(step_kernel, count), out_shape=(*(far(*d...  22.9 us
    all_to_all x4, starting transfers between devices, swap(): return lax.all_to_all(parts, axes, 0, 0, tiled=True).reshape(rows, columns)  20.7 us
    all_to_all x4, waiting for transfers between devices, swap(): return lax.all_to_all(parts, axes, 0, 0, tiled=True).reshape(rows, columns)  18.4 us
    ppermute x7, waiting for transfers between devices, partner(): return lax.ppermute(value, axis, [(i, i ^ bit) for i in range(length)])  11.8 us
    pallas_call x1, Pallas kernels, backward(): pl.pallas_call(back_kernel, out_shape=(near(8 * HALF + 16, HID, BF),) * 2...  8.23 us
    ppermute x7, starting transfers between devices, partner(): return lax.ppermute(value, axis, [(i, i ^ bit) for i in range(length)])  6.95 us
  transfers between devices with their start and end apart: 28, of which 13 were waited for; matrix products, arithmetic and copies ran while one was open for 0% of the time, Pallas kernels for 26%

profile of v2, /device:TPU:1, one launch (start us, length us, event | category | flops | bytes accessed | tf_op | source)
XLA Modules:
  0.0 193.8 jit_solution(6223006714009914742)
XLA Ops:
  0.6 4.9 %front.1 = (bf16[232,1024]{1,0:T(8,128)(2,1)S(1)}, f32[1,3072]{1,0:T(1,128)}) custom-call(bf16[32,1024]{1,0:T(8,128)(2,1)} %refs_2_.6, s32[1,32]{1,0:T(1,128)} %bitcast.41, bf16[64,3072]{1,0:T(8,128)(2,1)} %block_in.1, f32[49,3072]{1,0:T(8,128)} %taps.1, f32[1,3072]{1,0:T(1,128)} %bitcast.35, f32[1,3072]{1,0:T(1,128)} %bitcast.36), custom_call_target="tpu_custom_call" | custom-call | bytes 16605000 | tf_op jit(solution)/shard_map/front/pallas_call | solution.py:179
  5.5 3.7 %collective-permute-start = (bf16[232,1024]{1,0:T(8,128)(2,1)S(1)}, bf16[232,1024]{1,0:T(8,128)(2,1)S(1)}, u32[]{:S(2)}, u32[]{:S(2)}) collective-permute-start(bf16[232,1024]{1,0:T(8,128)(2,1)S(1)} %get-tuple-element.94.refs_0_), channel_id=1, source_target_pairs={{0,1},{1,0},{2,3},{3,2},{4,5},{5,4},{6,7},{7,6},{8,9},{9,8},{10,11... | collective-permute-start | bytes 1425416 | tf_op jit(solution)/shard_map/ppermute | solution.py:70
  9.3 5.6 %collective-permute-start.7 = (bf16[232,1024]{1,0:T(8,128)(2,1)S(1)}, bf16[232,1024]{1,0:T(8,128)(2,1)}, u32[]{:S(2)}, u32[]{:S(2)}) collective-permute-start(bf16[232,1024]{1,0:T(8,128)(2,1)S(1)} %get-tuple-element.94.refs_0_), channel_id=1, source_target_pairs={{0,14},{2,0},{4,2},{6,4},{8,6},{10,8},{12,10},{14,12},{1,15},{3,1}... | collective-permute-start | bytes 1425416 | tf_op jit(solution)/shard_map/ppermute | solution.py:70
  14.8 0.0 collective-permute-start.6
  14.9 4.0 %collective-permute-done.refs_1_ = bf16[232,1024]{1,0:T(8,128)(2,1)S(1)} collective-permute-done((bf16[232,1024]{1,0:T(8,128)(2,1)S(1)}, bf16[232,1024]{1,0:T(8,128)(2,1)S(1)}, u32[]{:S(2)}, u32[]{:S(2)}) %collective-permute-start) | collective-permute-done | bytes 475168 | tf_op jit(solution)/shard_map/ppermute | solution.py:70
  18.8 6.4 %collective-permute-start.3 = (bf16[232,1024]{1,0:T(8,128)(2,1)S(1)}, bf16[232,1024]{1,0:T(8,128)(2,1)}, u32[]{:S(2)}, u32[]{:S(2)}) collective-permute-start(bf16[232,1024]{1,0:T(8,128)(2,1)S(1)} %collective-permute-done.refs_1_), channel_id=1, source_target_pairs={{0,14},{2,0},{4,2},{6,4},{8,6},{10,8},{12,10},{14,12},{1,15},{3,1}... | collective-permute-start | bytes 1425416 | tf_op jit(solution)/shard_map/ppermute | solution.py:70
  25.2 2.2 %text_rows.1 = bf16[640,1024]{1,0:T(8,128)(2,1)} custom-call(bf16[32,1024]{1,0:T(8,128)(2,1)} %refs_2_.7, s32[1,32]{1,0:T(1,128)} %bitcast.40), custom_call_target="tpu_custom_call" | custom-call | bytes 3690000 | tf_op jit(solution)/shard_map/text_rows/pallas_call | solution.py:109
  27.4 0.0 copy-start
  27.4 7.3 %all-to-all-start = ((bf16[16,40,1024]{2,1,0:T(8,128)(2,1)}), bf16[16,40,1024]{2,1,0:T(8,128)(2,1)}, u32[]{:S(2)}, u32[]{:S(2)}) async-start(bf16[16,40,1024]{2,1,0:T(8,128)(2,1)} %bitcast.32), calls=%async_computation | async-start | bytes 2621440 | tf_op jit(solution)/shard_map/all_to_all | solution.py:632
  34.7 0.0 collective-permute-start.1
  34.7 0.0 collective-permute-done.7.refs_2_.refs_4_
  34.7 0.1 collective-permute-start.8
  34.8 0.0 collective-permute-done.3.refs_3_.refs_5_
  34.8 2.7 %collective-permute-start.4 = (bf16[232,1024]{1,0:T(8,128)(2,1)}, bf16[232,1024]{1,0:T(8,128)(2,1)}, u32[]{:S(2)}, u32[]{:S(2)}) collective-permute-start(bf16[232,1024]{1,0:T(8,128)(2,1)} %collective-permute-done.3.refs_3_.refs_5_), channel_id=1, source_target_pairs={{0,14},{2,0},{4,2},{6,4},{8,6},{10,8},{12,10},{14,12},{1,15},{3,1}... | collective-permute-start | bytes 1425416 | tf_op jit(solution)/shard_map/ppermute | solution.py:70
  37.5 1.3 collective-permute-start.9
  38.8 9.4 %collective-permute-done.1.refs_1_.refs_3_ = bf16[232,1024]{1,0:T(8,128)(2,1)} collective-permute-done((bf16[232,1024]{1,0:T(8,128)(2,1)S(1)}, bf16[232,1024]{1,0:T(8,128)(2,1)}, u32[]{:S(2)}, u32[]{:S(2)}) %collective-permute-start.1) | collective-permute-done | bytes 475168 | tf_op jit(solution)/shard_map/ppermute | solution.py:70
  48.2 10.2 %collective-permute-done.8.refs_0_.refs_6_ = bf16[232,1024]{1,0:T(8,128)(2,1)} collective-permute-done((bf16[232,1024]{1,0:T(8,128)(2,1)}, bf16[232,1024]{1,0:T(8,128)(2,1)}, u32[]{:S(2)}, u32[]{:S(2)}) %collective-permute-start.8) | collective-permute-done | bytes 475168 | tf_op jit(solution)/shard_map/ppermute | solution.py:70
  58.4 2.7 %collective-permute-start.5 = (bf16[232,1024]{1,0:T(8,128)(2,1)}, bf16[232,1024]{1,0:T(8,128)(2,1)}, u32[]{:S(2)}, u32[]{:S(2)}) collective-permute-start(bf16[232,1024]{1,0:T(8,128)(2,1)} %collective-permute-done.4.refs_3_.refs_9_), channel_id=1, source_target_pairs={{0,14},{2,0},{4,2},{6,4},{8,6},{10,8},{12,10},{14,12},{1,15},{3,1}... | collective-permute-start | bytes 1425416 | tf_op jit(solution)/shard_map/ppermute | solution.py:70
  62.4 0.3 collective-permute-start.12
  62.7 0.0 all-to-all-done
  62.7 3.5 %step.5 = (f32[128,384]{1,0:T(8,128)}, bf16[64,1024]{1,0:T(8,128)(2,1)}, bf16[64,512]{1,0:T(8,128)(2,1)}, bf16[3072,128]{1,0:T(8,128)(2,1)}, f32[2,384]{1,0:T(2,128)S(1)}, /*index=5*/f32[2,1024]{1,0:T(2,128)S(1)}) custom-call(bf16[232,1024]{1,0:T(8,128)(2,1)S(1)} %get-tuple-element.94.refs_0_, bf16[232,1024]{1,0:T(8,128)(2,1)S(1)} %collective-permute-done.refs_1_, ...), custom_call_target="tpu_custom_call" | custom-call | bytes 11439000 | tf_op jit(solution)/shard_map/step/pallas_call | solution.py:275
  66.3 5.1 %step.6 = (f32[256,384]{1,0:T(8,128)}, bf16[128,1024]{1,0:T(8,128)(2,1)}, bf16[128,512]{1,0:T(8,128)(2,1)}, bf16[3072,256]{1,0:T(8,128)(2,1)}, f32[4,384]{1,0:T(4,128)S(1)}, /*index=5*/f32[4,1024]{1,0:T(4,128)S(1)}) custom-call(bf16[232,1024]{1,0:T(8,128)(2,1)} %collective-permute-done.6.refs_0_.refs_2_, ...), custom_call_target="tpu_custom_call" | custom-call | bytes 17343000 | tf_op jit(solution)/shard_map/step/pallas_call | solution.py:275
  71.4 1.5 collective-permute-start.11
  72.9 5.9 %collective-permute-done.10.refs_0_.refs_10_ = bf16[232,1024]{1,0:T(8,128)(2,1)} collective-permute-done((bf16[232,1024]{1,0:T(8,128)(2,1)}, bf16[232,1024]{1,0:T(8,128)(2,1)}, u32[]{:S(2)}, u32[]{:S(2)}) %collective-permute-start.10) | collective-permute-done | bytes 475168 | tf_op jit(solution)/shard_map/ppermute | solution.py:70
  78.8 0.0 collective-permute-start.13
  78.8 0.0 collective-permute-done.5.refs_3_.refs_13_
  78.8 2.7 %collective-permute-start.14 = (bf16[232,1024]{1,0:T(8,128)(2,1)}, bf16[232,1024]{1,0:T(8,128)(2,1)S(1)}, u32[]{:S(2)}, u32[]{:S(2)}) collective-permute-start(bf16[232,1024]{1,0:T(8,128)(2,1)} %collective-permute-done.5.refs_3_.refs_13_), channel_id=1, source_target_pairs={{0,14},{2,0},{4,2},{6,4},{8,6},{10,8},{12,10},{14,12},{1,15},{3,1}... | collective-permute-start | bytes 1425416 | tf_op jit(solution)/shard_map/ppermute | solution.py:70
  81.5 5.1 %step.7 = (f32[256,384]{1,0:T(8,128)}, bf16[128,1024]{1,0:T(8,128)(2,1)}, bf16[128,512]{1,0:T(8,128)(2,1)}, bf16[3072,256]{1,0:T(8,128)(2,1)}, f32[4,384]{1,0:T(4,128)S(1)}, /*index=5*/f32[4,1024]{1,0:T(4,128)S(1)}) custom-call(bf16[232,1024]{1,0:T(8,128)(2,1)} %collective-permute-done.8.refs_0_.refs_6_, ...), custom_call_target="tpu_custom_call" | custom-call | bytes 17343000 | tf_op jit(solution)/shard_map/step/pallas_call | solution.py:275
  86.6 2.3 %collective-permute-done.11.refs_1_.refs_11_ = bf16[232,1024]{1,0:T(8,128)(2,1)S(1)} collective-permute-done((bf16[232,1024]{1,0:T(8,128)(2,1)}, bf16[232,1024]{1,0:T(8,128)(2,1)S(1)}, u32[]{:S(2)}, u32[]{:S(2)}) %collective-permute-start.11) | collective-permute-done | bytes 475168 | tf_op jit(solution)/shard_map/ppermute | solution.py:70
  88.9 5.1 %step.8 = (f32[256,384]{1,0:T(8,128)}, bf16[128,1024]{1,0:T(8,128)(2,1)}, bf16[128,512]{1,0:T(8,128)(2,1)}, bf16[3072,256]{1,0:T(8,128)(2,1)}, f32[4,384]{1,0:T(4,128)S(1)}, /*index=5*/f32[4,1024]{1,0:T(4,128)S(1)}) custom-call(bf16[232,1024]{1,0:T(8,128)(2,1)} %collective-permute-done.10.refs_0_.refs_10_, ...), custom_call_target="tpu_custom_call" | custom-call | bytes 17343000 | tf_op jit(solution)/shard_map/step/pallas_call | solution.py:275
  94.0 5.0 %collective-permute-done.13.refs_0_.refs_14_ = bf16[232,1024]{1,0:T(8,128)(2,1)S(1)} collective-permute-done((bf16[232,1024]{1,0:T(8,128)(2,1)}, bf16[232,1024]{1,0:T(8,128)(2,1)S(1)}, u32[]{:S(2)}, u32[]{:S(2)}) %collective-permute-start.13) | collective-permute-done | bytes 475168 | tf_op jit(solution)/shard_map/ppermute | solution.py:70
  99.1 4.0 %step.9 = (f32[128,384]{1,0:T(8,128)}, bf16[64,1024]{1,0:T(8,128)(2,1)}, bf16[64,512]{1,0:T(8,128)(2,1)}, bf16[3072,128]{1,0:T(8,128)(2,1)}, f32[2,384]{1,0:T(2,128)S(1)}, /*index=5*/f32[2,1024]{1,0:T(2,128)S(1)}) custom-call(bf16[232,1024]{1,0:T(8,128)(2,1)S(1)} %collective-permute-done.13.refs_0_.refs_14_, ...), custom_call_target="tpu_custom_call" | custom-call | bytes 11439000 | tf_op jit(solution)/shard_map/step/pallas_call | solution.py:275
  103.1 1.2 mean_rows.1
  104.3 4.9 %all-to-all-start.1 = ((bf16[16,8,512]{2,1,0:T(8,128)(2,1)}), bf16[16,8,512]{2,1,0:T(8,128)(2,1)S(1)}, u32[]{:S(2)}, u32[]{:S(2)}) async-start(bf16[16,8,512]{2,1,0:T(8,128)(2,1)} %bitcast.34), calls=%async_computation.1 | async-start | bytes 262144 | tf_op jit(solution)/shard_map/all_to_all | solution.py:632
  109.3 4.1 %text_parts.1 = (bf16[256,1024]{1,0:T(8,128)(2,1)}, bf16[256,1024]{1,0:T(8,128)(2,1)}, bf16[256,1024]{1,0:T(8,128)(2,1)}, bf16[256,1024]{1,0:T(8,128)(2,1)}) custom-call(bf16[232,1024]{1,0:T(8,128)(2,1)} %copy-done.3, bf16[232,1024]{1,0:T(8,128)(2,1)} %copy-done.4, bf16[232,1024]{1,0:T(8,128)(2,1)} %collective-permute-done.6.refs_0_.refs_2_, ...), custom_call_target="tpu_custom_call" | custom-call | bytes 14022000 | tf_op jit(solution)/shard_map/text_parts/pallas_call | solution.py:428
  113.4 6.0 %all-to-all-done.1 = bf16[16,8,512]{2,1,0:T(8,128)(2,1)S(1)} async-done(((bf16[16,8,512]{2,1,0:T(8,128)(2,1)}), bf16[16,8,512]{2,1,0:T(8,128)(2,1)S(1)}, u32[]{:S(2)}, u32[]{:S(2)}) %all-to-all-start.1) | async-done | bytes 131104 | tf_op jit(solution)/shard_map/all_to_all | solution.py:632
  119.4 2.6 %collective-permute-start.15 = (bf16[256,1024]{1,0:T(8,128)(2,1)}, bf16[256,1024]{1,0:T(8,128)(2,1)S(1)}, u32[]{:S(2)}, u32[]{:S(2)}) collective-permute-start(bf16[256,1024]{1,0:T(8,128)(2,1)} %get-tuple-element.144), channel_id=1, source_target_pairs={{0,64},{32,96},{64,0},{96,32},{1,65},{33,97},{65,1},{97,33},{2,66}... | collective-permute-start | bytes 1572872 | tf_op jit(solution)/shard_map/ppermute | solution.py:468
  122.0 0.5 collective-permute-start.16
  122.6 6.7 %head.1 = bf16[128,384]{1,0:T(8,128)(2,1)} custom-call(bf16[128,512]{1,0:T(8,128)(2,1)S(1)} %bitcast.29, f32[1,3072]{1,0:T(1,128)} %get-tuple-element.149.means, f32[1,3072]{1,0:T(1,128)} %bitcast.37, f32[1,3072]{1,0:T(1,128)} %bitcast.38, f32[1,3072]{1,0:T(1,128)} %bitcast.39, bf16[3072,1024]{1,0:T(8,128)(2,1)} %w_far.1), custom_call_target="tpu_custom_call" | custom-call | bytes 18450000 | tf_op jit(solution)/shard_map/head/pallas_call | solution.py:377
  129.3 4.4 %all-to-all-start.2 = ((bf16[16,8,384]{2,1,0:T(8,128)(2,1)}), bf16[16,8,384]{2,1,0:T(8,128)(2,1)S(1)}, u32[]{:S(2)}, u32[]{:S(2)}) async-start(bf16[16,8,384]{2,1,0:T(8,128)(2,1)} %bitcast.33), calls=%async_computation.2 | async-start | bytes 196608 | tf_op jit(solution)/shard_map/all_to_all | solution.py:632
  133.7 0.6 collective-permute-done.16.refs_3_
  134.3 2.3 %halved.3 = (bf16[128,1024]{1,0:T(8,128)(2,1)}, bf16[128,1024]{1,0:T(8,128)(2,1)}, bf16[128,1024]{1,0:T(8,128)(2,1)}, bf16[128,1024]{1,0:T(8,128)(2,1)}) custom-call(bf16[256,1024]{1,0:T(8,128)(2,1)} %get-tuple-element.142.refs_0_, bf16[256,1024]{1,0:T(8,128)(2,1)} %get-tuple-element.143.refs_1_, bf16[256,1024]{1,0:T(8,128)(2,1)S(1)} %collective-permute-done.15.refs_2_, ...), custom_call_target="tpu_custom_call" | custom-call | bytes 5535000 | tf_op jit(solution)/shard_map/halved/pallas_call | solution.py:456
  136.6 6.7 %all-to-all-done.2 = bf16[16,8,384]{2,1,0:T(8,128)(2,1)S(1)} async-done(((bf16[16,8,384]{2,1,0:T(8,128)(2,1)}), bf16[16,8,384]{2,1,0:T(8,128)(2,1)S(1)}, u32[]{:S(2)}, u32[]{:S(2)}) %all-to-all-start.2) | async-done | bytes 98336 | tf_op jit(solution)/shard_map/all_to_all | solution.py:632
  143.3 0.3 collective-permute-start.17
  143.6 0.2 collective-permute-start.18
  143.8 8.2 %backward.1 = (bf16[1680,384]{1,0:T(8,128)(2,1)S(1)}, bf16[1680,384]{1,0:T(8,128)(2,1)S(1)}) custom-call(bf16[128,384]{1,0:T(8,128)(2,1)S(1)} %bitcast.30, bf16[384,3072]{1,0:T(8,128)(2,1)S(1)} %copy-done.2, bf16[16,384]{1,0:T(8,128)(2,1)} %get-tuple-element.153.refs_2_, f32[128,384]{1,0:T(8,128)} %get-tuple-element.154.refs_3_, ...), custom_call_target="tpu_custom_call" | custom-call | bytes 23985000 | tf_op jit(solution)/shard_map/backward/pallas_call | solution.py:525
  152.1 4.9 %collective-permute-start.19 = (bf16[1680,384]{1,0:T(8,128)(2,1)S(1)}, bf16[1680,384]{1,0:T(8,128)(2,1)S(1)}, u32[]{:S(2)}, u32[]{:S(2)}) collective-permute-start(bf16[1680,384]{1,0:T(8,128)(2,1)S(1)} %get-tuple-element.172), channel_id=1, source_target_pairs={{0,16},{16,0},{1,17},{17,1},{2,18},{18,2},{3,19},{19,3},{4,20},{20... | collective-permute-start | bytes 3870728 | tf_op jit(solution)/shard_map/ppermute | solution.py:70
  157.0 1.9 halved.4
  158.9 0.6 collective-permute-start.20
  159.4 0.6 collective-permute-start.21
  160.0 1.6 join.1
  161.6 2.5 %collective-permute-done.20.refs_2_ = bf16[64,1024]{1,0:T(8,128)(2,1)S(1)} collective-permute-done((bf16[64,1024]{1,0:T(8,128)(2,1)}, bf16[64,1024]{1,0:T(8,128)(2,1)S(1)}, u32[]{:S(2)}, u32[]{:S(2)}) %collective-permute-start.20) | collective-permute-done | bytes 131104 | tf_op jit(solution)/shard_map/ppermute | solution.py:468
  164.2 4.0 %collective-permute-done.21.refs_3_ = bf16[64,1024]{1,0:T(8,128)(2,1)S(1)} collective-permute-done((bf16[64,1024]{1,0:T(8,128)(2,1)}, bf16[64,1024]{1,0:T(8,128)(2,1)S(1)}, u32[]{:S(2)}, u32[]{:S(2)}) %collective-permute-start.21) | collective-permute-done | bytes 131104 | tf_op jit(solution)/shard_map/ppermute | solution.py:468
  168.2 4.1 %all-to-all-start.3 = ((bf16[8,240,384]{2,1,0:T(8,128)(2,1)}), bf16[8,240,384]{2,1,0:T(8,128)(2,1)S(1)}, u32[]{:S(2)}, u32[]{:S(2)}) async-start(bf16[8,240,384]{2,1,0:T(8,128)(2,1)} %bitcast.31), calls=%async_computation.3 | async-start | bytes 2949120 | tf_op jit(solution)/shard_map/all_to_all | solution.py:632
  172.2 1.7 halved.5
  173.9 1.4 collective-permute-start.22
  175.3 1.3 collective-permute-start.23
  176.6 5.3 %collective-permute-done.22.refs_1_ = bf16[32,1024]{1,0:T(8,128)(2,1)S(1)} collective-permute-done((bf16[32,1024]{1,0:T(8,128)(2,1)}, bf16[32,1024]{1,0:T(8,128)(2,1)S(1)}, u32[]{:S(2)}, u32[]{:S(2)}) %collective-permute-start.22) | collective-permute-done | bytes 65568 | tf_op jit(solution)/shard_map/ppermute | solution.py:468
  181.8 0.8 copy-done.9
  182.7 1.7 img_rows.1
  184.4 0.8 copy-done.8
  185.2 1.7 txt_rows.1
  186.9 5.7 %all-to-all-done.3 = bf16[8,240,384]{2,1,0:T(8,128)(2,1)S(1)} async-done(((bf16[8,240,384]{2,1,0:T(8,128)(2,1)}), bf16[8,240,384]{2,1,0:T(8,128)(2,1)S(1)}, u32[]{:S(2)}, u32[]{:S(2)}) %all-to-all-start.3) | async-done | bytes 1474592 | tf_op jit(solution)/shard_map/all_to_all | solution.py:632
  192.6 1.3 last.1
  (30 shorter events, 0.1 us)
Async XLA Ops:
  5.5 57.2 %copy-start.3 = (bf16[232,1024]{1,0:T(8,128)(2,1)}, bf16[232,1024]{1,0:T(8,128)(2,1)S(1)}, u32[]{:S(2)}) copy-start(bf16[232,1024]{1,0:T(8,128)(2,1)S(1)} %get-tuple-element.94.refs_0_) | copy-start | bytes 1425412
  5.5 13.3 %collective-permute-start = (bf16[232,1024]{1,0:T(8,128)(2,1)S(1)}, bf16[232,1024]{1,0:T(8,128)(2,1)S(1)}, u32[]{:S(2)}, u32[]{:S(2)}) collective-permute-start(bf16[232,1024]{1,0:T(8,128)(2,1)S(1)} %get-tuple-element.94.refs_0_), channel_id=1, source_target_pairs={{0,1},{1,0},{2,3},{3,2},{4,5},{5,4},{6,7},{7,6},{8,9},{9,8},{10,11... | collective-permute-start | bytes 1425416 | tf_op jit(solution)/shard_map/ppermute | solution.py:70
  9.3 25.4 %collective-permute-start.7 = (bf16[232,1024]{1,0:T(8,128)(2,1)S(1)}, bf16[232,1024]{1,0:T(8,128)(2,1)}, u32[]{:S(2)}, u32[]{:S(2)}) collective-permute-start(bf16[232,1024]{1,0:T(8,128)(2,1)S(1)} %get-tuple-element.94.refs_0_), channel_id=1, source_target_pairs={{0,14},{2,0},{4,2},{6,4},{8,6},{10,8},{12,10},{14,12},{1,15},{3,1}... | collective-permute-start | bytes 1425416 | tf_op jit(solution)/shard_map/ppermute | solution.py:70
  14.8 19.8 %collective-permute-start.6 = (bf16[232,1024]{1,0:T(8,128)(2,1)S(1)}, bf16[232,1024]{1,0:T(8,128)(2,1)}, u32[]{:S(2)}, u32[]{:S(2)}) collective-permute-start(bf16[232,1024]{1,0:T(8,128)(2,1)S(1)} %get-tuple-element.94.refs_0_), channel_id=1, source_target_pairs={{0,2},{2,4},{4,6},{6,8},{8,10},{10,12},{12,14},{14,0},{1,3},{3,5},... | collective-permute-start | bytes 1425416 | tf_op jit(solution)/shard_map/ppermute | solution.py:70
  18.8 43.9 %copy-start.4 = (bf16[232,1024]{1,0:T(8,128)(2,1)}, bf16[232,1024]{1,0:T(8,128)(2,1)S(1)}, u32[]{:S(2)}) copy-start(bf16[232,1024]{1,0:T(8,128)(2,1)S(1)} %collective-permute-done.refs_1_) | copy-start | bytes 1425412
  18.8 16.0 %collective-permute-start.3 = (bf16[232,1024]{1,0:T(8,128)(2,1)S(1)}, bf16[232,1024]{1,0:T(8,128)(2,1)}, u32[]{:S(2)}, u32[]{:S(2)}) collective-permute-start(bf16[232,1024]{1,0:T(8,128)(2,1)S(1)} %collective-permute-done.refs_1_), channel_id=1, source_target_pairs={{0,14},{2,0},{4,2},{6,4},{8,6},{10,8},{12,10},{14,12},{1,15},{3,1}... | collective-permute-start | bytes 1425416 | tf_op jit(solution)/shard_map/ppermute | solution.py:70
  27.4 35.4 %copy-start = (bf16[3072,384]{1,0:T(8,128)(2,1)S(1)}, bf16[3072,384]{1,0:T(8,128)(2,1)}, u32[]{:S(2)}) copy-start(bf16[3072,384]{1,0:T(8,128)(2,1)} %refs_2_.5) | copy-start | bytes 7077892
  27.4 35.3 %all-to-all-start = ((bf16[16,40,1024]{2,1,0:T(8,128)(2,1)}), bf16[16,40,1024]{2,1,0:T(8,128)(2,1)}, u32[]{:S(2)}, u32[]{:S(2)}) async-start(bf16[16,40,1024]{2,1,0:T(8,128)(2,1)} %bitcast.32), calls=%async_computation | async-start | bytes 2621440 | tf_op jit(solution)/shard_map/all_to_all | solution.py:632
  34.7 13.6 %collective-permute-start.1 = (bf16[232,1024]{1,0:T(8,128)(2,1)S(1)}, bf16[232,1024]{1,0:T(8,128)(2,1)}, u32[]{:S(2)}, u32[]{:S(2)}) collective-permute-start(bf16[232,1024]{1,0:T(8,128)(2,1)S(1)} %collective-permute-done.refs_1_), channel_id=1, source_target_pairs={{0,2},{2,4},{4,6},{6,8},{8,10},{10,12},{12,14},{14,0},{1,3},{3,5},... | collective-permute-start | bytes 1425416 | tf_op jit(solution)/shard_map/ppermute | solution.py:70
  34.7 23.7 %collective-permute-start.8 = (bf16[232,1024]{1,0:T(8,128)(2,1)}, bf16[232,1024]{1,0:T(8,128)(2,1)}, u32[]{:S(2)}, u32[]{:S(2)}) collective-permute-start(bf16[232,1024]{1,0:T(8,128)(2,1)} %collective-permute-done.6.refs_0_.refs_2_), channel_id=1, source_target_pairs={{0,2},{2,4},{4,6},{6,8},{8,10},{10,12},{12,14},{14,0},{1,3},{3,5},... | collective-permute-start | bytes 1425416 | tf_op jit(solution)/shard_map/ppermute | solution.py:70
  34.8 23.6 %collective-permute-start.4 = (bf16[232,1024]{1,0:T(8,128)(2,1)}, bf16[232,1024]{1,0:T(8,128)(2,1)}, u32[]{:S(2)}, u32[]{:S(2)}) collective-permute-start(bf16[232,1024]{1,0:T(8,128)(2,1)} %collective-permute-done.3.refs_3_.refs_5_), channel_id=1, source_target_pairs={{0,14},{2,0},{4,2},{6,4},{8,6},{10,8},{12,10},{14,12},{1,15},{3,1}... | collective-permute-start | bytes 1425416 | tf_op jit(solution)/shard_map/ppermute | solution.py:70
  37.5 24.9 %collective-permute-start.9 = (bf16[232,1024]{1,0:T(8,128)(2,1)}, bf16[232,1024]{1,0:T(8,128)(2,1)}, u32[]{:S(2)}, u32[]{:S(2)}) collective-permute-start(bf16[232,1024]{1,0:T(8,128)(2,1)} %collective-permute-done.7.refs_2_.refs_4_), channel_id=1, source_target_pairs={{0,14},{2,0},{4,2},{6,4},{8,6},{10,8},{12,10},{14,12},{1,15},{3,1}... | collective-permute-start | bytes 1425416 | tf_op jit(solution)/shard_map/ppermute | solution.py:70
  48.2 23.1 %collective-permute-start.2 = (bf16[232,1024]{1,0:T(8,128)(2,1)}, bf16[232,1024]{1,0:T(8,128)(2,1)}, u32[]{:S(2)}, u32[]{:S(2)}) collective-permute-start(bf16[232,1024]{1,0:T(8,128)(2,1)} %collective-permute-done.1.refs_1_.refs_3_), channel_id=1, source_target_pairs={{0,2},{2,4},{4,6},{6,8},{8,10},{10,12},{12,14},{14,0},{1,3},{3,5},... | collective-permute-start | bytes 1425416 | tf_op jit(solution)/shard_map/ppermute | solution.py:70
  58.4 20.4 %collective-permute-start.10 = (bf16[232,1024]{1,0:T(8,128)(2,1)}, bf16[232,1024]{1,0:T(8,128)(2,1)}, u32[]{:S(2)}, u32[]{:S(2)}) collective-permute-start(bf16[232,1024]{1,0:T(8,128)(2,1)} %collective-permute-done.8.refs_0_.refs_6_), channel_id=1, source_target_pairs={{0,2},{2,4},{4,6},{6,8},{8,10},{10,12},{12,14},{14,0},{1,3},{3,5},... | collective-permute-start | bytes 1425416 | tf_op jit(solution)/shard_map/ppermute | solution.py:70
  58.4 20.4 %collective-permute-start.5 = (bf16[232,1024]{1,0:T(8,128)(2,1)}, bf16[232,1024]{1,0:T(8,128)(2,1)}, u32[]{:S(2)}, u32[]{:S(2)}) collective-permute-start(bf16[232,1024]{1,0:T(8,128)(2,1)} %collective-permute-done.4.refs_3_.refs_9_), channel_id=1, source_target_pairs={{0,14},{2,0},{4,2},{6,4},{8,6},{10,8},{12,10},{14,12},{1,15},{3,1}... | collective-permute-start | bytes 1425416 | tf_op jit(solution)/shard_map/ppermute | solution.py:70
  62.4 24.1 %collective-permute-start.12 = (bf16[232,1024]{1,0:T(8,128)(2,1)}, bf16[232,1024]{1,0:T(8,128)(2,1)}, u32[]{:S(2)}, u32[]{:S(2)}) collective-permute-start(bf16[232,1024]{1,0:T(8,128)(2,1)} %collective-permute-done.9.refs_2_.refs_8_), channel_id=1, source_target_pairs={{0,14},{2,0},{4,2},{6,4},{8,6},{10,8},{12,10},{14,12},{1,15},{3,1}... | collective-permute-start | bytes 1425416 | tf_op jit(solution)/shard_map/ppermute | solution.py:70
  71.4 17.5 %collective-permute-start.11 = (bf16[232,1024]{1,0:T(8,128)(2,1)}, bf16[232,1024]{1,0:T(8,128)(2,1)S(1)}, u32[]{:S(2)}, u32[]{:S(2)}) collective-permute-start(bf16[232,1024]{1,0:T(8,128)(2,1)} %collective-permute-done.2.refs_1_.refs_7_), channel_id=1, source_target_pairs={{0,2},{2,4},{4,6},{6,8},{8,10},{10,12},{12,14},{14,0},{1,3},{3,5},... | collective-permute-start | bytes 1425416 | tf_op jit(solution)/shard_map/ppermute | solution.py:70
  78.8 20.3 %collective-permute-start.13 = (bf16[232,1024]{1,0:T(8,128)(2,1)}, bf16[232,1024]{1,0:T(8,128)(2,1)S(1)}, u32[]{:S(2)}, u32[]{:S(2)}) collective-permute-start(bf16[232,1024]{1,0:T(8,128)(2,1)} %collective-permute-done.10.refs_0_.refs_10_), channel_id=1, source_target_pairs={{0,2},{2,4},{4,6},{6,8},{8,10},{10,12},{12,14},{14,0},{1,3},{3,5},... | collective-permute-start | bytes 1425416 | tf_op jit(solution)/shard_map/ppermute | solution.py:70
  78.8 20.3 %collective-permute-start.14 = (bf16[232,1024]{1,0:T(8,128)(2,1)}, bf16[232,1024]{1,0:T(8,128)(2,1)S(1)}, u32[]{:S(2)}, u32[]{:S(2)}) collective-permute-start(bf16[232,1024]{1,0:T(8,128)(2,1)} %collective-permute-done.5.refs_3_.refs_13_), channel_id=1, source_target_pairs={{0,14},{2,0},{4,2},{6,4},{8,6},{10,8},{12,10},{14,12},{1,15},{3,1}... | collective-permute-start | bytes 1425416 | tf_op jit(solution)/shard_map/ppermute | solution.py:70
  88.9 5.2 %copy-start.5 = (bf16[232,1024]{1,0:T(8,128)(2,1)}, bf16[232,1024]{1,0:T(8,128)(2,1)S(1)}, u32[]{:S(2)}) copy-start(bf16[232,1024]{1,0:T(8,128)(2,1)S(1)} %collective-permute-done.11.refs_1_.refs_11_) | copy-start | bytes 1425412
  99.0 4.1 %copy-start.6 = (bf16[232,1024]{1,0:T(8,128)(2,1)}, bf16[232,1024]{1,0:T(8,128)(2,1)S(1)}, u32[]{:S(2)}) copy-start(bf16[232,1024]{1,0:T(8,128)(2,1)S(1)} %collective-permute-done.13.refs_0_.refs_14_) | copy-start | bytes 1425412
  99.1 4.1 %copy-start.7 = (bf16[232,1024]{1,0:T(8,128)(2,1)}, bf16[232,1024]{1,0:T(8,128)(2,1)S(1)}, u32[]{:S(2)}) copy-start(bf16[232,1024]{1,0:T(8,128)(2,1)S(1)} %collective-permute-done.14.refs_1_.refs_15_) | copy-start | bytes 1425412
  99.1 4.1 %copy-start.1 = (bf16[384,3072]{1,0:T(8,128)(2,1)S(1)}, bf16[384,3072]{1,0:T(8,128)(2,1)}, u32[]{:S(2)}) copy-start(bf16[384,3072]{1,0:T(8,128)(2,1)} %refs_1_.1) | copy-start | bytes 7077892
  104.3 15.0 %all-to-all-start.1 = ((bf16[16,8,512]{2,1,0:T(8,128)(2,1)}), bf16[16,8,512]{2,1,0:T(8,128)(2,1)S(1)}, u32[]{:S(2)}, u32[]{:S(2)}) async-start(bf16[16,8,512]{2,1,0:T(8,128)(2,1)} %bitcast.34), calls=%async_computation.1 | async-start | bytes 262144 | tf_op jit(solution)/shard_map/all_to_all | solution.py:632
  119.4 14.3 %collective-permute-start.15 = (bf16[256,1024]{1,0:T(8,128)(2,1)}, bf16[256,1024]{1,0:T(8,128)(2,1)S(1)}, u32[]{:S(2)}, u32[]{:S(2)}) collective-permute-start(bf16[256,1024]{1,0:T(8,128)(2,1)} %get-tuple-element.144), channel_id=1, source_target_pairs={{0,64},{32,96},{64,0},{96,32},{1,65},{33,97},{65,1},{97,33},{2,66}... | collective-permute-start | bytes 1572872 | tf_op jit(solution)/shard_map/ppermute | solution.py:468
  122.0 12.3 %collective-permute-start.16 = (bf16[256,1024]{1,0:T(8,128)(2,1)}, bf16[256,1024]{1,0:T(8,128)(2,1)S(1)}, u32[]{:S(2)}, u32[]{:S(2)}) collective-permute-start(bf16[256,1024]{1,0:T(8,128)(2,1)} %get-tuple-element.145), channel_id=1, source_target_pairs={{0,1},{1,0},{2,3},{3,2},{4,5},{5,4},{6,7},{7,6},{8,9},{9,8},{10,11... | collective-permute-start | bytes 1572872 | tf_op jit(solution)/shard_map/ppermute | solution.py:70
  122.6 21.2 %copy-start.2 = (bf16[384,3072]{1,0:T(8,128)(2,1)S(1)}, bf16[384,3072]{1,0:T(8,128)(2,1)}, u32[]{:S(2)}) copy-start(bf16[384,3072]{1,0:T(8,128)(2,1)} %refs_1_.1) | copy-start | bytes 7077892
  129.3 14.1 %all-to-all-start.2 = ((bf16[16,8,384]{2,1,0:T(8,128)(2,1)}), bf16[16,8,384]{2,1,0:T(8,128)(2,1)S(1)}, u32[]{:S(2)}, u32[]{:S(2)}) async-start(bf16[16,8,384]{2,1,0:T(8,128)(2,1)} %bitcast.33), calls=%async_computation.2 | async-start | bytes 196608 | tf_op jit(solution)/shard_map/all_to_all | solution.py:632
  143.3 8.7 %collective-permute-start.17 = (bf16[128,1024]{1,0:T(8,128)(2,1)}, bf16[128,1024]{1,0:T(8,128)(2,1)S(1)}, u32[]{:S(2)}, u32[]{:S(2)}) collective-permute-start(bf16[128,1024]{1,0:T(8,128)(2,1)} %get-tuple-element.165), channel_id=1, source_target_pairs={{0,32},{32,0},{64,96},{96,64},{1,33},{33,1},{65,97},{97,65},{2,34}... | collective-permute-start | bytes 786440 | tf_op jit(solution)/shard_map/ppermute | solution.py:468
  143.6 8.4 %collective-permute-start.18 = (bf16[128,1024]{1,0:T(8,128)(2,1)}, bf16[128,1024]{1,0:T(8,128)(2,1)S(1)}, u32[]{:S(2)}, u32[]{:S(2)}) collective-permute-start(bf16[128,1024]{1,0:T(8,128)(2,1)} %get-tuple-element.166), channel_id=1, source_target_pairs={{0,2},{2,0},{4,6},{6,4},{8,10},{10,8},{12,14},{14,12},{1,3},{3,1},... | collective-permute-start | bytes 786440 | tf_op jit(solution)/shard_map/ppermute | solution.py:468
  152.1 8.0 %collective-permute-start.19 = (bf16[1680,384]{1,0:T(8,128)(2,1)S(1)}, bf16[1680,384]{1,0:T(8,128)(2,1)S(1)}, u32[]{:S(2)}, u32[]{:S(2)}) collective-permute-start(bf16[1680,384]{1,0:T(8,128)(2,1)S(1)} %get-tuple-element.172), channel_id=1, source_target_pairs={{0,16},{16,0},{1,17},{17,1},{2,18},{18,2},{3,19},{19,3},{4,20},{20... | collective-permute-start | bytes 3870728 | tf_op jit(solution)/shard_map/ppermute | solution.py:70
  158.9 5.3 %collective-permute-start.20 = (bf16[64,1024]{1,0:T(8,128)(2,1)}, bf16[64,1024]{1,0:T(8,128)(2,1)S(1)}, u32[]{:S(2)}, u32[]{:S(2)}) collective-permute-start(bf16[64,1024]{1,0:T(8,128)(2,1)} %get-tuple-element.173), channel_id=1, source_target_pairs={{0,128},{128,0},{1,129},{129,1},{2,130},{130,2},{3,131},{131,3},{4... | collective-permute-start | bytes 393224 | tf_op jit(solution)/shard_map/ppermute | solution.py:468
  159.4 8.7 %collective-permute-start.21 = (bf16[64,1024]{1,0:T(8,128)(2,1)}, bf16[64,1024]{1,0:T(8,128)(2,1)S(1)}, u32[]{:S(2)}, u32[]{:S(2)}) collective-permute-start(bf16[64,1024]{1,0:T(8,128)(2,1)} %get-tuple-element.174), channel_id=1, source_target_pairs={{0,4},{2,6},{4,0},{6,2},{8,12},{10,14},{12,8},{14,10},{1,5},{3,7},... | collective-permute-start | bytes 393224 | tf_op jit(solution)/shard_map/ppermute | solution.py:468
  168.2 24.4 %all-to-all-start.3 = ((bf16[8,240,384]{2,1,0:T(8,128)(2,1)}), bf16[8,240,384]{2,1,0:T(8,128)(2,1)S(1)}, u32[]{:S(2)}, u32[]{:S(2)}) async-start(bf16[8,240,384]{2,1,0:T(8,128)(2,1)} %bitcast.31), calls=%async_computation.3 | async-start | bytes 2949120 | tf_op jit(solution)/shard_map/all_to_all | solution.py:632
  173.9 7.9 %collective-permute-start.22 = (bf16[32,1024]{1,0:T(8,128)(2,1)}, bf16[32,1024]{1,0:T(8,128)(2,1)S(1)}, u32[]{:S(2)}, u32[]{:S(2)}) collective-permute-start(bf16[32,1024]{1,0:T(8,128)(2,1)} %get-tuple-element.178), channel_id=1, source_target_pairs={{0,8},{2,10},{4,12},{6,14},{8,0},{10,2},{12,4},{14,6},{1,9},{3,11}... | collective-permute-start | bytes 196616 | tf_op jit(solution)/shard_map/ppermute | solution.py:468
  175.3 9.1 %collective-permute-start.23 = (bf16[32,1024]{1,0:T(8,128)(2,1)}, bf16[32,1024]{1,0:T(8,128)(2,1)S(1)}, u32[]{:S(2)}, u32[]{:S(2)}) collective-permute-start(bf16[32,1024]{1,0:T(8,128)(2,1)} %get-tuple-element.180), channel_id=1, source_target_pairs={{0,16},{16,0},{1,17},{17,1},{2,18},{18,2},{3,19},{19,3},{4,20},{20... | collective-permute-start | bytes 196616 | tf_op jit(solution)/shard_map/ppermute | solution.py:468
  181.8 0.8 copy-start.9
  184.4 0.8 copy-start.8

commit v3 on v2

--- a/solution.py
+++ b/solution.py
@@ -89,7 +89,9 @@
     return jnp.where(row == 0, value >> 7, jnp.where(row == 1, value & 127, 0)).astype(F32)
 
 
-def text_rows_kernel(txt, txt_ids, txt_all, ids, txt_pay, sems):
+def front_kernel(
+    img, txt, img_ids, txt_ids, block_in, taps, gain, bias, blk, txt_all, means, mixed, ids, txt_pay, sems
+):
     txt_pay[0:PAIRS, :] = unit_rows(txt[...].astype(F32))[0].astype(BF)
     place = (lax.axis_index("ylo") * 4 + lax.axis_index("x")) * 2 + lax.axis_index("core")
     txt_pay[PAIRS:TXT_ROWS, :] = pltpu.roll(id_rows(txt_ids, ids), place * PAIRS, 1).astype(BF)
@@ -101,27 +103,6 @@
     ]
     for copy in copies:
         copy.start()
-    for copy in copies:
-        copy.wait()
-
-
-def text_rows(*args):
-    return pl.pallas_call(
-        text_rows_kernel,
-        out_shape=far(16 * TXT_ROWS, EMBED, BF),
-        out_specs=loose(1)[0],
-        scratch_shapes=[
-            pltpu.VMEM((8, EMBED), jnp.int32),
-            pltpu.VMEM((TXT_ROWS, EMBED), BF),
-            pltpu.SemaphoreType.DMA((16,)),
-        ],
-        compiler_params=params(4),
-        cost_estimate=cost(1.0),
-        name="text_rows",
-    )(*from_far(*args))
-
-
-def front_kernel(img, img_ids, block_in, taps, gain, bias, blk, means, mixed, ids):
     blk[IMG_AT : IMG_AT + PAIRS, :] = unit_rows(img[...].astype(F32))[0].astype(BF)
     blk[IMG_AT + PAIRS : ROWS, :] = id_rows(img_ids, ids).astype(BF)
     column = lax.broadcasted_iota(jnp.int32, (SIDE, 128), 0)
@@ -173,15 +154,24 @@
         blk[seg * PATCHES : (seg + 1) * PATCHES, lane : lane + 128] = (
             normal * gain[:, at] + bias[:, at]
         ).astype(BF)
+    for copy in copies:
+        copy.wait()
 
 
 def front(*args):
     return pl.pallas_call(
         front_kernel,
-        out_shape=(near(ROWS, EMBED, BF), far(1, WIDTH, F32)),
+        out_shape=(
+            near(ROWS, EMBED, BF),
+            far(16 * TXT_ROWS, EMBED, BF),
+            far(1, WIDTH, F32),
+        ),
+        out_specs=(pl.BlockSpec(), *loose(1), pl.BlockSpec()),
         scratch_shapes=[
             pltpu.VMEM((PATCHES, WIDTH), F32),
             pltpu.VMEM((8, EMBED), jnp.int32),
+            pltpu.VMEM((TXT_ROWS, EMBED), BF),
+            pltpu.SemaphoreType.DMA((16,)),
         ],
         compiler_params=params(8),
         cost_estimate=cost(4.5),
@@ -650,15 +640,17 @@
     head_bias,
     w_proj,
 ):
-    texts = swap(text_rows(txt_emb, txt_ids.reshape(1, PAIRS)), DP, 16)
-    blk, means = front(
+    blk, txt_all, means = front(
         img_emb,
+        txt_emb,
         img_ids.reshape(1, PAIRS),
+        txt_ids.reshape(1, PAIRS),
         block_in,
         dw_kernel,
         ln_gain.reshape(1, WIDTH),
         ln_bias.reshape(1, WIDTH),
     )
+    texts = swap(txt_all, DP, 16)
     temper = temp_log.reshape(1, 1)
     offset = logit_bias.reshape(1, 1)
     got = {(0, 0): blk}

time: 195 us -> 193 us (0.990)
    pallas_call x2 -> x1, Pallas kernels: 7.07 us -> 5.55 us  [front(): pl.pallas_call(front_kernel, out_shape=(near(ROWS, EMBED, BF), far(16 * T...]
  transfers between devices with their start and end apart: 28 -> 28, of which waited for: 13 -> 14; matrix products, arithmetic and copies ran while one was open for 0% -> 0% of each run, Pallas kernels for 26% -> 25%
where the time goes in v3:
time: 193 us; the launch traced here: 192 us
  waiting for transfers between devices  68.1 us (35%)
  Pallas kernels  60.8 us (32%)
  starting transfers between devices  59.4 us (31%)
  between operations  2.22 us (1%)
    ppermute x17, waiting for transfers between devices, hop(): lax.ppermute(value, axis, [(i, (i + step) % length) for i in range(length)])  37.9 us
    ppermute x17, starting transfers between devices, hop(): lax.ppermute(value, axis, [(i, (i + step) % length) for i in range(length)])  32 us
    pallas_call x5, Pallas kernels, step(): pl.pallas_call(functools.partial(step_kernel, count), out_shape=(*(far(*d...  22.9 us
    all_to_all x4, starting transfers between devices, swap(): return lax.all_to_all(parts, axes, 0, 0, tiled=True).reshape(rows, columns)  20.4 us
    all_to_all x4, waiting for transfers between devices, swap(): return lax.all_to_all(parts, axes, 0, 0, tiled=True).reshape(rows, columns)  18.4 us
    ppermute x7, waiting for transfers between devices, partner(): return lax.ppermute(value, axis, [(i, i ^ bit) for i in range(length)])  11.8 us
    pallas_call x1, Pallas kernels, backward(): pl.pallas_call(back_kernel, out_shape=(near(8 * HALF + 16, HID, BF),) * 2...  8.23 us
    ppermute x7, starting transfers between devices, partner(): return lax.ppermute(value, axis, [(i, i ^ bit) for i in range(length)])  6.95 us
  transfers between devices with their start and end apart: 28, of which 14 were waited for; matrix products, arithmetic and copies ran while one was open for 0% of the time, Pallas kernels for 25%

profile of v3, /device:TPU:1, one launch (start us, length us, event | category | flops | bytes accessed | tf_op | source)
XLA Modules:
  0.0 192.2 jit_solution(16620436003106791949)
XLA Ops:
  0.6 5.6 %front.1 = (bf16[232,1024]{1,0:T(8,128)(2,1)S(1)}, bf16[640,1024]{1,0:T(8,128)(2,1)}, f32[1,3072]{1,0:T(1,128)}) custom-call(bf16[32,1024]{1,0:T(8,128)(2,1)} %refs_2_.6, bf16[32,1024]{1,0:T(8,128)(2,1)} %refs_2_.7, s32[1,32]{1,0:T(1,128)} %bitcast.40, s32[1,32]{1,0:T(1,128)} %bitcast.41, bf16[64,3072]{1,0:T(8,128)(2,1)} %block_in.1, f32[49,3072]{1,0:T(8,128)} %taps.1, ...), custom_call_target="tpu_custom_call" | custom-call | bytes 16605000 | tf_op jit(solution)/shard_map/front/pallas_call | solution.py:162
  6.2 0.0 copy-start
  6.2 3.8 %collective-permute-start = (bf16[232,1024]{1,0:T(8,128)(2,1)S(1)}, bf16[232,1024]{1,0:T(8,128)(2,1)S(1)}, u32[]{:S(2)}, u32[]{:S(2)}) collective-permute-start(bf16[232,1024]{1,0:T(8,128)(2,1)S(1)} %get-tuple-element.95.refs_0_), channel_id=1, source_target_pairs={{0,1},{1,0},{2,3},{3,2},{4,5},{5,4},{6,7},{7,6},{8,9},{9,8},{10,11... | collective-permute-start | bytes 1425416 | tf_op jit(solution)/shard_map/ppermute | solution.py:70
  10.0 5.6 %collective-permute-start.7 = (bf16[232,1024]{1,0:T(8,128)(2,1)S(1)}, bf16[232,1024]{1,0:T(8,128)(2,1)}, u32[]{:S(2)}, u32[]{:S(2)}) collective-permute-start(bf16[232,1024]{1,0:T(8,128)(2,1)S(1)} %get-tuple-element.95.refs_0_), channel_id=1, source_target_pairs={{0,14},{2,0},{4,2},{6,4},{8,6},{10,8},{12,10},{14,12},{1,15},{3,1}... | collective-permute-start | bytes 1425416 | tf_op jit(solution)/shard_map/ppermute | solution.py:70
  15.6 4.0 %collective-permute-done.refs_1_ = bf16[232,1024]{1,0:T(8,128)(2,1)S(1)} collective-permute-done((bf16[232,1024]{1,0:T(8,128)(2,1)S(1)}, bf16[232,1024]{1,0:T(8,128)(2,1)S(1)}, u32[]{:S(2)}, u32[]{:S(2)}) %collective-permute-start) | collective-permute-done | bytes 475168 | tf_op jit(solution)/shard_map/ppermute | solution.py:70
  19.6 6.4 %collective-permute-start.3 = (bf16[232,1024]{1,0:T(8,128)(2,1)S(1)}, bf16[232,1024]{1,0:T(8,128)(2,1)}, u32[]{:S(2)}, u32[]{:S(2)}) collective-permute-start(bf16[232,1024]{1,0:T(8,128)(2,1)S(1)} %collective-permute-done.refs_1_), channel_id=1, source_target_pairs={{0,14},{2,0},{4,2},{6,4},{8,6},{10,8},{12,10},{14,12},{1,15},{3,1}... | collective-permute-start | bytes 1425416 | tf_op jit(solution)/shard_map/ppermute | solution.py:70
  26.0 7.2 %all-to-all-start = ((bf16[16,40,1024]{2,1,0:T(8,128)(2,1)}), bf16[16,40,1024]{2,1,0:T(8,128)(2,1)}, u32[]{:S(2)}, u32[]{:S(2)}) async-start(bf16[16,40,1024]{2,1,0:T(8,128)(2,1)} %bitcast.32), calls=%async_computation | async-start | bytes 2621440 | tf_op jit(solution)/shard_map/all_to_all | solution.py:622
  33.1 0.0 collective-permute-done.6.refs_0_.refs_2_
  33.1 0.1 collective-permute-start.8
  33.2 1.3 collective-permute-done.3.refs_3_.refs_5_
  34.6 3.5 %collective-permute-start.4 = (bf16[232,1024]{1,0:T(8,128)(2,1)}, bf16[232,1024]{1,0:T(8,128)(2,1)}, u32[]{:S(2)}, u32[]{:S(2)}) collective-permute-start(bf16[232,1024]{1,0:T(8,128)(2,1)} %collective-permute-done.3.refs_3_.refs_5_), channel_id=1, source_target_pairs={{0,14},{2,0},{4,2},{6,4},{8,6},{10,8},{12,10},{14,12},{1,15},{3,1}... | collective-permute-start | bytes 1425416 | tf_op jit(solution)/shard_map/ppermute | solution.py:70
  38.1 0.0 collective-permute-start.9
  38.1 8.6 %collective-permute-done.1.refs_1_.refs_3_ = bf16[232,1024]{1,0:T(8,128)(2,1)} collective-permute-done((bf16[232,1024]{1,0:T(8,128)(2,1)S(1)}, bf16[232,1024]{1,0:T(8,128)(2,1)}, u32[]{:S(2)}, u32[]{:S(2)}) %collective-permute-start.1) | collective-permute-done | bytes 475168 | tf_op jit(solution)/shard_map/ppermute | solution.py:70
  46.7 0.0 collective-permute-start.2
  46.7 10.2 %collective-permute-done.8.refs_0_.refs_6_ = bf16[232,1024]{1,0:T(8,128)(2,1)} collective-permute-done((bf16[232,1024]{1,0:T(8,128)(2,1)}, bf16[232,1024]{1,0:T(8,128)(2,1)}, u32[]{:S(2)}, u32[]{:S(2)}) %collective-permute-start.8) | collective-permute-done | bytes 475168 | tf_op jit(solution)/shard_map/ppermute | solution.py:70
  56.9 0.0 collective-permute-start.10
  56.9 0.0 collective-permute-done.4.refs_3_.refs_9_
  56.9 2.7 %collective-permute-start.5 = (bf16[232,1024]{1,0:T(8,128)(2,1)}, bf16[232,1024]{1,0:T(8,128)(2,1)}, u32[]{:S(2)}, u32[]{:S(2)}) collective-permute-start(bf16[232,1024]{1,0:T(8,128)(2,1)} %collective-permute-done.4.refs_3_.refs_9_), channel_id=1, source_target_pairs={{0,14},{2,0},{4,2},{6,4},{8,6},{10,8},{12,10},{14,12},{1,15},{3,1}... | collective-permute-start | bytes 1425416 | tf_op jit(solution)/shard_map/ppermute | solution.py:70
  60.8 0.0 collective-permute-done.9.refs_2_.refs_8_
  60.8 0.3 collective-permute-start.12
  61.1 3.5 %step.5 = (f32[128,384]{1,0:T(8,128)}, bf16[64,1024]{1,0:T(8,128)(2,1)}, bf16[64,512]{1,0:T(8,128)(2,1)}, bf16[3072,128]{1,0:T(8,128)(2,1)}, f32[2,384]{1,0:T(2,128)S(1)}, /*index=5*/f32[2,1024]{1,0:T(2,128)S(1)}) custom-call(bf16[232,1024]{1,0:T(8,128)(2,1)S(1)} %get-tuple-element.95.refs_0_, bf16[232,1024]{1,0:T(8,128)(2,1)S(1)} %collective-permute-done.refs_1_, ...), custom_call_target="tpu_custom_call" | custom-call | bytes 11439000 | tf_op jit(solution)/shard_map/step/pallas_call | solution.py:265
  64.7 5.1 %step.6 = (f32[256,384]{1,0:T(8,128)}, bf16[128,1024]{1,0:T(8,128)(2,1)}, bf16[128,512]{1,0:T(8,128)(2,1)}, bf16[3072,256]{1,0:T(8,128)(2,1)}, f32[4,384]{1,0:T(4,128)S(1)}, /*index=5*/f32[4,1024]{1,0:T(4,128)S(1)}) custom-call(bf16[232,1024]{1,0:T(8,128)(2,1)} %collective-permute-done.6.refs_0_.refs_2_, ...), custom_call_target="tpu_custom_call" | custom-call | bytes 17343000 | tf_op jit(solution)/shard_map/step/pallas_call | solution.py:265
  69.8 0.0 collective-permute-done.2.refs_1_.refs_7_
  69.8 1.5 collective-permute-start.11
  71.3 5.9 %collective-permute-done.10.refs_0_.refs_10_ = bf16[232,1024]{1,0:T(8,128)(2,1)} collective-permute-done((bf16[232,1024]{1,0:T(8,128)(2,1)}, bf16[232,1024]{1,0:T(8,128)(2,1)}, u32[]{:S(2)}, u32[]{:S(2)}) %collective-permute-start.10) | collective-permute-done | bytes 475168 | tf_op jit(solution)/shard_map/ppermute | solution.py:70
  77.2 0.0 collective-permute-start.13
  77.2 2.7 %collective-permute-start.14 = (bf16[232,1024]{1,0:T(8,128)(2,1)}, bf16[232,1024]{1,0:T(8,128)(2,1)S(1)}, u32[]{:S(2)}, u32[]{:S(2)}) collective-permute-start(bf16[232,1024]{1,0:T(8,128)(2,1)} %collective-permute-done.5.refs_3_.refs_13_), channel_id=1, source_target_pairs={{0,14},{2,0},{4,2},{6,4},{8,6},{10,8},{12,10},{14,12},{1,15},{3,1}... | collective-permute-start | bytes 1425416 | tf_op jit(solution)/shard_map/ppermute | solution.py:70
  79.9 5.1 %step.7 = (f32[256,384]{1,0:T(8,128)}, bf16[128,1024]{1,0:T(8,128)(2,1)}, bf16[128,512]{1,0:T(8,128)(2,1)}, bf16[3072,256]{1,0:T(8,128)(2,1)}, f32[4,384]{1,0:T(4,128)S(1)}, /*index=5*/f32[4,1024]{1,0:T(4,128)S(1)}) custom-call(bf16[232,1024]{1,0:T(8,128)(2,1)} %collective-permute-done.8.refs_0_.refs_6_, ...), custom_call_target="tpu_custom_call" | custom-call | bytes 17343000 | tf_op jit(solution)/shard_map/step/pallas_call | solution.py:265
  85.0 2.3 %collective-permute-done.11.refs_1_.refs_11_ = bf16[232,1024]{1,0:T(8,128)(2,1)S(1)} collective-permute-done((bf16[232,1024]{1,0:T(8,128)(2,1)}, bf16[232,1024]{1,0:T(8,128)(2,1)S(1)}, u32[]{:S(2)}, u32[]{:S(2)}) %collective-permute-start.11) | collective-permute-done | bytes 475168 | tf_op jit(solution)/shard_map/ppermute | solution.py:70
  87.3 5.1 %step.8 = (f32[256,384]{1,0:T(8,128)}, bf16[128,1024]{1,0:T(8,128)(2,1)}, bf16[128,512]{1,0:T(8,128)(2,1)}, bf16[3072,256]{1,0:T(8,128)(2,1)}, f32[4,384]{1,0:T(4,128)S(1)}, /*index=5*/f32[4,1024]{1,0:T(4,128)S(1)}) custom-call(bf16[232,1024]{1,0:T(8,128)(2,1)} %collective-permute-done.10.refs_0_.refs_10_, ...), custom_call_target="tpu_custom_call" | custom-call | bytes 17343000 | tf_op jit(solution)/shard_map/step/pallas_call | solution.py:265
  92.5 5.0 %collective-permute-done.13.refs_0_.refs_14_ = bf16[232,1024]{1,0:T(8,128)(2,1)S(1)} collective-permute-done((bf16[232,1024]{1,0:T(8,128)(2,1)}, bf16[232,1024]{1,0:T(8,128)(2,1)S(1)}, u32[]{:S(2)}, u32[]{:S(2)}) %collective-permute-start.13) | collective-permute-done | bytes 475168 | tf_op jit(solution)/shard_map/ppermute | solution.py:70
  97.5 4.0 %step.9 = (f32[128,384]{1,0:T(8,128)}, bf16[64,1024]{1,0:T(8,128)(2,1)}, bf16[64,512]{1,0:T(8,128)(2,1)}, bf16[3072,128]{1,0:T(8,128)(2,1)}, f32[2,384]{1,0:T(2,128)S(1)}, /*index=5*/f32[2,1024]{1,0:T(2,128)S(1)}) custom-call(bf16[232,1024]{1,0:T(8,128)(2,1)S(1)} %collective-permute-done.13.refs_0_.refs_14_, ...), custom_call_target="tpu_custom_call" | custom-call | bytes 11439000 | tf_op jit(solution)/shard_map/step/pallas_call | solution.py:265
  101.6 1.2 mean_rows.1
  102.8 4.9 %all-to-all-start.1 = ((bf16[16,8,512]{2,1,0:T(8,128)(2,1)}), bf16[16,8,512]{2,1,0:T(8,128)(2,1)S(1)}, u32[]{:S(2)}, u32[]{:S(2)}) async-start(bf16[16,8,512]{2,1,0:T(8,128)(2,1)} %bitcast.34), calls=%async_computation.1 | async-start | bytes 262144 | tf_op jit(solution)/shard_map/all_to_all | solution.py:622
  107.6 4.1 %text_parts.1 = (bf16[256,1024]{1,0:T(8,128)(2,1)}, bf16[256,1024]{1,0:T(8,128)(2,1)}, bf16[256,1024]{1,0:T(8,128)(2,1)}, bf16[256,1024]{1,0:T(8,128)(2,1)}) custom-call(bf16[232,1024]{1,0:T(8,128)(2,1)} %copy-done.3, bf16[232,1024]{1,0:T(8,128)(2,1)} %copy-done.4, bf16[232,1024]{1,0:T(8,128)(2,1)} %collective-permute-done.6.refs_0_.refs_2_, ...), custom_call_target="tpu_custom_call" | custom-call | bytes 14022000 | tf_op jit(solution)/shard_map/text_parts/pallas_call | solution.py:418
  111.7 6.0 %all-to-all-done.1 = bf16[16,8,512]{2,1,0:T(8,128)(2,1)S(1)} async-done(((bf16[16,8,512]{2,1,0:T(8,128)(2,1)}), bf16[16,8,512]{2,1,0:T(8,128)(2,1)S(1)}, u32[]{:S(2)}, u32[]{:S(2)}) %all-to-all-start.1) | async-done | bytes 131104 | tf_op jit(solution)/shard_map/all_to_all | solution.py:622
  117.7 2.6 %collective-permute-start.15 = (bf16[256,1024]{1,0:T(8,128)(2,1)}, bf16[256,1024]{1,0:T(8,128)(2,1)S(1)}, u32[]{:S(2)}, u32[]{:S(2)}) collective-permute-start(bf16[256,1024]{1,0:T(8,128)(2,1)} %get-tuple-element.146), channel_id=1, source_target_pairs={{0,64},{32,96},{64,0},{96,32},{1,65},{33,97},{65,1},{97,33},{2,66}... | collective-permute-start | bytes 1572872 | tf_op jit(solution)/shard_map/ppermute | solution.py:458
  120.4 0.5 collective-permute-start.16
  120.9 6.7 %head.1 = bf16[128,384]{1,0:T(8,128)(2,1)} custom-call(bf16[128,512]{1,0:T(8,128)(2,1)S(1)} %bitcast.29, f32[1,3072]{1,0:T(1,128)} %get-tuple-element.151.means, f32[1,3072]{1,0:T(1,128)} %bitcast.37, f32[1,3072]{1,0:T(1,128)} %bitcast.38, f32[1,3072]{1,0:T(1,128)} %bitcast.39, bf16[3072,1024]{1,0:T(8,128)(2,1)} %w_far.1), custom_call_target="tpu_custom_call" | custom-call | bytes 18450000 | tf_op jit(solution)/shard_map/head/pallas_call | solution.py:367
  127.6 4.4 %all-to-all-start.2 = ((bf16[16,8,384]{2,1,0:T(8,128)(2,1)}), bf16[16,8,384]{2,1,0:T(8,128)(2,1)S(1)}, u32[]{:S(2)}, u32[]{:S(2)}) async-start(bf16[16,8,384]{2,1,0:T(8,128)(2,1)} %bitcast.33), calls=%async_computation.2 | async-start | bytes 196608 | tf_op jit(solution)/shard_map/all_to_all | solution.py:622
  132.0 0.6 collective-permute-done.16.refs_3_
  132.6 2.3 %halved.3 = (bf16[128,1024]{1,0:T(8,128)(2,1)}, bf16[128,1024]{1,0:T(8,128)(2,1)}, bf16[128,1024]{1,0:T(8,128)(2,1)}, bf16[128,1024]{1,0:T(8,128)(2,1)}) custom-call(bf16[256,1024]{1,0:T(8,128)(2,1)} %get-tuple-element.144.refs_0_, bf16[256,1024]{1,0:T(8,128)(2,1)} %get-tuple-element.145.refs_1_, bf16[256,1024]{1,0:T(8,128)(2,1)S(1)} %collective-permute-done.15.refs_2_, ...), custom_call_target="tpu_custom_call" | custom-call | bytes 5535000 | tf_op jit(solution)/shard_map/halved/pallas_call | solution.py:446
  135.0 6.7 %all-to-all-done.2 = bf16[16,8,384]{2,1,0:T(8,128)(2,1)S(1)} async-done(((bf16[16,8,384]{2,1,0:T(8,128)(2,1)}), bf16[16,8,384]{2,1,0:T(8,128)(2,1)S(1)}, u32[]{:S(2)}, u32[]{:S(2)}) %all-to-all-start.2) | async-done | bytes 98336 | tf_op jit(solution)/shard_map/all_to_all | solution.py:622
  141.7 0.3 collective-permute-start.17
  142.0 0.2 collective-permute-start.18
  142.1 8.2 %backward.1 = (bf16[1680,384]{1,0:T(8,128)(2,1)S(1)}, bf16[1680,384]{1,0:T(8,128)(2,1)S(1)}) custom-call(bf16[128,384]{1,0:T(8,128)(2,1)S(1)} %bitcast.30, bf16[384,3072]{1,0:T(8,128)(2,1)S(1)} %copy-done.2, bf16[16,384]{1,0:T(8,128)(2,1)} %get-tuple-element.155.refs_2_, f32[128,384]{1,0:T(8,128)} %get-tuple-element.156.refs_3_, ...), custom_call_target="tpu_custom_call" | custom-call | bytes 23985000 | tf_op jit(solution)/shard_map/backward/pallas_call | solution.py:515
  150.4 4.9 %collective-permute-start.19 = (bf16[1680,384]{1,0:T(8,128)(2,1)S(1)}, bf16[1680,384]{1,0:T(8,128)(2,1)S(1)}, u32[]{:S(2)}, u32[]{:S(2)}) collective-permute-start(bf16[1680,384]{1,0:T(8,128)(2,1)S(1)} %get-tuple-element.174), channel_id=1, source_target_pairs={{0,16},{16,0},{1,17},{17,1},{2,18},{18,2},{3,19},{19,3},{4,20},{20... | collective-permute-start | bytes 3870728 | tf_op jit(solution)/shard_map/ppermute | solution.py:70
  155.3 1.9 halved.4
  157.2 0.6 collective-permute-start.20
  157.8 0.6 collective-permute-start.21
  158.4 1.6 join.1
  160.0 2.5 %collective-permute-done.20.refs_2_ = bf16[64,1024]{1,0:T(8,128)(2,1)S(1)} collective-permute-done((bf16[64,1024]{1,0:T(8,128)(2,1)}, bf16[64,1024]{1,0:T(8,128)(2,1)S(1)}, u32[]{:S(2)}, u32[]{:S(2)}) %collective-permute-start.20) | collective-permute-done | bytes 131104 | tf_op jit(solution)/shard_map/ppermute | solution.py:458
  162.5 4.0 %collective-permute-done.21.refs_3_ = bf16[64,1024]{1,0:T(8,128)(2,1)S(1)} collective-permute-done((bf16[64,1024]{1,0:T(8,128)(2,1)}, bf16[64,1024]{1,0:T(8,128)(2,1)S(1)}, u32[]{:S(2)}, u32[]{:S(2)}) %collective-permute-start.21) | collective-permute-done | bytes 131104 | tf_op jit(solution)/shard_map/ppermute | solution.py:458
  166.5 4.1 %all-to-all-start.3 = ((bf16[8,240,384]{2,1,0:T(8,128)(2,1)}), bf16[8,240,384]{2,1,0:T(8,128)(2,1)S(1)}, u32[]{:S(2)}, u32[]{:S(2)}) async-start(bf16[8,240,384]{2,1,0:T(8,128)(2,1)} %bitcast.31), calls=%async_computation.3 | async-start | bytes 2949120 | tf_op jit(solution)/shard_map/all_to_all | solution.py:622
  170.6 1.7 halved.5
  172.3 1.4 collective-permute-start.22
  173.7 1.3 collective-permute-start.23
  174.9 5.3 %collective-permute-done.22.refs_1_ = bf16[32,1024]{1,0:T(8,128)(2,1)S(1)} collective-permute-done((bf16[32,1024]{1,0:T(8,128)(2,1)}, bf16[32,1024]{1,0:T(8,128)(2,1)S(1)}, u32[]{:S(2)}, u32[]{:S(2)}) %collective-permute-start.22) | collective-permute-done | bytes 65568 | tf_op jit(solution)/shard_map/ppermute | solution.py:458
  180.2 0.8 copy-done.9
  181.0 1.7 img_rows.1
  182.7 0.8 copy-done.8
  183.6 1.7 txt_rows.1
  185.3 5.7 %all-to-all-done.3 = bf16[8,240,384]{2,1,0:T(8,128)(2,1)S(1)} async-done(((bf16[8,240,384]{2,1,0:T(8,128)(2,1)}), bf16[8,240,384]{2,1,0:T(8,128)(2,1)S(1)}, u32[]{:S(2)}, u32[]{:S(2)}) %all-to-all-start.3) | async-done | bytes 1474592 | tf_op jit(solution)/shard_map/all_to_all | solution.py:622
  190.9 1.3 last.1
  (29 shorter events, 0.1 us)
Async XLA Ops:
  6.2 58.5 %copy-start.3 = (bf16[232,1024]{1,0:T(8,128)(2,1)}, bf16[232,1024]{1,0:T(8,128)(2,1)S(1)}, u32[]{:S(2)}) copy-start(bf16[232,1024]{1,0:T(8,128)(2,1)S(1)} %get-tuple-element.95.refs_0_) | copy-start | bytes 1425412
  6.2 54.9 %copy-start = (bf16[3072,384]{1,0:T(8,128)(2,1)S(1)}, bf16[3072,384]{1,0:T(8,128)(2,1)}, u32[]{:S(2)}) copy-start(bf16[3072,384]{1,0:T(8,128)(2,1)} %refs_2_.5) | copy-start | bytes 7077892
  6.2 13.4 %collective-permute-start = (bf16[232,1024]{1,0:T(8,128)(2,1)S(1)}, bf16[232,1024]{1,0:T(8,128)(2,1)S(1)}, u32[]{:S(2)}, u32[]{:S(2)}) collective-permute-start(bf16[232,1024]{1,0:T(8,128)(2,1)S(1)} %get-tuple-element.95.refs_0_), channel_id=1, source_target_pairs={{0,1},{1,0},{2,3},{3,2},{4,5},{5,4},{6,7},{7,6},{8,9},{9,8},{10,11... | collective-permute-start | bytes 1425416 | tf_op jit(solution)/shard_map/ppermute | solution.py:70
  10.0 23.1 %collective-permute-start.7 = (bf16[232,1024]{1,0:T(8,128)(2,1)S(1)}, bf16[232,1024]{1,0:T(8,128)(2,1)}, u32[]{:S(2)}, u32[]{:S(2)}) collective-permute-start(bf16[232,1024]{1,0:T(8,128)(2,1)S(1)} %get-tuple-element.95.refs_0_), channel_id=1, source_target_pairs={{0,14},{2,0},{4,2},{6,4},{8,6},{10,8},{12,10},{14,12},{1,15},{3,1}... | collective-permute-start | bytes 1425416 | tf_op jit(solution)/shard_map/ppermute | solution.py:70
  15.6 17.5 %collective-permute-start.6 = (bf16[232,1024]{1,0:T(8,128)(2,1)S(1)}, bf16[232,1024]{1,0:T(8,128)(2,1)}, u32[]{:S(2)}, u32[]{:S(2)}) collective-permute-start(bf16[232,1024]{1,0:T(8,128)(2,1)S(1)} %get-tuple-element.95.refs_0_), channel_id=1, source_target_pairs={{0,2},{2,4},{4,6},{6,8},{8,10},{10,12},{12,14},{14,0},{1,3},{3,5},... | collective-permute-start | bytes 1425416 | tf_op jit(solution)/shard_map/ppermute | solution.py:70
  19.6 45.1 %copy-start.4 = (bf16[232,1024]{1,0:T(8,128)(2,1)}, bf16[232,1024]{1,0:T(8,128)(2,1)S(1)}, u32[]{:S(2)}) copy-start(bf16[232,1024]{1,0:T(8,128)(2,1)S(1)} %collective-permute-done.refs_1_) | copy-start | bytes 1425412
  19.6 15.0 %collective-permute-start.3 = (bf16[232,1024]{1,0:T(8,128)(2,1)S(1)}, bf16[232,1024]{1,0:T(8,128)(2,1)}, u32[]{:S(2)}, u32[]{:S(2)}) collective-permute-start(bf16[232,1024]{1,0:T(8,128)(2,1)S(1)} %collective-permute-done.refs_1_), channel_id=1, source_target_pairs={{0,14},{2,0},{4,2},{6,4},{8,6},{10,8},{12,10},{14,12},{1,15},{3,1}... | collective-permute-start | bytes 1425416 | tf_op jit(solution)/shard_map/ppermute | solution.py:70
  26.0 35.2 %all-to-all-start = ((bf16[16,40,1024]{2,1,0:T(8,128)(2,1)}), bf16[16,40,1024]{2,1,0:T(8,128)(2,1)}, u32[]{:S(2)}, u32[]{:S(2)}) async-start(bf16[16,40,1024]{2,1,0:T(8,128)(2,1)} %bitcast.32), calls=%async_computation | async-start | bytes 2621440 | tf_op jit(solution)/shard_map/all_to_all | solution.py:622
  33.1 13.6 %collective-permute-start.1 = (bf16[232,1024]{1,0:T(8,128)(2,1)S(1)}, bf16[232,1024]{1,0:T(8,128)(2,1)}, u32[]{:S(2)}, u32[]{:S(2)}) collective-permute-start(bf16[232,1024]{1,0:T(8,128)(2,1)S(1)} %collective-permute-done.refs_1_), channel_id=1, source_target_pairs={{0,2},{2,4},{4,6},{6,8},{8,10},{10,12},{12,14},{14,0},{1,3},{3,5},... | collective-permute-start | bytes 1425416 | tf_op jit(solution)/shard_map/ppermute | solution.py:70
  33.1 23.7 %collective-permute-start.8 = (bf16[232,1024]{1,0:T(8,128)(2,1)}, bf16[232,1024]{1,0:T(8,128)(2,1)}, u32[]{:S(2)}, u32[]{:S(2)}) collective-permute-start(bf16[232,1024]{1,0:T(8,128)(2,1)} %collective-permute-done.6.refs_0_.refs_2_), channel_id=1, source_target_pairs={{0,2},{2,4},{4,6},{6,8},{8,10},{10,12},{12,14},{14,0},{1,3},{3,5},... | collective-permute-start | bytes 1425416 | tf_op jit(solution)/shard_map/ppermute | solution.py:70
  34.6 22.3 %collective-permute-start.4 = (bf16[232,1024]{1,0:T(8,128)(2,1)}, bf16[232,1024]{1,0:T(8,128)(2,1)}, u32[]{:S(2)}, u32[]{:S(2)}) collective-permute-start(bf16[232,1024]{1,0:T(8,128)(2,1)} %collective-permute-done.3.refs_3_.refs_5_), channel_id=1, source_target_pairs={{0,14},{2,0},{4,2},{6,4},{8,6},{10,8},{12,10},{14,12},{1,15},{3,1}... | collective-permute-start | bytes 1425416 | tf_op jit(solution)/shard_map/ppermute | solution.py:70
  38.1 22.8 %collective-permute-start.9 = (bf16[232,1024]{1,0:T(8,128)(2,1)}, bf16[232,1024]{1,0:T(8,128)(2,1)}, u32[]{:S(2)}, u32[]{:S(2)}) collective-permute-start(bf16[232,1024]{1,0:T(8,128)(2,1)} %collective-permute-done.7.refs_2_.refs_4_), channel_id=1, source_target_pairs={{0,14},{2,0},{4,2},{6,4},{8,6},{10,8},{12,10},{14,12},{1,15},{3,1}... | collective-permute-start | bytes 1425416 | tf_op jit(solution)/shard_map/ppermute | solution.py:70
  46.7 23.1 %collective-permute-start.2 = (bf16[232,1024]{1,0:T(8,128)(2,1)}, bf16[232,1024]{1,0:T(8,128)(2,1)}, u32[]{:S(2)}, u32[]{:S(2)}) collective-permute-start(bf16[232,1024]{1,0:T(8,128)(2,1)} %collective-permute-done.1.refs_1_.refs_3_), channel_id=1, source_target_pairs={{0,2},{2,4},{4,6},{6,8},{8,10},{10,12},{12,14},{14,0},{1,3},{3,5},... | collective-permute-start | bytes 1425416 | tf_op jit(solution)/shard_map/ppermute | solution.py:70
  56.9 20.4 %collective-permute-start.10 = (bf16[232,1024]{1,0:T(8,128)(2,1)}, bf16[232,1024]{1,0:T(8,128)(2,1)}, u32[]{:S(2)}, u32[]{:S(2)}) collective-permute-start(bf16[232,1024]{1,0:T(8,128)(2,1)} %collective-permute-done.8.refs_0_.refs_6_), channel_id=1, source_target_pairs={{0,2},{2,4},{4,6},{6,8},{8,10},{10,12},{12,14},{14,0},{1,3},{3,5},... | collective-permute-start | bytes 1425416 | tf_op jit(solution)/shard_map/ppermute | solution.py:70
  56.9 20.4 %collective-permute-start.5 = (bf16[232,1024]{1,0:T(8,128)(2,1)}, bf16[232,1024]{1,0:T(8,128)(2,1)}, u32[]{:S(2)}, u32[]{:S(2)}) collective-permute-start(bf16[232,1024]{1,0:T(8,128)(2,1)} %collective-permute-done.4.refs_3_.refs_9_), channel_id=1, source_target_pairs={{0,14},{2,0},{4,2},{6,4},{8,6},{10,8},{12,10},{14,12},{1,15},{3,1}... | collective-permute-start | bytes 1425416 | tf_op jit(solution)/shard_map/ppermute | solution.py:70
  60.8 24.2 %collective-permute-start.12 = (bf16[232,1024]{1,0:T(8,128)(2,1)}, bf16[232,1024]{1,0:T(8,128)(2,1)}, u32[]{:S(2)}, u32[]{:S(2)}) collective-permute-start(bf16[232,1024]{1,0:T(8,128)(2,1)} %collective-permute-done.9.refs_2_.refs_8_), channel_id=1, source_target_pairs={{0,14},{2,0},{4,2},{6,4},{8,6},{10,8},{12,10},{14,12},{1,15},{3,1}... | collective-permute-start | bytes 1425416 | tf_op jit(solution)/shard_map/ppermute | solution.py:70
  69.8 17.5 %collective-permute-start.11 = (bf16[232,1024]{1,0:T(8,128)(2,1)}, bf16[232,1024]{1,0:T(8,128)(2,1)S(1)}, u32[]{:S(2)}, u32[]{:S(2)}) collective-permute-start(bf16[232,1024]{1,0:T(8,128)(2,1)} %collective-permute-done.2.refs_1_.refs_7_), channel_id=1, source_target_pairs={{0,2},{2,4},{4,6},{6,8},{8,10},{10,12},{12,14},{14,0},{1,3},{3,5},... | collective-permute-start | bytes 1425416 | tf_op jit(solution)/shard_map/ppermute | solution.py:70
  77.2 20.3 %collective-permute-start.13 = (bf16[232,1024]{1,0:T(8,128)(2,1)}, bf16[232,1024]{1,0:T(8,128)(2,1)S(1)}, u32[]{:S(2)}, u32[]{:S(2)}) collective-permute-start(bf16[232,1024]{1,0:T(8,128)(2,1)} %collective-permute-done.10.refs_0_.refs_10_), channel_id=1, source_target_pairs={{0,2},{2,4},{4,6},{6,8},{8,10},{10,12},{12,14},{14,0},{1,3},{3,5},... | collective-permute-start | bytes 1425416 | tf_op jit(solution)/shard_map/ppermute | solution.py:70
  77.2 20.3 %collective-permute-start.14 = (bf16[232,1024]{1,0:T(8,128)(2,1)}, bf16[232,1024]{1,0:T(8,128)(2,1)S(1)}, u32[]{:S(2)}, u32[]{:S(2)}) collective-permute-start(bf16[232,1024]{1,0:T(8,128)(2,1)} %collective-permute-done.5.refs_3_.refs_13_), channel_id=1, source_target_pairs={{0,14},{2,0},{4,2},{6,4},{8,6},{10,8},{12,10},{14,12},{1,15},{3,1}... | collective-permute-start | bytes 1425416 | tf_op jit(solution)/shard_map/ppermute | solution.py:70
  87.3 5.1 %copy-start.5 = (bf16[232,1024]{1,0:T(8,128)(2,1)}, bf16[232,1024]{1,0:T(8,128)(2,1)S(1)}, u32[]{:S(2)}) copy-start(bf16[232,1024]{1,0:T(8,128)(2,1)S(1)} %collective-permute-done.11.refs_1_.refs_11_) | copy-start | bytes 1425412
  97.5 4.1 %copy-start.6 = (bf16[232,1024]{1,0:T(8,128)(2,1)}, bf16[232,1024]{1,0:T(8,128)(2,1)S(1)}, u32[]{:S(2)}) copy-start(bf16[232,1024]{1,0:T(8,128)(2,1)S(1)} %collective-permute-done.13.refs_0_.refs_14_) | copy-start | bytes 1425412
  97.5 4.1 %copy-start.7 = (bf16[232,1024]{1,0:T(8,128)(2,1)}, bf16[232,1024]{1,0:T(8,128)(2,1)S(1)}, u32[]{:S(2)}) copy-start(bf16[232,1024]{1,0:T(8,128)(2,1)S(1)} %collective-permute-done.14.refs_1_.refs_15_) | copy-start | bytes 1425412
  97.5 4.1 %copy-start.1 = (bf16[384,3072]{1,0:T(8,128)(2,1)S(1)}, bf16[384,3072]{1,0:T(8,128)(2,1)}, u32[]{:S(2)}) copy-start(bf16[384,3072]{1,0:T(8,128)(2,1)} %refs_1_.1) | copy-start | bytes 7077892
  102.8 15.0 %all-to-all-start.1 = ((bf16[16,8,512]{2,1,0:T(8,128)(2,1)}), bf16[16,8,512]{2,1,0:T(8,128)(2,1)S(1)}, u32[]{:S(2)}, u32[]{:S(2)}) async-start(bf16[16,8,512]{2,1,0:T(8,128)(2,1)} %bitcast.34), calls=%async_computation.1 | async-start | bytes 262144 | tf_op jit(solution)/shard_map/all_to_all | solution.py:622
  117.7 14.3 %collective-permute-start.15 = (bf16[256,1024]{1,0:T(8,128)(2,1)}, bf16[256,1024]{1,0:T(8,128)(2,1)S(1)}, u32[]{:S(2)}, u32[]{:S(2)}) collective-permute-start(bf16[256,1024]{1,0:T(8,128)(2,1)} %get-tuple-element.146), channel_id=1, source_target_pairs={{0,64},{32,96},{64,0},{96,32},{1,65},{33,97},{65,1},{97,33},{2,66}... | collective-permute-start | bytes 1572872 | tf_op jit(solution)/shard_map/ppermute | solution.py:458
  120.4 12.3 %collective-permute-start.16 = (bf16[256,1024]{1,0:T(8,128)(2,1)}, bf16[256,1024]{1,0:T(8,128)(2,1)S(1)}, u32[]{:S(2)}, u32[]{:S(2)}) collective-permute-start(bf16[256,1024]{1,0:T(8,128)(2,1)} %get-tuple-element.147), channel_id=1, source_target_pairs={{0,1},{1,0},{2,3},{3,2},{4,5},{5,4},{6,7},{7,6},{8,9},{9,8},{10,11... | collective-permute-start | bytes 1572872 | tf_op jit(solution)/shard_map/ppermute | solution.py:70
  120.9 21.2 %copy-start.2 = (bf16[384,3072]{1,0:T(8,128)(2,1)S(1)}, bf16[384,3072]{1,0:T(8,128)(2,1)}, u32[]{:S(2)}) copy-start(bf16[384,3072]{1,0:T(8,128)(2,1)} %refs_1_.1) | copy-start | bytes 7077892
  127.6 14.1 %all-to-all-start.2 = ((bf16[16,8,384]{2,1,0:T(8,128)(2,1)}), bf16[16,8,384]{2,1,0:T(8,128)(2,1)S(1)}, u32[]{:S(2)}, u32[]{:S(2)}) async-start(bf16[16,8,384]{2,1,0:T(8,128)(2,1)} %bitcast.33), calls=%async_computation.2 | async-start | bytes 196608 | tf_op jit(solution)/shard_map/all_to_all | solution.py:622
  141.7 8.7 %collective-permute-start.17 = (bf16[128,1024]{1,0:T(8,128)(2,1)}, bf16[128,1024]{1,0:T(8,128)(2,1)S(1)}, u32[]{:S(2)}, u32[]{:S(2)}) collective-permute-start(bf16[128,1024]{1,0:T(8,128)(2,1)} %get-tuple-element.167), channel_id=1, source_target_pairs={{0,32},{32,0},{64,96},{96,64},{1,33},{33,1},{65,97},{97,65},{2,34}... | collective-permute-start | bytes 786440 | tf_op jit(solution)/shard_map/ppermute | solution.py:458
  142.0 8.4 %collective-permute-start.18 = (bf16[128,1024]{1,0:T(8,128)(2,1)}, bf16[128,1024]{1,0:T(8,128)(2,1)S(1)}, u32[]{:S(2)}, u32[]{:S(2)}) collective-permute-start(bf16[128,1024]{1,0:T(8,128)(2,1)} %get-tuple-element.168), channel_id=1, source_target_pairs={{0,2},{2,0},{4,6},{6,4},{8,10},{10,8},{12,14},{14,12},{1,3},{3,1},... | collective-permute-start | bytes 786440 | tf_op jit(solution)/shard_map/ppermute | solution.py:458
  150.4 8.0 %collective-permute-start.19 = (bf16[1680,384]{1,0:T(8,128)(2,1)S(1)}, bf16[1680,384]{1,0:T(8,128)(2,1)S(1)}, u32[]{:S(2)}, u32[]{:S(2)}) collective-permute-start(bf16[1680,384]{1,0:T(8,128)(2,1)S(1)} %get-tuple-element.174), channel_id=1, source_target_pairs={{0,16},{16,0},{1,17},{17,1},{2,18},{18,2},{3,19},{19,3},{4,20},{20... | collective-permute-start | bytes 3870728 | tf_op jit(solution)/shard_map/ppermute | solution.py:70
  157.2 5.3 %collective-permute-start.20 = (bf16[64,1024]{1,0:T(8,128)(2,1)}, bf16[64,1024]{1,0:T(8,128)(2,1)S(1)}, u32[]{:S(2)}, u32[]{:S(2)}) collective-permute-start(bf16[64,1024]{1,0:T(8,128)(2,1)} %get-tuple-element.175), channel_id=1, source_target_pairs={{0,128},{128,0},{1,129},{129,1},{2,130},{130,2},{3,131},{131,3},{4... | collective-permute-start | bytes 393224 | tf_op jit(solution)/shard_map/ppermute | solution.py:458
  157.8 8.7 %collective-permute-start.21 = (bf16[64,1024]{1,0:T(8,128)(2,1)}, bf16[64,1024]{1,0:T(8,128)(2,1)S(1)}, u32[]{:S(2)}, u32[]{:S(2)}) collective-permute-start(bf16[64,1024]{1,0:T(8,128)(2,1)} %get-tuple-element.176), channel_id=1, source_target_pairs={{0,4},{2,6},{4,0},{6,2},{8,12},{10,14},{12,8},{14,10},{1,5},{3,7},... | collective-permute-start | bytes 393224 | tf_op jit(solution)/shard_map/ppermute | solution.py:458
  166.5 24.4 %all-to-all-start.3 = ((bf16[8,240,384]{2,1,0:T(8,128)(2,1)}), bf16[8,240,384]{2,1,0:T(8,128)(2,1)S(1)}, u32[]{:S(2)}, u32[]{:S(2)}) async-start(bf16[8,240,384]{2,1,0:T(8,128)(2,1)} %bitcast.31), calls=%async_computation.3 | async-start | bytes 2949120 | tf_op jit(solution)/shard_map/all_to_all | solution.py:622
  172.3 7.9 %collective-permute-start.22 = (bf16[32,1024]{1,0:T(8,128)(2,1)}, bf16[32,1024]{1,0:T(8,128)(2,1)S(1)}, u32[]{:S(2)}, u32[]{:S(2)}) collective-permute-start(bf16[32,1024]{1,0:T(8,128)(2,1)} %get-tuple-element.180), channel_id=1, source_target_pairs={{0,8},{2,10},{4,12},{6,14},{8,0},{10,2},{12,4},{14,6},{1,9},{3,11}... | collective-permute-start | bytes 196616 | tf_op jit(solution)/shard_map/ppermute | solution.py:458
  173.7 9.1 %collective-permute-start.23 = (bf16[32,1024]{1,0:T(8,128)(2,1)}, bf16[32,1024]{1,0:T(8,128)(2,1)S(1)}, u32[]{:S(2)}, u32[]{:S(2)}) collective-permute-start(bf16[32,1024]{1,0:T(8,128)(2,1)} %get-tuple-element.182), channel_id=1, source_target_pairs={{0,16},{16,0},{1,17},{17,1},{2,18},{18,2},{3,19},{19,3},{4,20},{20... | collective-permute-start | bytes 196616 | tf_op jit(solution)/shard_map/ppermute | solution.py:458
  180.2 0.8 copy-start.9
  182.7 0.8 copy-start.8
